TPU v7x, 128 devices: a whole 4x4x4 slice. The times are simulated.
128 devices in a mesh: gx: 8 (over z, core), gy: 16 (over y, x).
Axes of the slice: x: 4, y: 4, z: 4, core: 2. Of those that a mesh axis runs over, the one named last changes fastest.
Arguments:
- e_fields: float32 [3, 128, 256, 128], P(None, 'gx', 'gy'), may hold values from -0.6 to 0.6
- h_fields: float32 [3, 128, 256, 128], P(None, 'gx', 'gy'), may hold values from -6 to 6
- material: int32 [128, 256, 128], P('gx', 'gy'), may hold values from 0 to 7
- permittivity: float32 [8], replicated, may hold values from 1 to 10
- conductivity: float32 [8], replicated, may hold values from 0.05 to 0.5
- electrode_cells: int32 [16384], P(('gx', 'gy')), may hold values from 0 to 255
- electrode_dest: int32 [16384, 1], P(('gx', 'gy')), may hold values from 0 to 127; in each aligned block of 128 rows (0 to 127, 128 to 255, ...) at most 2 rows name the same one
- target_cells: int32 [16384], P(('gx', 'gy')), may hold values from 0 to 255
- electrode_gain: float32 [16384], P(('gx', 'gy')), may hold values from 1 to 4
Outputs:
- e_out: float32 [3, 128, 256, 128], P(None, 'gx', 'gy')
- h_out: float32 [3, 128, 256, 128], P(None, 'gx', 'gy')
Inputs may be any that keep to these rules, and one draw needn't show every extreme that they name: `electrode_dest`: no tile is named by more than 2 of the 128 rows of one device, and in every draw some device names some tile exactly 2 times. `electrode_cells`: a cell of the owning tile, numbered with x slower than y. `target_cells`: a cell of the receiving tile, numbered with x slower than y.
All inputs are finite; a program needn't handle non-finite values.
Results may differ from a plain program's by a relative error of at most 0.0003.
Values sent between devices are 32-bit elements; how exact they have to be, the bound alone decides.
No kernel may reach another device: no remote copies, remote signals or barrier semaphores. Data moves between devices by JAX's collectives and lax.ppermute only.
A program may use at most 128 MiB of HBM per device.

v0:
```python
import jax
import jax.numpy as jnp
from jax import lax
from jax.experimental import pallas as pl
from jax.experimental.pallas import tpu as pltpu
from jax.sharding import PartitionSpec as P

F32 = jnp.float32
BF16 = jnp.bfloat16
CX = 16
CY = 16
NZ = 128
CELLS = CX * CY
GX = 8
GY = 16
HS = 16.0
INV = 1.0 / 256.0

R1_VAL, R1_HALO, R1_G11, R1_G1N, R1_GNN, R1_CODE, R1 = 0, 32, 48, 64, 80, 96, 104
R2_VAL, R2_CODE, R2_HA, R2_HB, R2_P1, R2_P2, R2_G11, R2_G1N, R2_GNN, R2 = (
    0, 16, 24, 40, 56, 72, 88, 104, 120, 136)
R3_Z, R3_Y, R3_T, R3 = 0, 16, 32, 48
R4 = 16


def iota(shape, dim):
    return lax.broadcasted_iota(jnp.int32, shape, dim)


def z_up(f):
    return jnp.where(iota(f.shape, 1) == NZ - 1, 0.0, pltpu.roll(f, NZ - 1, 1))


def z_down(f):
    return jnp.where(iota(f.shape, 1) == 0, 0.0, pltpu.roll(f, 1, 1))


def y_up(f, last):
    return jnp.where(iota(f.shape, 0) == CY - 1, last, pltpu.roll(f, CY - 1, 0))


def y_down(f, first):
    return jnp.where(iota(f.shape, 0) == 0, first, pltpu.roll(f, 1, 0))


def rows(x):
    return pl.ds(x * CY, CY)


def strided(y):
    return pl.ds(y, CX, stride=CY)


def z_solve(w, d):
    lane = iota(w.shape, 1)
    a = jnp.where(lane == 0, 0.0, 1.0)
    c = jnp.where(lane == NZ - 1, 0.0, 1.0)
    e = w + (2.0 - a - c)
    step = 1
    while step < NZ:
        rb = 1.0 / (e + a + c)
        eb = e * rb
        db = d * rb
        e = e + a * pltpu.roll(eb, step, 1) + c * pltpu.roll(eb, NZ - step, 1)
        d = d + a * pltpu.roll(db, step, 1) + c * pltpu.roll(db, NZ - step, 1)
        if 2 * step < NZ:
            a, c = a * pltpu.roll(a * rb, step, 1), c * pltpu.roll(c * rb, NZ - step, 1)
        step *= 2
    return d / e


def pivots(ws):
    def sweep(seq):
        s, l = seq[0], None
        rf = 1.0 / (1.0 + 1.0 + s)
        out = [rf]
        l = rf
        for w in seq[1:]:
            s = w + s * rf
            rf = 1.0 / (1.0 + l + s)
            out.append(rf)
            l = l * rf
        return out, l
    fwd, link = sweep(ws)
    bwd, _ = sweep(ws[::-1])
    return fwd, bwd[::-1], link


def ends(ds, fwd, bwd):
    y = ds[0]
    b = ds[-1]
    n = len(ds)
    for k in range(1, n):
        y = ds[k] + fwd[k - 1] * y
        b = ds[n - 1 - k] + bwd[n - k] * b
    return b * bwd[0], y * fwd[n - 1]


def block_solve(ds, fwd, left, right):
    ys = [ds[0] + left]
    for k in range(1, len(ds)):
        ys.append(ds[k] + fwd[k - 1] * ys[-1])
    u = (ys[-1] + right) * fwd[-1]
    us = [u]
    for k in range(len(ds) - 2, -1, -1):
        u = (ys[k] + u) * fwd[k]
        us.append(u)
    return us[::-1]


def static_fold(n, g11, g1n, gnn, h_ref, hr_ref, be_ref, de_ref):
    zero = jnp.zeros((16, NZ), F32)
    be = zero
    de = zero
    be_ref[0] = be
    de_ref[n] = de
    for k in range(n):
        a1, a2, a3 = g11(k), g1n(k), gnn(k)
        h = a2 / (1.0 - a1 * be)
        be = a3 + a2 * h * be
        h_ref[k] = h
        be_ref[k + 1] = be
        j = n - 1 - k
        b1, b2, b3 = g11(j), g1n(j), gnn(j)
        hr = b2 / (1.0 - b3 * de)
        de = b1 + b2 * hr * de
        hr_ref[j] = hr
        de_ref[j] = de


def interface(n, me, own_m, own_n, recv, h_ref, hr_ref, be_ref, de_ref):
    al = jnp.zeros((16, NZ), F32)
    ga = jnp.zeros((16, NZ), F32)
    for k in range(n - 1):
        al = jnp.where(k < me, recv(k) + h_ref[k] * al, al)
        j = n - 1 - k
        ga = jnp.where(j > me, recv(j) + hr_ref[j] * ga, ga)
    be, be1 = be_ref[me], be_ref[me + 1]
    de, de1 = de_ref[me], de_ref[me + 1]
    own_ga = own_n + hr_ref[me] * ga
    own_al = own_m + h_ref[me] * al
    left = (al + be * own_ga) / (1.0 - be * de)
    right = (ga + de1 * own_al) / (1.0 - be1 * de1)
    return left, right


def to_messages(me, p1, p2, h_ref, hr_ref, be_ref, de_ref):
    m = p2 + h_ref[me] * be_ref[me] * p1
    n = p1 + hr_ref[me] * de_ref[me + 1] * p2
    return m, n


def split_dot(sel, values):
    hi = values.astype(BF16)
    rest = values - hi.astype(F32)
    mid = rest.astype(BF16)
    low = (rest - mid.astype(F32)).astype(BF16)
    dims = (((1,), (0,)), ((), ()))

    def part(v):
        return lax.dot_general(sel, v, dims, preferred_element_type=F32)

    return part(hi) + part(mid) + part(low)


def k1(e, h, mat, perm, cond, cells, dest, tgt, gain, msg, w_o, v_o, fx_o, bx_o):
    me = lax.axis_index("gx")
    ws = [(perm[k] + 8.0 * cond[k]) * (1.0 / 4096.0) for k in range(8)]
    vs = [(perm[k] - 8.0 * cond[k]) * (1.0 / 4096.0) for k in range(8)]

    def pick(table, bits):
        for bit in bits:
            table = [jnp.where(bit, table[2 * k + 1], table[2 * k]) for k in range(len(table) // 2)]
        return table[0]

    wx = []
    for x in range(CX):
        m = mat[rows(x), :]
        bits = [(m & 1) != 0, (m & 2) != 0, (m & 4) != 0]
        w = pick(ws, bits)
        w_o[rows(x), :] = w
        v_o[rows(x), :] = pick(vs, bits)
        wx.append(w)
    fwd, bwd, link = pivots(wx)
    for x in range(CX):
        fx_o[x] = fwd[x]
        bx_o[x] = bwd[x]
    to = dest[...]
    to_b = jnp.broadcast_to(to, (128, 128))
    same = (to_b.T == to_b) & (iota((128, 128), 0) < iota((128, 128), 1))
    rank = jnp.sum(same.astype(jnp.int32), axis=0, keepdims=True)
    lane_slot = rank * GY + (to & (GY - 1))
    dest_x = to >> 4
    hot = iota((CELLS, 128), 0) == dest_x * 32 + lane_slot
    slot_gain = jnp.sum(jnp.where(hot, gain[...], 0.0), axis=1, keepdims=True)
    from_cell = (iota((CELLS, 128), 0) == cells[...]).astype(BF16)
    nt = (((1,), (1,)), ((), ()))
    pickm = lax.dot_general(hot.astype(BF16), from_cell, nt, preferred_element_type=F32)
    vals = split_dot(pickm.astype(BF16), e[2]) * slot_gain
    code_at = jnp.where(iota((8, 128), 0) == dest_x, (tgt[...] + 1).astype(F32), 0.0).astype(BF16)
    lane_hot = (iota((128, 128), 0) == lane_slot).astype(BF16)
    code = lax.dot_general(code_at, lane_hot, nt, preferred_element_type=F32)
    hz_last = h[2, rows(CX - 1), :]
    ey_first = e[1, rows(0), :]
    for d in range(GX):
        msg[d, 0:32, :] = vals[d * 32:(d + 1) * 32]
        msg[d, R1_HALO:R1_HALO + 16, :] = jnp.where(d > me, hz_last, ey_first)
        msg[d, R1_G11:R1_G11 + 16, :] = bwd[0]
        msg[d, R1_G1N:R1_G1N + 16, :] = link
        msg[d, R1_GNN:R1_GNN + 16, :] = fwd[CX - 1]
        msg[d, R1_CODE:R1_CODE + 8, :] = jnp.broadcast_to(code[d:d + 1], (8, NZ))


def k1b(w, fy_o, by_o, g_o):
    ws = [w[strided(y), :] for y in range(CY)]
    fwd, bwd, link = pivots(ws)
    for y in range(CY):
        fy_o[y] = fwd[y]
        by_o[y] = bwd[y]
    g_o[0] = bwd[0]
    g_o[1] = link
    g_o[2] = fwd[CY - 1]


def k2(m1, e, h, w, v, fy, by, g, msg, hzp_o, dx_o, halo_o):
    gx = lax.axis_index("gx")
    me = lax.axis_index("gy")
    lo = jnp.maximum(gx - 1, 0) * R1 + R1_HALO
    hi = jnp.minimum(gx + 1, GX - 1) * R1 + R1_HALO
    hz_low = jnp.where(gx > 0, m1[pl.ds(lo, 16), :], 0.0)
    ey_high = jnp.where(gx < GX - 1, m1[pl.ds(hi, 16), :], 0.0)
    halo_o[...] = hz_low
    for x in range(CX):
        ey = e[1, rows(x), :]
        ey_next = e[1, rows(x + 1), :] if x < CX - 1 else ey_high
        hzp = h[2, rows(x), :] - HS * (ey_next - ey)
        hzp_o[rows(x), :] = hzp
        hy = h[1, rows(x), :]
        curl = (hzp - y_down(hzp, 0.0)) - (hy - z_down(hy))
        dx_o[rows(x), :] = v[rows(x), :] * e[0, rows(x), :] + INV * curl
    bwd = [by[y] for y in range(CY)]
    fwd = [fy[y] for y in range(CY)]
    p1, p2 = ends([dx_o[strided(y), :] for y in range(CY)], fwd, bwd)
    t = -INV * hzp_o[strided(CY - 1), :]
    p2 = p2 + t
    ez_first = e[2, strided(0), :]
    hx_last = h[0, strided(CY - 1), :]
    code = m1[pl.ds(R1_CODE, 8, stride=R1), :]
    for d in range(GY):
        for r in range(2):
            msg[d, r * 8:r * 8 + 8, :] = m1[pl.ds(r * GY + d, 8, stride=R1), :]
        msg[d, R2_CODE:R2_CODE + 8, :] = code
        msg[d, R2_HA:R2_HA + 16, :] = jnp.where(d > me, hx_last, ez_first)
        msg[d, R2_HB:R2_HB + 16, :] = t
        msg[d, R2_P1:R2_P1 + 16, :] = p1
        msg[d, R2_P2:R2_P2 + 16, :] = p2
        msg[d, R2_G11:R2_G11 + 16, :] = g[0]
        msg[d, R2_G1N:R2_G1N + 16, :] = g[1]
        msg[d, R2_GNN:R2_GNN + 16, :] = g[2]


def k2b(m1, h_o, hr_o, be_o, de_o):
    static_fold(
        GX,
        lambda j: m1[pl.ds(j * R1 + R1_G11, 16), :],
        lambda j: m1[pl.ds(j * R1 + R1_G1N, 16), :],
        lambda j: m1[pl.ds(j * R1 + R1_GNN, 16), :],
        h_o, hr_o, be_o, de_o)


def k3(m2, e, h, w, v, hzp, dx, hz_low, fy, fx, bx, hx_c, hrx_c, bex, dex,
       msg, hy_c, hry_c, bey, dey, ex1_o, hz1_o, hz1m_o, inj_o, hyp_o, hxpp_o, hzpp_o,
       dz_o, dy2_o, own_o, hxp_s, ey1_s, dy1_s):
    gx = lax.axis_index("gx")
    me = lax.axis_index("gy")
    static_fold(GY, lambda j: m2[j, R2_G11:R2_G11 + 16, :], lambda j: m2[j, R2_G1N:R2_G1N + 16, :],
                lambda j: m2[j, R2_GNN:R2_GNN + 16, :], hy_c, hry_c, bey, dey)
    p1 = m2[me, R2_P1:R2_P1 + 16, :]
    p2 = m2[me, R2_P2:R2_P2 + 16, :]
    own_m, own_n = to_messages(me, p1, p2, hy_c, hry_c, bey, dey)

    def recv(j):
        q1 = m2[j, R2_P1:R2_P1 + 16, :]
        q2 = m2[j, R2_P2:R2_P2 + 16, :]
        return jnp.where(j < me, q2 + hy_c[j] * bey[j] * q1, q1 + hry_c[j] * dey[j + 1] * q2)

    left, right = interface(GY, me, own_m, own_n, recv, hy_c, hry_c, bey, dey)
    us = block_solve([dx[strided(y), :] for y in range(CY)], [fy[y] for y in range(CY)], left, right)
    for y in range(CY):
        ex1_o[strided(y), :] = us[y]
    below = jnp.maximum(me - 1, 0)
    above = jnp.minimum(me + 1, GY - 1)
    t = m2[below, R2_HB:R2_HB + 16, :]
    hz1m_o[...] = jnp.where(me > 0, HS * (us[0] - left) - 240.0 * t, 0.0)
    hx_low = jnp.where(me > 0, m2[below, R2_HA:R2_HA + 16, :], 0.0)
    ez_high = jnp.where(me < GY - 1, m2[above, R2_HA:R2_HA + 16, :], 0.0)
    codes = jnp.concatenate([m2[j, R2_CODE:R2_CODE + 8, :] for j in range(GY)], axis=0).astype(BF16)
    inj = None
    for r in range(2):
        lane = (iota((8, 128), 1) == r * GY + me).astype(BF16)
        code_row = lax.dot_general(lane, codes, (((1,), (1,)), ((), ())), preferred_element_type=F32)[0:1]
        land = ((iota((CELLS, 128), 0) + 1).astype(F32) == code_row).astype(BF16)
        vals = jnp.concatenate([m2[j, r * 8:r * 8 + 8, :] for j in range(GY)], axis=0)
        part = split_dot(land, vals)
        inj = part if inj is None else inj + part
    inj_o[...] = inj
    prev_hyp = None
    for x in range(CX):
        ez = e[2, rows(x), :]
        hx = h[0, rows(x), :]
        ex = e[0, rows(x), :]
        hz = h[2, rows(x), :]
        hxp = hx - HS * (y_up(ez, ez_high[x:x + 1]) - ez)
        hxp_s[rows(x), :] = hxp
        hyp = h[1, rows(x), :] - HS * (z_up(ex) - ex)
        hyp_o[rows(x), :] = hyp
        curl = hyp - (hx - y_down(hx, hx_low[x:x + 1])) - inj_o[rows(x), :]
        if x > 0:
            curl = curl - prev_hyp
        prev_hyp = hyp
        dz_o[rows(x), :] = v[rows(x), :] * ez + INV * curl
        hz_prev = h[2, rows(x - 1), :] if x > 0 else hz_low[...]
        curl = (hxp - z_down(hxp)) - (hz - hz_prev)
        dy1_s[rows(x), :] = v[rows(x), :] * e[1, rows(x), :] + INV * curl
    for q in range(4):
        part = pl.ds(q * 64, 64)
        ey1_s[part, :] = z_solve(w[part, :], dy1_s[part, :])
    prev = None
    for x in range(CX):
        ey1 = ey1_s[rows(x), :]
        dey1 = HS * (z_up(ey1) - ey1)
        hx1 = hxp_s[rows(x), :] + dey1
        hxpp_o[rows(x), :] = hx1 + dey1
        ex1 = ex1_o[rows(x), :]
        dex1 = HS * (y_up(ex1, right[x:x + 1]) - ex1)
        hz1 = hzp[rows(x), :] + dex1
        hz1_o[rows(x), :] = hz1
        hzpp = hz1 + dex1
        hzpp_o[rows(x), :] = hzpp
        curl = (hx1 - z_down(hx1)) - hzpp
        if x > 0:
            curl = curl + prev
        prev = hzpp
        dy2_o[rows(x), :] = v[rows(x), :] * ey1 + INV * curl
    fwd = [fx[x] for x in range(CX)]
    bwd = [bx[x] for x in range(CX)]
    tz = -INV * hyp_o[rows(CX - 1), :]
    p1, p2 = ends([dz_o[rows(x), :] for x in range(CX)], fwd, bwd)
    mz, nz = to_messages(gx, p1, p2 + tz, hx_c, hrx_c, bex, dex)
    ty = INV * hzpp_o[rows(CX - 1), :]
    p1, p2 = ends([dy2_o[rows(x), :] for x in range(CX)], fwd, bwd)
    my, ny = to_messages(gx, p1, p2 + ty, hx_c, hrx_c, bex, dex)
    own_o[0], own_o[1], own_o[2], own_o[3] = mz, nz, my, ny
    for d in range(GX):
        msg[d, 0:16, :] = jnp.where(d > gx, mz, nz)
        msg[d, 16:32, :] = jnp.where(d > gx, my, ny)
        msg[d, 32:48, :] = tz


def k4(m3, own, v, w, dz, fx, fy, by, hyp, hxpp, inj, hx_c, hrx_c, bex, dex, hy_c, hry_c, bey, dey,
       msg, dz2_o, hypp_o, own_o):
    gx = lax.axis_index("gx")
    me = lax.axis_index("gy")
    left, right = interface(GX, gx, own[0], own[1], lambda j: m3[j, 0:16, :], hx_c, hrx_c, bex, dex)
    us = block_solve([dz[rows(x), :] for x in range(CX)], [fx[x] for x in range(CX)], left, right)
    t = m3[jnp.maximum(gx - 1, 0), 32:48, :]
    prev = jnp.where(gx > 0, HS * (us[0] - left) - 240.0 * t, 0.0)
    for x in range(CX):
        dez = HS * ((us[x + 1] if x < CX - 1 else right) - us[x])
        hy1 = hyp[rows(x), :] + dez
        hypp_o[rows(x), :] = hy1 + dez
        hx2 = hxpp[rows(x), :]
        curl = (hy1 - prev) - (hx2 - y_down(hx2, 0.0)) - inj[rows(x), :]
        prev = hy1
        dz2_o[rows(x), :] = v[rows(x), :] * us[x] + INV * curl
    p1, p2 = ends([dz2_o[strided(y), :] for y in range(CY)], [fy[y] for y in range(CY)], [by[y] for y in range(CY)])
    p2 = p2 + INV * hxpp[strided(CY - 1), :]
    m, n = to_messages(me, p1, p2, hy_c, hry_c, bey, dey)
    own_o[0], own_o[1] = m, n
    for d in range(GY):
        msg[d] = jnp.where(d > me, m, n)


def k4b(m3, own, v, w, fx, ex1, hz1, hz1m, hypp, hzpp, dy2, hx_c, hrx_c, bex, dex,
        ex2_o, ey2_o, hy2_o, hz2_o, dx2_s):
    gx = lax.axis_index("gx")
    left, right = interface(GX, gx, own[2], own[3], lambda j: m3[j, 16:32, :], hx_c, hrx_c, bex, dex)
    us = block_solve([dy2[rows(x), :] for x in range(CX)], [fx[x] for x in range(CX)], left, right)
    for x in range(CX):
        ey2_o[rows(x), :] = us[x]
        hz2_o[rows(x), :] = hzpp[rows(x), :] - HS * ((us[x + 1] if x < CX - 1 else right) - us[x])
        hz = hz1[rows(x), :]
        hy = hypp[rows(x), :]
        curl = (hz - y_down(hz, hz1m[x:x + 1, :])) - (hy - z_down(hy))
        dx2_s[rows(x), :] = v[rows(x), :] * ex1[rows(x), :] + INV * curl
    for q in range(4):
        part = pl.ds(q * 64, 64)
        ex2 = z_solve(w[part, :], dx2_s[part, :])
        ex2_o[part, :] = ex2
        hy2_o[part, :] = hypp[part, :] - HS * (z_up(ex2) - ex2)


def k5(m4, own, dz2, fy, hxpp, ex2, ey2, hy2, hz2, hy_c, hry_c, bey, dey, e_o, h_o):
    me = lax.axis_index("gy")
    left, right = interface(GY, me, own[0], own[1], lambda j: m4[j], hy_c, hry_c, bey, dey)
    us = block_solve([dz2[strided(y), :] for y in range(CY)], [fy[y] for y in range(CY)], left, right)
    for y in range(CY):
        e_o[2, strided(y), :] = us[y]
    e_o[0] = ex2[...]
    e_o[1] = ey2[...]
    h_o[1] = hy2[...]
    h_o[2] = hz2[...]
    for x in range(CX):
        ez2 = e_o[2, rows(x), :]
        h_o[0, rows(x), :] = hxpp[rows(x), :] - HS * (y_up(ez2, right[x:x + 1]) - ez2)


def call(kernel, shapes, args, scratch=(), smem=()):
    specs = [
        pl.BlockSpec(memory_space=pltpu.SMEM if k in smem else pltpu.VMEM) for k in range(len(args))
    ]
    return pl.pallas_call(
        kernel,
        out_shape=[jax.ShapeDtypeStruct(s, F32) for s in shapes],
        in_specs=specs,
        out_specs=[pl.BlockSpec(memory_space=pltpu.VMEM) for _ in shapes],
        scratch_shapes=[pltpu.VMEM(s, F32) for s in scratch],
        name=kernel.__name__,
    )(*args)


def exchange(message, axis):
    return lax.all_to_all(message, axis, split_axis=0, concat_axis=0, tiled=True)


FIELD = (CELLS, NZ)
FACE = (16, NZ)
LINE = (16, 16, NZ)


def body(e_fields, h_fields, material, permittivity, conductivity, electrode_cells, electrode_dest,
         target_cells, electrode_gain):
    e = e_fields.reshape(3, CELLS, NZ)
    h = h_fields.reshape(3, CELLS, NZ)
    mat = material.reshape(CELLS, NZ)
    msg1, w, v, fx, bx = call(
        k1, [(GX, R1, NZ), FIELD, FIELD, LINE, LINE],
        (e, h, mat, permittivity, conductivity, electrode_cells.reshape(1, 128),
         electrode_dest.reshape(1, 128), target_cells.reshape(1, 128), electrode_gain.reshape(1, 128)),
        smem=(3, 4))
    m1 = exchange(msg1, "gx").reshape(GX * R1, NZ)
    fy, by, g = call(k1b, [LINE, LINE, (3,) + FACE], (w,))
    msg2, hzp, dx, hz_low = call(
        k2, [(GY, R2, NZ), FIELD, FIELD, FACE], (m1, e, h, w, v, fy, by, g))
    m2 = exchange(msg2, "gy")
    xstat = call(k2b, [(GX,) + FACE, (GX,) + FACE, (GX + 1,) + FACE, (GX + 1,) + FACE], (m1,))
    (msg3, hyc, hryc, bey, dey, ex1, hz1, hz1m, inj, hyp, hxpp, hzpp, dz, dy2, own) = call(
        k3, [(GX, R3, NZ), (GY,) + FACE, (GY,) + FACE, (GY + 1,) + FACE, (GY + 1,) + FACE,
             FIELD, FIELD, FACE, FIELD, FIELD, FIELD, FIELD, FIELD, FIELD, (4,) + FACE],
        (m2, e, h, w, v, hzp, dx, hz_low, fy, fx, bx, *xstat), scratch=[FIELD, FIELD, FIELD])
    ystat = (hyc, hryc, bey, dey)
    m3 = exchange(msg3, "gx")
    msg4, dz2, hypp, own2 = call(
        k4, [(GY, R4, NZ), FIELD, FIELD, (2,) + FACE],
        (m3, own, v, w, dz, fx, fy, by, hyp, hxpp, inj, *xstat, *ystat))
    m4 = exchange(msg4, "gy")
    ex2, ey2, hy2, hz2 = call(
        k4b, [FIELD] * 4, (m3, own, v, w, fx, ex1, hz1, hz1m, hypp, hzpp, dy2, *xstat), scratch=[FIELD])
    e_out, h_out = call(
        k5, [(3,) + FIELD, (3,) + FIELD], (m4, own2, dz2, fy, hxpp, ex2, ey2, hy2, hz2, *ystat))
    return e_out.reshape(3, CX, CY, NZ), h_out.reshape(3, CX, CY, NZ)


def solution(mesh):
    in_specs = (
        P(None, "gx", "gy", None),
        P(None, "gx", "gy", None),
        P("gx", "gy", None),
        P(),
        P(),
        P(("gx", "gy")),
        P(("gx", "gy"), None),
        P(("gx", "gy")),
        P(("gx", "gy")),
    )
    out_specs = (P(None, "gx", "gy", None), P(None, "gx", "gy", None))
    return jax.shard_map(body, mesh=mesh, in_specs=in_specs, out_specs=out_specs, check_vma=False)
```

profile of v0, /device:TPU:0, one launch (start us, length us, event | category | flops | bytes accessed | tf_op | source)
XLA Modules:
  0.0 81.6 jit_solution(10880227060695229087)
XLA Ops:
  0.6 2.6 %k1.1 = (f32[8,104,128]{2,1,0:T(8,128)}, f32[256,128]{1,0:T(8,128)}, f32[256,128]{1,0:T(8,128)}, f32[16,16,128]{2,1,0:T(8,128)}, f32[16,16,128]{2,1,0:T(8,128)}) custom-call(f32[3,256,128]{2,1,0:T(8,128)} %bitcast.12, f32[3,256,128]{2,1,0:T(8,128)} %bitcast.15, s32[256,128]{1,0:T(8,128)} %bitcast.18, f32[8]{0:T(128)} %perm.1, f32[8]{0:T(128)} %cond.1, ...), custom_call_target="tpu_custom_call" | custom-call | tf_op jit(solution)/shard_map/k1/pallas_call | solution.py:422
  3.2 5.4 %all-to-all-start = ((f32[8,104,128]{2,1,0:T(8,128)}), f32[8,104,128]{2,1,0:T(8,128)S(1)}, u32[]{:S(2)}, u32[]{:S(2)}) async-start(f32[8,104,128]{2,1,0:T(8,128)} %get-tuple-element.43), calls=%async_computation | async-start | bytes 851968 | tf_op jit(solution)/shard_map/all_to_all | solution.py:433
  8.6 1.7 %k1b.1 = (f32[16,16,128]{2,1,0:T(8,128)}, f32[16,16,128]{2,1,0:T(8,128)}, f32[3,16,128]{2,1,0:T(8,128)}) custom-call(f32[256,128]{1,0:T(8,128)} %get-tuple-element.44.w), custom_call_target="tpu_custom_call" | custom-call | tf_op jit(solution)/shard_map/k1b/pallas_call | solution.py:422
  10.4 7.5 %all-to-all-done = f32[8,104,128]{2,1,0:T(8,128)S(1)} async-done(((f32[8,104,128]{2,1,0:T(8,128)}), f32[8,104,128]{2,1,0:T(8,128)S(1)}, u32[]{:S(2)}, u32[]{:S(2)}) %all-to-all-start) | async-done | bytes 426016 | tf_op jit(solution)/shard_map/all_to_all | solution.py:433
  17.9 0.0 copy-start.1
  17.9 0.8 copy-done.1
  18.7 2.6 %k2.1 = (f32[16,136,128]{2,1,0:T(8,128)}, f32[256,128]{1,0:T(8,128)}, f32[256,128]{1,0:T(8,128)}, f32[16,128]{1,0:T(8,128)}) custom-call(f32[832,128]{1,0:T(8,128)} %bitcast.10, f32[3,256,128]{2,1,0:T(8,128)} %bitcast.13, f32[3,256,128]{2,1,0:T(8,128)} %bitcast.16, f32[256,128]{1,0:T(8,128)} %get-tuple-element.44.w, f32[256,128]{1,0:T(8,128)} %get-tuple-element.45.v, ...), custom_call_target="tpu_custom_call" | custom-call | tf_op jit(solution)/shard_map/k2/pallas_call | solution.py:422
  21.4 7.0 %all-to-all-start.1 = ((f32[16,136,128]{2,1,0:T(8,128)}), f32[16,136,128]{2,1,0:T(8,128)S(1)}, u32[]{:S(2)}, u32[]{:S(2)}) async-start(f32[16,136,128]{2,1,0:T(8,128)} %get-tuple-element.49), calls=%async_computation.1 | async-start | bytes 2228224 | tf_op jit(solution)/shard_map/all_to_all | solution.py:433
  28.4 1.8 %k2b.1 = (f32[8,16,128]{2,1,0:T(8,128)}, f32[8,16,128]{2,1,0:T(8,128)}, f32[9,16,128]{2,1,0:T(8,128)}, f32[9,16,128]{2,1,0:T(8,128)}) custom-call(f32[832,128]{1,0:T(8,128)} %bitcast.11), custom_call_target="tpu_custom_call" | custom-call | tf_op jit(solution)/shard_map/k2b/pallas_call | solution.py:422
  30.2 16.4 %all-to-all-done.1.m2 = f32[16,136,128]{2,1,0:T(8,128)S(1)} async-done(((f32[16,136,128]{2,1,0:T(8,128)}), f32[16,136,128]{2,1,0:T(8,128)S(1)}, u32[]{:S(2)}, u32[]{:S(2)}) %all-to-all-start.1) | async-done | bytes 1114144 | tf_op jit(solution)/shard_map/all_to_all | solution.py:433
  46.6 0.0 copy-start
  46.6 1.0 %copy-done = f32[16,136,128]{2,1,0:T(8,128)} copy-done((f32[16,136,128]{2,1,0:T(8,128)}, f32[16,136,128]{2,1,0:T(8,128)S(1)}, u32[]{:S(2)}) %copy-start) | copy-done | bytes 1114136
  47.6 5.9 %k3.1 = (f32[8,48,128]{2,1,0:T(8,128)}, f32[16,16,128]{2,1,0:T(8,128)}, f32[16,16,128]{2,1,0:T(8,128)}, f32[17,16,128]{2,1,0:T(8,128)}, f32[17,16,128]{2,1,0:T(8...) custom-call(f32[16,136,128]{2,1,0:T(8,128)} %copy-done, ...), custom_call_target="tpu_custom_call" | custom-call | tf_op jit(solution)/shard_map/k3/pallas_call | solution.py:422
  53.6 10.9 %all_to_all.20.m3 = f32[8,48,128]{2,1,0:T(8,128)} all-to-all(f32[8,48,128]{2,1,0:T(8,128)} %get-tuple-element.59), channel_id=1, replica_groups=mesh['gx'=8,'gy'=16] {'gx'}, dimensions={0} | all-to-all | bytes 393216 | tf_op jit(solution)/shard_map/all_to_all | solution.py:433
  64.4 2.5 %k4.1 = (f32[16,16,128]{2,1,0:T(8,128)}, f32[256,128]{1,0:T(8,128)}, f32[256,128]{1,0:T(8,128)}, f32[2,16,128]{2,1,0:T(8,128)}) custom-call(f32[8,48,128]{2,1,0:T(8,128)} %all_to_all.20.m3, f32[4,16,128]{2,1,0:T(8,128)} %get-tuple-element.60.own, f32[256,128]{1,0:T(8,128)} %get-tuple-element.45.v, f32[256,128]{1,0:T(8,128)} %get-tuple-element.44.w, ...), custom_call_target="tpu_custom_call" | custom-call | tf_op jit(solution)/shard_map/k4/pallas_call | solution.py:422
  66.9 3.5 %all-to-all-start.3 = ((f32[16,16,128]{2,1,0:T(8,128)}), f32[16,16,128]{2,1,0:T(8,128)S(1)}, u32[]{:S(2)}, u32[]{:S(2)}) async-start(f32[16,16,128]{2,1,0:T(8,128)} %get-tuple-element.69), calls=%async_computation.3 | async-start | bytes 262144 | tf_op jit(solution)/shard_map/all_to_all | solution.py:433
  70.5 5.0 %k4b.1 = (f32[256,128]{1,0:T(8,128)}, f32[256,128]{1,0:T(8,128)}, f32[256,128]{1,0:T(8,128)}, f32[256,128]{1,0:T(8,128)}) custom-call(f32[8,48,128]{2,1,0:T(8,128)} %all_to_all.20.m3, f32[4,16,128]{2,1,0:T(8,128)} %get-tuple-element.60.own, f32[256,128]{1,0:T(8,128)} %get-tuple-element.45.v, f32[256,128]{1,0:T(8,128)} %get-tuple-element.44.w, ...), custom_call_target="tpu_custom_call" | custom-call | tf_op jit(solution)/shard_map/k4b/pallas_call | solution.py:422
  75.5 2.9 %all-to-all-done.3.m4 = f32[16,16,128]{2,1,0:T(8,128)S(1)} async-done(((f32[16,16,128]{2,1,0:T(8,128)}), f32[16,16,128]{2,1,0:T(8,128)S(1)}, u32[]{:S(2)}, u32[]{:S(2)}) %all-to-all-start.3) | async-done | bytes 131104 | tf_op jit(solution)/shard_map/all_to_all | solution.py:433
  78.4 0.0 copy-start.2
  78.4 0.7 copy-done.2
  79.1 2.5 %k5.1 = (f32[3,256,128]{2,1,0:T(8,128)}, f32[3,256,128]{2,1,0:T(8,128)}) custom-call(f32[16,16,128]{2,1,0:T(8,128)} %copy-done.2, f32[2,16,128]{2,1,0:T(8,128)} %get-tuple-element.70.own, f32[256,128]{1,0:T(8,128)} %get-tuple-element.71.dz2, f32[16,16,128]{2,1,0:T(8,128)} %get-tuple-element.46.fy, f32[256,128]{1,0:T(8,128)} %get-tuple-element.63.hxpp, ...), custom_call_target="tpu_custom_call" | custom-call | tf_op jit(solution)/shard_map/k5/pallas_call | solution.py:422
Async XLA Ops:
  3.2 14.7 %all-to-all-start = ((f32[8,104,128]{2,1,0:T(8,128)}), f32[8,104,128]{2,1,0:T(8,128)S(1)}, u32[]{:S(2)}, u32[]{:S(2)}) async-start(f32[8,104,128]{2,1,0:T(8,128)} %get-tuple-element.43), calls=%async_computation | async-start | bytes 851968 | tf_op jit(solution)/shard_map/all_to_all | solution.py:433
  17.9 0.8 copy-start.1
  21.4 25.3 %all-to-all-start.1 = ((f32[16,136,128]{2,1,0:T(8,128)}), f32[16,136,128]{2,1,0:T(8,128)S(1)}, u32[]{:S(2)}, u32[]{:S(2)}) async-start(f32[16,136,128]{2,1,0:T(8,128)} %get-tuple-element.49), calls=%async_computation.1 | async-start | bytes 2228224 | tf_op jit(solution)/shard_map/all_to_all | solution.py:433
  46.6 1.0 %copy-start = (f32[16,136,128]{2,1,0:T(8,128)}, f32[16,136,128]{2,1,0:T(8,128)S(1)}, u32[]{:S(2)}) copy-start(f32[16,136,128]{2,1,0:T(8,128)S(1)} %all-to-all-done.1.m2) | copy-start | bytes 3342340
  66.9 11.5 %all-to-all-start.3 = ((f32[16,16,128]{2,1,0:T(8,128)}), f32[16,16,128]{2,1,0:T(8,128)S(1)}, u32[]{:S(2)}, u32[]{:S(2)}) async-start(f32[16,16,128]{2,1,0:T(8,128)} %get-tuple-element.69), calls=%async_computation.3 | async-start | bytes 262144 | tf_op jit(solution)/shard_map/all_to_all | solution.py:433
  78.4 0.7 copy-start.2
where the time goes:
time: 82.3 us; the launch traced here: 81.6 us
  waiting for transfers between devices  26.9 us (33%)
  Pallas kernels  24.7 us (30%)
  starting transfers between devices  16 us (19%)
  blocking collectives  10.9 us (13%)
  local copies, waits for them, and re-layouts  2.45 us (3%)
    all_to_all x3, waiting for transfers between devices, exchange(): lax.all_to_all(message, axis, split_axis=0, concat_axis=0, tiled=True)  26.9 us
    pallas_call x8, Pallas kernels, call(): pl.pallas_call(kernel, out_shape=[jax.ShapeDtypeStruct(s, F32) for s in s...  24.7 us
    all_to_all x3, starting transfers between devices, exchange(): lax.all_to_all(message, axis, split_axis=0, concat_axis=0, tiled=True)  16 us
    all_to_all x1, blocking collectives, exchange(): lax.all_to_all(message, axis, split_axis=0, concat_axis=0, tiled=True)  10.9 us
    unnamed x6, local copies, waits for them, and re-layouts  2.45 us
  transfers between devices with their start and end apart: 3, of which 3 were waited for; matrix products, arithmetic and copies ran while one was open for 0% of the time, Pallas kernels for 11%

commit v1 on v0

--- a/solution.py
+++ b/solution.py
@@ -67,6 +67,30 @@
             a, c = a * pltpu.roll(a * rb, step, 1), c * pltpu.roll(c * rb, NZ - step, 1)
         step *= 2
     return d / e
+
+
+def z_factors(w, out):
+    lane = iota(w.shape, 1)
+    a = jnp.where(lane == 0, 0.0, 1.0)
+    c = jnp.where(lane == NZ - 1, 0.0, 1.0)
+    e = w + (2.0 - a - c)
+    for k in range(7):
+        step = 1 << k
+        rb = 1.0 / (e + a + c)
+        low = a * pltpu.roll(rb, step, 1)
+        high = c * pltpu.roll(rb, NZ - step, 1)
+        out[2 * k], out[2 * k + 1] = low, high
+        e = e + low * pltpu.roll(e, step, 1) + high * pltpu.roll(e, NZ - step, 1)
+        if k < 6:
+            a, c = low * pltpu.roll(a, step, 1), high * pltpu.roll(c, NZ - step, 1)
+    out[14] = 1.0 / e
+
+
+def z_apply(d, f):
+    for k in range(7):
+        step = 1 << k
+        d = d + f[2 * k] * pltpu.roll(d, step, 1) + f[2 * k + 1] * pltpu.roll(d, NZ - step, 1)
+    return d * f[14]
 
 
 def pivots(ws):
@@ -163,7 +187,18 @@
     return part(hi) + part(mid) + part(low)
 
 
-def k1(e, h, mat, perm, cond, cells, dest, tgt, gain, msg, w_o, v_o, fx_o, bx_o):
+def k1(e_h, h_h, mat_h, perm_h, cond_h, cells_h, dest_h, tgt_h, gain_h, msg, w_o, v_o, fx_o, bx_o,
+       ez, ey_first, hz_last, mat, perm, cond, cells, dest, tgt, gain, sem):
+    copies = [
+        pltpu.make_async_copy(src, dst, sem.at[k])
+        for k, (src, dst) in enumerate([
+            (perm_h, perm), (cond_h, cond), (mat_h, mat), (dest_h, dest), (cells_h, cells), (tgt_h, tgt),
+            (gain_h, gain), (e_h.at[2], ez), (e_h.at[1, rows(0)], ey_first), (h_h.at[2, rows(CX - 1)], hz_last)])
+    ]
+    for copy in copies:
+        copy.start()
+    for copy in copies[:3]:
+        copy.wait()
     me = lax.axis_index("gx")
     ws = [(perm[k] + 8.0 * cond[k]) * (1.0 / 4096.0) for k in range(8)]
     vs = [(perm[k] - 8.0 * cond[k]) * (1.0 / 4096.0) for k in range(8)]
@@ -185,6 +220,8 @@
     for x in range(CX):
         fx_o[x] = fwd[x]
         bx_o[x] = bwd[x]
+    for copy in copies[3:]:
+        copy.wait()
     to = dest[...]
     to_b = jnp.broadcast_to(to, (128, 128))
     same = (to_b.T == to_b) & (iota((128, 128), 0) < iota((128, 128), 1))
@@ -196,22 +233,20 @@
     from_cell = (iota((CELLS, 128), 0) == cells[...]).astype(BF16)
     nt = (((1,), (1,)), ((), ()))
     pickm = lax.dot_general(hot.astype(BF16), from_cell, nt, preferred_element_type=F32)
-    vals = split_dot(pickm.astype(BF16), e[2]) * slot_gain
+    vals = split_dot(pickm.astype(BF16), ez[...]) * slot_gain
     code_at = jnp.where(iota((8, 128), 0) == dest_x, (tgt[...] + 1).astype(F32), 0.0).astype(BF16)
     lane_hot = (iota((128, 128), 0) == lane_slot).astype(BF16)
     code = lax.dot_general(code_at, lane_hot, nt, preferred_element_type=F32)
-    hz_last = h[2, rows(CX - 1), :]
-    ey_first = e[1, rows(0), :]
     for d in range(GX):
         msg[d, 0:32, :] = vals[d * 32:(d + 1) * 32]
-        msg[d, R1_HALO:R1_HALO + 16, :] = jnp.where(d > me, hz_last, ey_first)
+        msg[d, R1_HALO:R1_HALO + 16, :] = jnp.where(d > me, hz_last[...], ey_first[...])
         msg[d, R1_G11:R1_G11 + 16, :] = bwd[0]
         msg[d, R1_G1N:R1_G1N + 16, :] = link
         msg[d, R1_GNN:R1_GNN + 16, :] = fwd[CX - 1]
         msg[d, R1_CODE:R1_CODE + 8, :] = jnp.broadcast_to(code[d:d + 1], (8, NZ))
 
 
-def k1b(w, fy_o, by_o, g_o):
+def k1b(e, h, w, v, fy_o, by_o, g_o, hyp_o, dz_o, hxpp_o, dy2_o, zx_o, zy_o, hxp_s, ey1_s, dy1_s):
     ws = [w[strided(y), :] for y in range(CY)]
     fwd, bwd, link = pivots(ws)
     for y in range(CY):
@@ -220,9 +255,40 @@
     g_o[0] = bwd[0]
     g_o[1] = link
     g_o[2] = fwd[CY - 1]
-
-
-def k2(m1, e, h, w, v, fy, by, g, msg, hzp_o, dx_o, halo_o):
+    z_factors(w[rows(0), :], zx_o)
+    z_factors(w[strided(CY - 1), :], zy_o)
+    prev_hyp = None
+    prev_hz = None
+    for x in range(CX):
+        ez = e[2, rows(x), :]
+        hx = h[0, rows(x), :]
+        ex = e[0, rows(x), :]
+        hz = h[2, rows(x), :]
+        hxp = hx - HS * (y_up(ez, 0.0) - ez)
+        hxp_s[rows(x), :] = hxp
+        hyp = h[1, rows(x), :] - HS * (z_up(ex) - ex)
+        hyp_o[rows(x), :] = hyp
+        curl_z = hyp - (hx - y_down(hx, 0.0))
+        curl_y = (hxp - z_down(hxp)) - hz
+        if x > 0:
+            curl_z = curl_z - prev_hyp
+            curl_y = curl_y + prev_hz
+        prev_hyp = hyp
+        prev_hz = hz
+        dz_o[rows(x), :] = v[rows(x), :] * ez + INV * curl_z
+        dy1_s[rows(x), :] = v[rows(x), :] * e[1, rows(x), :] + INV * curl_y
+    for q in range(4):
+        part = pl.ds(q * 64, 64)
+        ey1_s[part, :] = z_solve(w[part, :], dy1_s[part, :])
+    for x in range(CX):
+        ey1 = ey1_s[rows(x), :]
+        dey1 = HS * (z_up(ey1) - ey1)
+        hx1 = hxp_s[rows(x), :] + dey1
+        hxpp_o[rows(x), :] = hx1 + dey1
+        dy2_o[rows(x), :] = v[rows(x), :] * ey1 + INV * (hx1 - z_down(hx1))
+
+
+def k2(m1, e, h, v, fy, by, g, msg, hzp_o, dx_o, halo_o, h_o, hr_o, be_o, de_o):
     gx = lax.axis_index("gx")
     me = lax.axis_index("gy")
     lo = jnp.maximum(gx - 1, 0) * R1 + R1_HALO
@@ -257,9 +323,6 @@
         msg[d, R2_G11:R2_G11 + 16, :] = g[0]
         msg[d, R2_G1N:R2_G1N + 16, :] = g[1]
         msg[d, R2_GNN:R2_GNN + 16, :] = g[2]
-
-
-def k2b(m1, h_o, hr_o, be_o, de_o):
     static_fold(
         GX,
         lambda j: m1[pl.ds(j * R1 + R1_G11, 16), :],
@@ -268,9 +331,8 @@
         h_o, hr_o, be_o, de_o)
 
 
-def k3(m2, e, h, w, v, hzp, dx, hz_low, fy, fx, bx, hx_c, hrx_c, bex, dex,
-       msg, hy_c, hry_c, bey, dey, ex1_o, hz1_o, hz1m_o, inj_o, hyp_o, hxpp_o, hzpp_o,
-       dz_o, dy2_o, own_o, hxp_s, ey1_s, dy1_s):
+def k3(m2, v, hzp, dx, fy, fx, bx, hz_low, hx_c, hrx_c, bex, dex, hyp, dz0, hxpp0, dy20, zx, zy,
+       msg, hy_c, hry_c, bey, dey, ex1_o, hz1_o, hz1m_o, inj_o, hxpp_o, hzpp_o, dz_o, dy2_o, own_o):
     gx = lax.axis_index("gx")
     me = lax.axis_index("gy")
     static_fold(GY, lambda j: m2[j, R2_G11:R2_G11 + 16, :], lambda j: m2[j, R2_G1N:R2_G1N + 16, :],
@@ -304,47 +366,33 @@
         part = split_dot(land, vals)
         inj = part if inj is None else inj + part
     inj_o[...] = inj
-    prev_hyp = None
-    for x in range(CX):
-        ez = e[2, rows(x), :]
-        hx = h[0, rows(x), :]
-        ex = e[0, rows(x), :]
-        hz = h[2, rows(x), :]
-        hxp = hx - HS * (y_up(ez, ez_high[x:x + 1]) - ez)
-        hxp_s[rows(x), :] = hxp
-        hyp = h[1, rows(x), :] - HS * (z_up(ex) - ex)
-        hyp_o[rows(x), :] = hyp
-        curl = hyp - (hx - y_down(hx, hx_low[x:x + 1])) - inj_o[rows(x), :]
-        if x > 0:
-            curl = curl - prev_hyp
-        prev_hyp = hyp
-        dz_o[rows(x), :] = v[rows(x), :] * ez + INV * curl
-        hz_prev = h[2, rows(x - 1), :] if x > 0 else hz_low[...]
-        curl = (hxp - z_down(hxp)) - (hz - hz_prev)
-        dy1_s[rows(x), :] = v[rows(x), :] * e[1, rows(x), :] + INV * curl
-    for q in range(4):
-        part = pl.ds(q * 64, 64)
-        ey1_s[part, :] = z_solve(w[part, :], dy1_s[part, :])
+    dz_o[...] = dz0[...] - INV * inj
+    dz_o[strided(0), :] = dz_o[strided(0), :] + INV * hx_low
+    c_h = -HS * ez_high
+    c_e = z_apply(INV * (c_h - z_down(c_h)), zy)
+    c_d = HS * (z_up(c_e) - c_e)
+    c_1 = c_h + c_d
+    b_e = z_apply(INV * hz_low[...], zx)
+    b_d = HS * (z_up(b_e) - b_e)
+    hxpp_o[...] = hxpp0[...]
+    hxpp_o[rows(0), :] = hxpp_o[rows(0), :] + (b_d + b_d)
+    hxpp_o[strided(CY - 1), :] = hxpp_o[strided(CY - 1), :] + (c_1 + c_d)
     prev = None
     for x in range(CX):
-        ey1 = ey1_s[rows(x), :]
-        dey1 = HS * (z_up(ey1) - ey1)
-        hx1 = hxp_s[rows(x), :] + dey1
-        hxpp_o[rows(x), :] = hx1 + dey1
         ex1 = ex1_o[rows(x), :]
         dex1 = HS * (y_up(ex1, right[x:x + 1]) - ex1)
         hz1 = hzp[rows(x), :] + dex1
         hz1_o[rows(x), :] = hz1
         hzpp = hz1 + dex1
         hzpp_o[rows(x), :] = hzpp
-        curl = (hx1 - z_down(hx1)) - hzpp
-        if x > 0:
-            curl = curl + prev
+        curl = prev - hzpp if x > 0 else -hzpp
         prev = hzpp
-        dy2_o[rows(x), :] = v[rows(x), :] * ey1 + INV * curl
+        dy2_o[rows(x), :] = dy20[rows(x), :] + INV * curl
+    dy2_o[rows(0), :] = dy2_o[rows(0), :] + v[rows(0), :] * b_e + INV * (b_d - z_down(b_d))
+    dy2_o[strided(CY - 1), :] = dy2_o[strided(CY - 1), :] + v[strided(CY - 1), :] * c_e + INV * (c_1 - z_down(c_1))
     fwd = [fx[x] for x in range(CX)]
     bwd = [bx[x] for x in range(CX)]
-    tz = -INV * hyp_o[rows(CX - 1), :]
+    tz = -INV * hyp[rows(CX - 1), :]
     p1, p2 = ends([dz_o[rows(x), :] for x in range(CX)], fwd, bwd)
     mz, nz = to_messages(gx, p1, p2 + tz, hx_c, hrx_c, bex, dex)
     ty = INV * hzpp_o[rows(CX - 1), :]
@@ -357,7 +405,7 @@
         msg[d, 32:48, :] = tz
 
 
-def k4(m3, own, v, w, dz, fx, fy, by, hyp, hxpp, inj, hx_c, hrx_c, bex, dex, hy_c, hry_c, bey, dey,
+def k4(m3, own, v, dz, fx, fy, by, hyp, hxpp, inj, hx_c, hrx_c, bex, dex, hy_c, hry_c, bey, dey,
        msg, dz2_o, hypp_o, own_o):
     gx = lax.axis_index("gx")
     me = lax.axis_index("gy")
@@ -382,49 +430,60 @@
 
 
 def k4b(m3, own, v, w, fx, ex1, hz1, hz1m, hypp, hzpp, dy2, hx_c, hrx_c, bex, dex,
-        ex2_o, ey2_o, hy2_o, hz2_o, dx2_s):
+        e_o, h_o, ex2_s, ey2_s, hy2_s, hz2_s, dx2_s, sem):
     gx = lax.axis_index("gx")
     left, right = interface(GX, gx, own[2], own[3], lambda j: m3[j, 16:32, :], hx_c, hrx_c, bex, dex)
     us = block_solve([dy2[rows(x), :] for x in range(CX)], [fx[x] for x in range(CX)], left, right)
     for x in range(CX):
-        ey2_o[rows(x), :] = us[x]
-        hz2_o[rows(x), :] = hzpp[rows(x), :] - HS * ((us[x + 1] if x < CX - 1 else right) - us[x])
+        ey2_s[rows(x), :] = us[x]
+        hz2_s[rows(x), :] = hzpp[rows(x), :] - HS * ((us[x + 1] if x < CX - 1 else right) - us[x])
         hz = hz1[rows(x), :]
         hy = hypp[rows(x), :]
         curl = (hz - y_down(hz, hz1m[x:x + 1, :])) - (hy - z_down(hy))
         dx2_s[rows(x), :] = v[rows(x), :] * ex1[rows(x), :] + INV * curl
+    copies = [pltpu.make_async_copy(ey2_s, e_o.at[1], sem.at[0]), pltpu.make_async_copy(hz2_s, h_o.at[2], sem.at[1]),
+              pltpu.make_async_copy(ex2_s, e_o.at[0], sem.at[2]), pltpu.make_async_copy(hy2_s, h_o.at[1], sem.at[3])]
+    copies[0].start()
+    copies[1].start()
     for q in range(4):
         part = pl.ds(q * 64, 64)
         ex2 = z_solve(w[part, :], dx2_s[part, :])
-        ex2_o[part, :] = ex2
-        hy2_o[part, :] = hypp[part, :] - HS * (z_up(ex2) - ex2)
-
-
-def k5(m4, own, dz2, fy, hxpp, ex2, ey2, hy2, hz2, hy_c, hry_c, bey, dey, e_o, h_o):
+        ex2_s[part, :] = ex2
+        hy2_s[part, :] = hypp[part, :] - HS * (z_up(ex2) - ex2)
+    copies[2].start()
+    copies[3].start()
+    for copy in copies:
+        copy.wait()
+
+
+def k5(m4, own, dz2, fy, hxpp, hy_c, hry_c, bey, dey, e_in, h_in, e_o, h_o, ez2_s, hx2_s, sem):
     me = lax.axis_index("gy")
     left, right = interface(GY, me, own[0], own[1], lambda j: m4[j], hy_c, hry_c, bey, dey)
     us = block_solve([dz2[strided(y), :] for y in range(CY)], [fy[y] for y in range(CY)], left, right)
     for y in range(CY):
-        e_o[2, strided(y), :] = us[y]
-    e_o[0] = ex2[...]
-    e_o[1] = ey2[...]
-    h_o[1] = hy2[...]
-    h_o[2] = hz2[...]
-    for x in range(CX):
-        ez2 = e_o[2, rows(x), :]
-        h_o[0, rows(x), :] = hxpp[rows(x), :] - HS * (y_up(ez2, right[x:x + 1]) - ez2)
-
-
-def call(kernel, shapes, args, scratch=(), smem=()):
-    specs = [
-        pl.BlockSpec(memory_space=pltpu.SMEM if k in smem else pltpu.VMEM) for k in range(len(args))
-    ]
+        ez2_s[strided(y), :] = us[y]
+    first = pltpu.make_async_copy(ez2_s, e_o.at[2], sem.at[0])
+    first.start()
+    for x in range(CX):
+        ez2 = ez2_s[rows(x), :]
+        hx2_s[rows(x), :] = hxpp[rows(x), :] - HS * (y_up(ez2, right[x:x + 1]) - ez2)
+    second = pltpu.make_async_copy(hx2_s, h_o.at[0], sem.at[1])
+    second.start()
+    first.wait()
+    second.wait()
+
+
+def call(kernel, shapes, args, scratch=(), hbm_in=(), hbm_out=(), alias=None):
+    def spec(in_hbm):
+        return pl.BlockSpec(memory_space=pltpu.HBM if in_hbm else pltpu.VMEM)
     return pl.pallas_call(
         kernel,
         out_shape=[jax.ShapeDtypeStruct(s, F32) for s in shapes],
-        in_specs=specs,
-        out_specs=[pl.BlockSpec(memory_space=pltpu.VMEM) for _ in shapes],
-        scratch_shapes=[pltpu.VMEM(s, F32) for s in scratch],
+        in_specs=[spec(k in hbm_in) for k in range(len(args))],
+        out_specs=[spec(k in hbm_out) for k in range(len(shapes))],
+        scratch_shapes=[pltpu.VMEM(s, F32) if isinstance(s, tuple) else s for s in scratch],
+        input_output_aliases=alias or {},
+        compiler_params=pltpu.CompilerParams(vmem_limit_bytes=12 << 20),
         name=kernel.__name__,
     )(*args)
 
@@ -443,31 +502,41 @@
     e = e_fields.reshape(3, CELLS, NZ)
     h = h_fields.reshape(3, CELLS, NZ)
     mat = material.reshape(CELLS, NZ)
+    row = (1, 128)
+    dma = pltpu.SemaphoreType.DMA
+    hbm = [pltpu.with_memory_space_constraint(a, pltpu.HBM) for a in (
+        e, h, mat, permittivity, conductivity, electrode_cells.reshape(row),
+        electrode_dest.reshape(row), target_cells.reshape(row), electrode_gain.reshape(row))]
     msg1, w, v, fx, bx = call(
         k1, [(GX, R1, NZ), FIELD, FIELD, LINE, LINE],
-        (e, h, mat, permittivity, conductivity, electrode_cells.reshape(1, 128),
-         electrode_dest.reshape(1, 128), target_cells.reshape(1, 128), electrode_gain.reshape(1, 128)),
-        smem=(3, 4))
+        hbm,
+        scratch=[FIELD, FACE, FACE, pltpu.VMEM(FIELD, jnp.int32), pltpu.SMEM((8,), F32), pltpu.SMEM((8,), F32),
+                 pltpu.VMEM(row, jnp.int32), pltpu.VMEM(row, jnp.int32), pltpu.VMEM(row, jnp.int32), row, dma((10,))],
+        hbm_in=range(9))
     m1 = exchange(msg1, "gx").reshape(GX * R1, NZ)
-    fy, by, g = call(k1b, [LINE, LINE, (3,) + FACE], (w,))
-    msg2, hzp, dx, hz_low = call(
-        k2, [(GY, R2, NZ), FIELD, FIELD, FACE], (m1, e, h, w, v, fy, by, g))
+    (fy, by, g, hyp, dz0, hxpp0, dy20, zx, zy) = call(
+        k1b, [LINE, LINE, (3,) + FACE, FIELD, FIELD, FIELD, FIELD, (15,) + FACE, (15,) + FACE],
+        (e, h, w, v), scratch=[FIELD, FIELD, FIELD])
+    (msg2, hzp, dx, hz_low, *xstat) = call(
+        k2, [(GY, R2, NZ), FIELD, FIELD, FACE, (GX,) + FACE, (GX,) + FACE, (GX + 1,) + FACE, (GX + 1,) + FACE],
+        (m1, e, h, v, fy, by, g))
     m2 = exchange(msg2, "gy")
-    xstat = call(k2b, [(GX,) + FACE, (GX,) + FACE, (GX + 1,) + FACE, (GX + 1,) + FACE], (m1,))
-    (msg3, hyc, hryc, bey, dey, ex1, hz1, hz1m, inj, hyp, hxpp, hzpp, dz, dy2, own) = call(
+    (msg3, hyc, hryc, bey, dey, ex1, hz1, hz1m, inj, hxpp, hzpp, dz, dy2, own) = call(
         k3, [(GX, R3, NZ), (GY,) + FACE, (GY,) + FACE, (GY + 1,) + FACE, (GY + 1,) + FACE,
-             FIELD, FIELD, FACE, FIELD, FIELD, FIELD, FIELD, FIELD, FIELD, (4,) + FACE],
-        (m2, e, h, w, v, hzp, dx, hz_low, fy, fx, bx, *xstat), scratch=[FIELD, FIELD, FIELD])
+             FIELD, FIELD, FACE, FIELD, FIELD, FIELD, FIELD, FIELD, (4,) + FACE],
+        (m2, v, hzp, dx, fy, fx, bx, hz_low, *xstat, hyp, dz0, hxpp0, dy20, zx, zy))
     ystat = (hyc, hryc, bey, dey)
     m3 = exchange(msg3, "gx")
     msg4, dz2, hypp, own2 = call(
         k4, [(GY, R4, NZ), FIELD, FIELD, (2,) + FACE],
-        (m3, own, v, w, dz, fx, fy, by, hyp, hxpp, inj, *xstat, *ystat))
+        (m3, own, v, dz, fx, fy, by, hyp, hxpp, inj, *xstat, *ystat))
     m4 = exchange(msg4, "gy")
-    ex2, ey2, hy2, hz2 = call(
-        k4b, [FIELD] * 4, (m3, own, v, w, fx, ex1, hz1, hz1m, hypp, hzpp, dy2, *xstat), scratch=[FIELD])
     e_out, h_out = call(
-        k5, [(3,) + FIELD, (3,) + FIELD], (m4, own2, dz2, fy, hxpp, ex2, ey2, hy2, hz2, *ystat))
+        k4b, [(3,) + FIELD, (3,) + FIELD], (m3, own, v, w, fx, ex1, hz1, hz1m, hypp, hzpp, dy2, *xstat),
+        scratch=[FIELD] * 5 + [dma((4,))], hbm_out=(0, 1))
+    e_out, h_out = call(
+        k5, [(3,) + FIELD, (3,) + FIELD], (m4, own2, dz2, fy, hxpp, *ystat, e_out, h_out),
+        scratch=[FIELD, FIELD, dma((2,))], hbm_in=(9, 10), hbm_out=(0, 1), alias={9: 0, 10: 1})
     return e_out.reshape(3, CX, CY, NZ), h_out.reshape(3, CX, CY, NZ)
 
 

time: 82.3 us -> 66.5 us (0.81)
  blocking collectives: 10.9 us -> 33.9 us
  waiting for transfers between devices: 26.9 us -> 9.73 us
  Pallas kernels: 24.7 us -> 12.2 us
  starting transfers between devices: 16 us -> 8.92 us
  local copies, waits for them, and re-layouts: 2.45 us -> 0.66 us
    all_to_all x1 -> x2, blocking collectives: 10.9 us -> 33.9 us  [exchange(): lax.all_to_all(message, axis, split_axis=0, concat_axis=0, tiled=True)]
    all_to_all x3 -> x2, waiting for transfers between devices: 26.9 us -> 9.73 us  [exchange(): lax.all_to_all(message, axis, split_axis=0, concat_axis=0, tiled=True)]
    pallas_call x8 -> x7, Pallas kernels: 24.7 us -> 12.2 us  [call(): pl.pallas_call(kernel, out_shape=[jax.ShapeDtypeStruct(s, F32) for s in s...]
    all_to_all x3 -> x2, starting transfers between devices: 16 us -> 8.92 us  [exchange(): lax.all_to_all(message, axis, split_axis=0, concat_axis=0, tiled=True)]
    unnamed x6 -> x8, local copies, waits for them, and re-layouts: 2.45 us -> 0.66 us
  transfers between devices with their start and end apart: 3 -> 2, of which waited for: 3 -> 2; matrix products, arithmetic and copies ran while one was open for 0% -> 0% of each run, Pallas kernels for 11% -> 10%
where the time goes in v1:
time: 66.5 us; the launch traced here: 66.2 us
  blocking collectives  33.9 us (51%)
  Pallas kernels  12.2 us (18%)
  waiting for transfers between devices  9.73 us (15%)
  starting transfers between devices  8.92 us (13%)
  between operations  0.72 us (1%)
    all_to_all x2, blocking collectives, exchange(): lax.all_to_all(message, axis, split_axis=0, concat_axis=0, tiled=True)  33.9 us
    pallas_call x7, Pallas kernels, call(): pl.pallas_call(kernel, out_shape=[jax.ShapeDtypeStruct(s, F32) for s in s...  12.2 us
    all_to_all x2, waiting for transfers between devices, exchange(): lax.all_to_all(message, axis, split_axis=0, concat_axis=0, tiled=True)  9.73 us
    all_to_all x2, starting transfers between devices, exchange(): lax.all_to_all(message, axis, split_axis=0, concat_axis=0, tiled=True)  8.92 us
  transfers between devices with their start and end apart: 2, of which 2 were waited for; matrix products, arithmetic and copies ran while one was open for 0% of the time, Pallas kernels for 10%

profile of v1, /device:TPU:0, one launch (start us, length us, event | category | flops | bytes accessed | tf_op | source)
XLA Modules:
  0.0 66.2 jit_solution(18381775743837995092)
XLA Ops:
  0.6 0.0 copy-start.1
  0.6 0.0 copy-start
  0.7 2.6 %k1.1 = (f32[8,104,128]{2,1,0:T(8,128)}, f32[256,128]{1,0:T(8,128)S(1)}, f32[256,128]{1,0:T(8,128)S(1)}, f32[16,16,128]{2,1,0:T(8,128)S(1)}, f32[16,16,128]{2,1,0:T(8,128)S(1)}) custom-call(f32[3,256,128]{2,1,0:T(8,128)} %bitcast.10, f32[3,256,128]{2,1,0:T(8,128)} %bitcast.13, s32[256,128]{1,0:T(8,128)} %bitcast.19, f32[8]{0:T(128)} %perm_h.1, f32[8]{0:T(128)} %cond_h.1, ...), custom_call_target="tpu_custom_call" | custom-call | tf_op jit(solution)/shard_map/k1/pallas_call | solution.py:479
  3.3 5.4 %all-to-all-start = ((f32[8,104,128]{2,1,0:T(8,128)}), f32[8,104,128]{2,1,0:T(8,128)S(1)}, u32[]{:S(2)}, u32[]{:S(2)}) async-start(f32[8,104,128]{2,1,0:T(8,128)} %get-tuple-element.46), calls=%async_computation | async-start | bytes 851968 | tf_op jit(solution)/shard_map/all_to_all | solution.py:492
  8.7 0.0 copy-done.1
  8.7 0.0 copy-done
  8.7 3.3 %k1b.1 = (f32[16,16,128]{2,1,0:T(8,128)S(1)}, f32[16,16,128]{2,1,0:T(8,128)S(1)}, f32[3,16,128]{2,1,0:T(8,128)S(1)}, f32[256,128]{1,0:T(8,128)S(1)}, f32[256,128...) custom-call(f32[3,256,128]{2,1,0:T(8,128)S(1)} %bitcast.11, ...), custom_call_target="tpu_custom_call" | custom-call | tf_op jit(solution)/shard_map/k1b/pallas_call | solution.py:479
  12.0 0.0 copy-start.2
  12.0 0.6 copy-done.2
  12.6 5.3 %all-to-all-done = f32[8,104,128]{2,1,0:T(8,128)S(1)} async-done(((f32[8,104,128]{2,1,0:T(8,128)}), f32[8,104,128]{2,1,0:T(8,128)S(1)}, u32[]{:S(2)}, u32[]{:S(2)}) %all-to-all-start) | async-done | bytes 426016 | tf_op jit(solution)/shard_map/all_to_all | solution.py:492
  18.0 0.2 k2.1
  18.2 0.0 copy-start.3
  18.2 24.7 %all_to_all.20.m2 = f32[16,136,128]{2,1,0:T(8,128)S(1)} all-to-all(f32[16,136,128]{2,1,0:T(8,128)S(1)} %get-tuple-element.52), channel_id=1, replica_groups=mesh['gx'=8,'gy'=16] {'gy'}, dimensions={0} | all-to-all | bytes 2228224 | tf_op jit(solution)/shard_map/all_to_all | solution.py:492
  42.9 0.0 copy-done.3
  42.9 0.9 %k3.1 = (f32[8,48,128]{2,1,0:T(8,128)S(1)}, f32[16,16,128]{2,1,0:T(8,128)S(1)}, f32[16,16,128]{2,1,0:T(8,128)S(1)}, f32[17,16,128]{2,1,0:T(8,128)S(1)}, f32[17,1...) custom-call(f32[16,136,128]{2,1,0:T(8,128)S(1)} %all_to_all.20.m2, ...), custom_call_target="tpu_custom_call" | custom-call | tf_op jit(solution)/shard_map/k3/pallas_call | solution.py:479
  43.8 9.2 %all_to_all.21.m3 = f32[8,48,128]{2,1,0:T(8,128)S(1)} all-to-all(f32[8,48,128]{2,1,0:T(8,128)S(1)} %get-tuple-element.68), channel_id=1, replica_groups=mesh['gx'=8,'gy'=16] {'gx'}, dimensions={0} | all-to-all | bytes 393216 | tf_op jit(solution)/shard_map/all_to_all | solution.py:492
  53.0 0.9 %k4.1 = (f32[16,16,128]{2,1,0:T(8,128)}, f32[256,128]{1,0:T(8,128)S(1)}, f32[256,128]{1,0:T(8,128)S(1)}, f32[2,16,128]{2,1,0:T(8,128)S(1)}) custom-call(f32[8,48,128]{2,1,0:T(8,128)S(1)} %all_to_all.21.m3, f32[4,16,128]{2,1,0:T(8,128)S(1)} %get-tuple-element.69.own, f32[256,128]{1,0:T(8,128)S(1)} %get-tuple-element.47.v, ...), custom_call_target="tpu_custom_call" | custom-call | tf_op jit(solution)/shard_map/k4/pallas_call | solution.py:479
  53.9 3.5 %all-to-all-start.3 = ((f32[16,16,128]{2,1,0:T(8,128)}), f32[16,16,128]{2,1,0:T(8,128)S(1)}, u32[]{:S(2)}, u32[]{:S(2)}) async-start(f32[16,16,128]{2,1,0:T(8,128)} %get-tuple-element.77), calls=%async_computation.3 | async-start | bytes 262144 | tf_op jit(solution)/shard_map/all_to_all | solution.py:492
  57.4 3.5 %k4b.1 = (f32[3,256,128]{2,1,0:T(8,128)}, f32[3,256,128]{2,1,0:T(8,128)}) custom-call(f32[8,48,128]{2,1,0:T(8,128)S(1)} %all_to_all.21.m3, f32[4,16,128]{2,1,0:T(8,128)S(1)} %get-tuple-element.69.own, f32[256,128]{1,0:T(8,128)S(1)} %get-tuple-element.47.v, f32[256,128]{1,0:T(8,128)S(1)} %get-tuple-element.48.w, f32[16,16,128]{2,1,0:T(8,128)S(1)} %get-tuple-element.55.fx, ...), custom_call_target="tpu_custom_call" | custom-call | tf_op jit(solution)/shard_map/k4b/pallas_call | solution.py:479
  60.9 4.4 %all-to-all-done.3.m4 = f32[16,16,128]{2,1,0:T(8,128)S(1)} async-done(((f32[16,16,128]{2,1,0:T(8,128)}), f32[16,16,128]{2,1,0:T(8,128)S(1)}, u32[]{:S(2)}, u32[]{:S(2)}) %all-to-all-start.3) | async-done | bytes 131104 | tf_op jit(solution)/shard_map/all_to_all | solution.py:492
  65.3 0.8 %k5.1 = (f32[3,256,128]{2,1,0:T(8,128)}, f32[3,256,128]{2,1,0:T(8,128)}) custom-call(f32[16,16,128]{2,1,0:T(8,128)S(1)} %all-to-all-done.3.m4, f32[2,16,128]{2,1,0:T(8,128)S(1)} %get-tuple-element.78.own, f32[256,128]{1,0:T(8,128)S(1)} %get-tuple-element.79.dz2, ...), custom_call_target="tpu_custom_call", output_to_operand_aliasing={{0}: (9, {}), {1}: (10, {})} | custom-call | tf_op jit(solution)/shard_map/k5/pallas_call | solution.py:479
Async XLA Ops:
  0.6 8.0 %copy-start.1 = (f32[3,16,16,128]{3,2,1,0:T(8,128)S(1)}, f32[3,16,16,128]{3,2,1,0:T(8,128)}, u32[]{:S(2)}) copy-start(f32[3,16,16,128]{3,2,1,0:T(8,128)} %param.10) | copy-start | bytes 1179652
  0.6 8.0 %copy-start = (f32[3,16,16,128]{3,2,1,0:T(8,128)S(1)}, f32[3,16,16,128]{3,2,1,0:T(8,128)}, u32[]{:S(2)}) copy-start(f32[3,16,16,128]{3,2,1,0:T(8,128)} %param.9) | copy-start | bytes 1179652
  3.3 14.7 %all-to-all-start = ((f32[8,104,128]{2,1,0:T(8,128)}), f32[8,104,128]{2,1,0:T(8,128)S(1)}, u32[]{:S(2)}, u32[]{:S(2)}) async-start(f32[8,104,128]{2,1,0:T(8,128)} %get-tuple-element.46), calls=%async_computation | async-start | bytes 851968 | tf_op jit(solution)/shard_map/all_to_all | solution.py:492
  12.0 0.7 copy-start.2
  18.2 24.7 %copy-start.3 = (f32[15,16,128]{2,1,0:T(8,128)S(1)}, f32[15,16,128]{2,1,0:T(8,128)}, u32[]{:S(2)}) copy-start(f32[15,16,128]{2,1,0:T(8,128)} %copy-done.2) | copy-start | bytes 368644
  53.9 11.5 %all-to-all-start.3 = ((f32[16,16,128]{2,1,0:T(8,128)}), f32[16,16,128]{2,1,0:T(8,128)S(1)}, u32[]{:S(2)}, u32[]{:S(2)}) async-start(f32[16,16,128]{2,1,0:T(8,128)} %get-tuple-element.77), calls=%async_computation.3 | async-start | bytes 262144 | tf_op jit(solution)/shard_map/all_to_all | solution.py:492

commit v2 on v1

--- a/solution.py
+++ b/solution.py
@@ -17,8 +17,9 @@
 INV = 1.0 / 256.0
 
 R1_VAL, R1_HALO, R1_G11, R1_G1N, R1_GNN, R1_CODE, R1 = 0, 32, 48, 64, 80, 96, 104
-R2_VAL, R2_CODE, R2_HA, R2_HB, R2_P1, R2_P2, R2_G11, R2_G1N, R2_GNN, R2 = (
-    0, 16, 24, 40, 56, 72, 88, 104, 120, 136)
+X_CODE, X_BLOCK, X_HALO = 64, 72, 152
+Y_CODE, Y_BLOCK, Y_HALO = 64, 96, 176
+HALO = (0, 32, 0, 16)
 R3_Z, R3_Y, R3_T, R3 = 0, 16, 32, 48
 R4 = 16
 
@@ -132,10 +133,10 @@
     return us[::-1]
 
 
-def static_fold(n, g11, g1n, gnn, h_ref, hr_ref, be_ref, de_ref):
+def static_fold(n, g11, g1n, gnn, h_ref, hr_ref, be_ref, de_ref, be=None, de=None):
     zero = jnp.zeros((16, NZ), F32)
-    be = zero
-    de = zero
+    be = zero if be is None else be
+    de = zero if de is None else de
     be_ref[0] = be
     de_ref[n] = de
     for k in range(n):
@@ -152,13 +153,19 @@
         de_ref[j] = de
 
 
-def interface(n, me, own_m, own_n, recv, h_ref, hr_ref, be_ref, de_ref):
-    al = jnp.zeros((16, NZ), F32)
-    ga = jnp.zeros((16, NZ), F32)
+def incoming(n, me, recv, h_ref, hr_ref, al=None, ga=None):
+    zero = jnp.zeros((16, NZ), F32)
+    al = zero if al is None else al
+    ga = zero if ga is None else ga
     for k in range(n - 1):
         al = jnp.where(k < me, recv(k) + h_ref[k] * al, al)
         j = n - 1 - k
         ga = jnp.where(j > me, recv(j) + hr_ref[j] * ga, ga)
+    return al, ga
+
+
+def interface(n, me, own_m, own_n, recv, h_ref, hr_ref, be_ref, de_ref, al=None, ga=None):
+    al, ga = incoming(n, me, recv, h_ref, hr_ref, al, ga)
     be, be1 = be_ref[me], be_ref[me + 1]
     de, de1 = de_ref[me], de_ref[me + 1]
     own_ga = own_n + hr_ref[me] * ga
@@ -166,6 +173,20 @@
     left = (al + be * own_ga) / (1.0 - be * de)
     right = (ga + de1 * own_al) / (1.0 - be1 * de1)
     return left, right
+
+
+def pair_terms(k, q1, q2, h_ref, hr_ref, be_ref, de_ref):
+    return q2 + h_ref[k] * be_ref[k] * q1, q1 + hr_ref[k] * de_ref[k + 1] * q2
+
+
+def faces(ref, k):
+    return [ref[k, pl.ds(16 * f, 16), :] for f in range(5)]
+
+
+def place(buf, own_at, own, others):
+    buf[own_at] = own
+    for d, value in enumerate(others, 1):
+        buf[(own_at + 4 - d) & 3] = value
 
 
 def to_messages(me, p1, p2, h_ref, hr_ref, be_ref, de_ref):
@@ -288,7 +309,7 @@
         dy2_o[rows(x), :] = v[rows(x), :] * ey1 + INV * (hx1 - z_down(hx1))
 
 
-def k2(m1, e, h, v, fy, by, g, msg, hzp_o, dx_o, halo_o, h_o, hr_o, be_o, de_o):
+def k2(m1, e, h, v, fy, by, g, mx1, mx2, mx3, own_o, hzp_o, dx_o, halo_o, h_o, hr_o, be_o, de_o, vals_s):
     gx = lax.axis_index("gx")
     me = lax.axis_index("gy")
     lo = jnp.maximum(gx - 1, 0) * R1 + R1_HALO
@@ -309,20 +330,20 @@
     p1, p2 = ends([dx_o[strided(y), :] for y in range(CY)], fwd, bwd)
     t = -INV * hzp_o[strided(CY - 1), :]
     p2 = p2 + t
-    ez_first = e[2, strided(0), :]
-    hx_last = h[0, strided(CY - 1), :]
+    for to in range(4):
+        for r in range(2):
+            for y in range(4):
+                at = (r * 4 + y) * 8
+                vals_s[to, at:at + 8, :] = m1[pl.ds(r * GY + 4 * y + to, 8, stride=R1), :]
     code = m1[pl.ds(R1_CODE, 8, stride=R1), :]
-    for d in range(GY):
-        for r in range(2):
-            msg[d, r * 8:r * 8 + 8, :] = m1[pl.ds(r * GY + d, 8, stride=R1), :]
-        msg[d, R2_CODE:R2_CODE + 8, :] = code
-        msg[d, R2_HA:R2_HA + 16, :] = jnp.where(d > me, hx_last, ez_first)
-        msg[d, R2_HB:R2_HB + 16, :] = t
-        msg[d, R2_P1:R2_P1 + 16, :] = p1
-        msg[d, R2_P2:R2_P2 + 16, :] = p2
-        msg[d, R2_G11:R2_G11 + 16, :] = g[0]
-        msg[d, R2_G1N:R2_G1N + 16, :] = g[1]
-        msg[d, R2_GNN:R2_GNN + 16, :] = g[2]
+    for d, ref in enumerate((own_o, mx1, mx2, mx3)):
+        ref[0:64, :] = vals_s[(me + d) & 3]
+        ref[X_CODE:X_CODE + 8, :] = code
+        for f, face in enumerate((p1, p2, g[0], g[1], g[2])):
+            ref[X_BLOCK + 16 * f:X_BLOCK + 16 * f + 16, :] = face
+    mx1[X_HALO:X_HALO + 16, :] = h[0, strided(CY - 1), :]
+    mx1[X_HALO + 16:X_HALO + 32, :] = t
+    mx3[X_HALO:X_HALO + 16, :] = e[2, strided(0), :]
     static_fold(
         GX,
         lambda j: m1[pl.ds(j * R1 + R1_G11, 16), :],
@@ -331,38 +352,81 @@
         h_o, hr_o, be_o, de_o)
 
 
-def k3(m2, v, hzp, dx, fy, fx, bx, hz_low, hx_c, hrx_c, bex, dex, hyp, dz0, hxpp0, dy20, zx, zy,
-       msg, hy_c, hry_c, bey, dey, ex1_o, hz1_o, hz1m_o, inj_o, hxpp_o, hzpp_o, dz_o, dy2_o, own_o):
+def k2c(own, r1, r2, r3, my1, my2, my3, own_o, blk_o, h_o, hr_o, be_o, de_o):
+    at = lax.axis_index("gy") & 3
+    to = lax.axis_index("gy") >> 2
+    srcs = (own, r1, r2, r3)
+    place(blk_o, at, own[X_BLOCK:X_HALO, :], [r[X_BLOCK:X_HALO, :] for r in srcs[1:]])
+    static_fold(4, lambda k: blk_o[k, 32:48, :], lambda k: blk_o[k, 48:64, :], lambda k: blk_o[k, 64:80, :],
+                h_o, hr_o, be_o, de_o)
+    terms = [pair_terms(k, blk_o[k, 0:16, :], blk_o[k, 16:32, :], h_o, hr_o, be_o, de_o) for k in range(4)]
+    al, ga, link = terms[0][0], terms[3][1], h_o[0]
+    for k in range(1, 4):
+        al = terms[k][0] + h_o[k] * al
+        ga = terms[3 - k][1] + hr_o[3 - k] * ga
+        link = link * h_o[k]
+    for d, ref in enumerate((own_o, my1, my2, my3)):
+        y = (to + d) & 3
+        for k, src in enumerate(srcs):
+            for r in range(2):
+                row = pl.multiple_of((r * 4 + y) * 8, 8)
+                ref[(k * 2 + r) * 8:(k * 2 + r) * 8 + 8, :] = src[pl.ds(row, 8), :]
+            ref[Y_CODE + k * 8:Y_CODE + k * 8 + 8, :] = src[X_CODE:X_CODE + 8, :]
+        for f, face in enumerate((ga, al, de_o[0], link, be_o[4])):
+            ref[Y_BLOCK + 16 * f:Y_BLOCK + 16 * f + 16, :] = face
+    my1[Y_HALO:Y_HALO + 32, :] = r1[X_HALO:X_HALO + 32, :]
+    my3[Y_HALO:Y_HALO + 16, :] = r3[X_HALO:X_HALO + 16, :]
+
+
+def k3(own, s1, s2, s3, r1, r3, blk, h0, hr0, v, hzp, dx, fy, fx, bx, hz_low, hx_c, hrx_c, bex, dex,
+       hyp, dz0, hxpp0, dy20, zx, zy,
+       msg, hs_c, hrs_c, bes, des, hg_c, hrg_c, beg, deg, tr_o, ex1_o, hz1_o, hz1m_o, inj_o, hxpp_o, hzpp_o,
+       dz_o, dy2_o, own_o, grp):
     gx = lax.axis_index("gx")
-    me = lax.axis_index("gy")
-    static_fold(GY, lambda j: m2[j, R2_G11:R2_G11 + 16, :], lambda j: m2[j, R2_G1N:R2_G1N + 16, :],
-                lambda j: m2[j, R2_GNN:R2_GNN + 16, :], hy_c, hry_c, bey, dey)
-    p1 = m2[me, R2_P1:R2_P1 + 16, :]
-    p2 = m2[me, R2_P2:R2_P2 + 16, :]
-    own_m, own_n = to_messages(me, p1, p2, hy_c, hry_c, bey, dey)
-
-    def recv(j):
-        q1 = m2[j, R2_P1:R2_P1 + 16, :]
-        q2 = m2[j, R2_P2:R2_P2 + 16, :]
-        return jnp.where(j < me, q2 + hy_c[j] * bey[j] * q1, q1 + hry_c[j] * dey[j + 1] * q2)
-
-    left, right = interface(GY, me, own_m, own_n, recv, hy_c, hry_c, bey, dey)
+    gy = lax.axis_index("gy")
+    at = gy & 3
+    me = gy >> 2
+    place(grp, me, own[Y_BLOCK:Y_HALO, :], [r[Y_BLOCK:Y_HALO, :] for r in (s1, s2, s3)])
+    static_fold(4, lambda k: grp[k, 32:48, :], lambda k: grp[k, 48:64, :], lambda k: grp[k, 64:80, :],
+                hs_c, hrs_c, bes, des)
+    static_fold(4, lambda k: blk[k, 32:48, :], lambda k: blk[k, 48:64, :], lambda k: blk[k, 64:80, :],
+                hg_c, hrg_c, beg, deg, bes[me], des[me + 1])
+
+    def group_term(k):
+        m, n = pair_terms(k, grp[k, 0:16, :], grp[k, 16:32, :], hs_c, hrs_c, bes, des)
+        return jnp.where(k < me, m, n)
+
+    def tile_term(k):
+        m, n = pair_terms(k, blk[k, 0:16, :], blk[k, 16:32, :], hg_c, hrg_c, beg, deg)
+        return jnp.where(k < at, m, n)
+
+    al, ga = incoming(4, me, group_term, hs_c, hrs_c)
+    own_m, own_n = pair_terms(at, blk[at, 0:16, :], blk[at, 16:32, :], hg_c, hrg_c, beg, deg)
+    left, right = interface(4, at, own_m, own_n, tile_term, hg_c, hrg_c, beg, deg, al, ga)
+    one = jnp.ones((16, NZ), F32)
+    to_right, to_left = one, one
+    for k in range(4):
+        to_right = jnp.where(k > at, to_right * h0[k], to_right)
+        to_left = jnp.where(k < at, to_left * hr0[k], to_left)
+    tr_o[0] = to_right
+    tr_o[1] = to_left
     us = block_solve([dx[strided(y), :] for y in range(CY)], [fy[y] for y in range(CY)], left, right)
     for y in range(CY):
         ex1_o[strided(y), :] = us[y]
-    below = jnp.maximum(me - 1, 0)
-    above = jnp.minimum(me + 1, GY - 1)
-    t = m2[below, R2_HB:R2_HB + 16, :]
-    hz1m_o[...] = jnp.where(me > 0, HS * (us[0] - left) - 240.0 * t, 0.0)
-    hx_low = jnp.where(me > 0, m2[below, R2_HA:R2_HA + 16, :], 0.0)
-    ez_high = jnp.where(me < GY - 1, m2[above, R2_HA:R2_HA + 16, :], 0.0)
-    codes = jnp.concatenate([m2[j, R2_CODE:R2_CODE + 8, :] for j in range(GY)], axis=0).astype(BF16)
+    low = jnp.where(at > 0, r1[X_HALO:X_HALO + 32, :], s1[Y_HALO:Y_HALO + 32, :])
+    high = jnp.where(at < 3, r3[X_HALO:X_HALO + 16, :], s3[Y_HALO:Y_HALO + 16, :])
+    hz1m_o[...] = jnp.where(gy > 0, HS * (us[0] - left) - 240.0 * low[16:32], 0.0)
+    hx_low = jnp.where(gy > 0, low[0:16], 0.0)
+    ez_high = jnp.where(gy < GY - 1, high, 0.0)
+    srcs = (own, s1, s2, s3)
+    codes = jnp.concatenate([r[Y_CODE:Y_CODE + 32, :] for r in srcs], axis=0).astype(BF16)
     inj = None
     for r in range(2):
-        lane = (iota((8, 128), 1) == r * GY + me).astype(BF16)
+        lane = (iota((8, 128), 1) == r * GY + gy).astype(BF16)
         code_row = lax.dot_general(lane, codes, (((1,), (1,)), ((), ())), preferred_element_type=F32)[0:1]
         land = ((iota((CELLS, 128), 0) + 1).astype(F32) == code_row).astype(BF16)
-        vals = jnp.concatenate([m2[j, r * 8:r * 8 + 8, :] for j in range(GY)], axis=0)
+        vals = jnp.concatenate(
+            [ref[(k * 2 + r) * 8:(k * 2 + r) * 8 + 8, :] for ref in srcs for k in range(4)], axis=0)
         part = split_dot(land, vals)
         inj = part if inj is None else inj + part
     inj_o[...] = inj
@@ -405,10 +469,11 @@
         msg[d, 32:48, :] = tz
 
 
-def k4(m3, own, v, dz, fx, fy, by, hyp, hxpp, inj, hx_c, hrx_c, bex, dex, hy_c, hry_c, bey, dey,
-       msg, dz2_o, hypp_o, own_o):
+def k4(m3, own, v, dz, fx, fy, by, hyp, hxpp, inj, hx_c, hrx_c, bex, dex,
+       h0, hr0, be0, de0, hs_c, hrs_c, bes, des, hg_c, hrg_c, beg, deg, tr, msg, dz2_o, hypp_o, own_o):
     gx = lax.axis_index("gx")
-    me = lax.axis_index("gy")
+    at = lax.axis_index("gy") & 3
+    me = lax.axis_index("gy") >> 2
     left, right = interface(GX, gx, own[0], own[1], lambda j: m3[j, 0:16, :], hx_c, hrx_c, bex, dex)
     us = block_solve([dz[rows(x), :] for x in range(CX)], [fx[x] for x in range(CX)], left, right)
     t = m3[jnp.maximum(gx - 1, 0), 32:48, :]
@@ -423,10 +488,14 @@
         dz2_o[rows(x), :] = v[rows(x), :] * us[x] + INV * curl
     p1, p2 = ends([dz2_o[strided(y), :] for y in range(CY)], [fy[y] for y in range(CY)], [by[y] for y in range(CY)])
     p2 = p2 + INV * hxpp[strided(CY - 1), :]
-    m, n = to_messages(me, p1, p2, hy_c, hry_c, bey, dey)
+    m, n = pair_terms(at, p1, p2, hg_c, hrg_c, beg, deg)
     own_o[0], own_o[1] = m, n
+    m0, n0 = pair_terms(at, p1, p2, h0, hr0, be0, de0)
+    m0, n0 = tr[0] * m0, tr[1] * n0
+    group_m, group_n = pair_terms(me, n0, m0, hs_c, hrs_c, bes, des)
     for d in range(GY):
-        msg[d] = jnp.where(d > me, m, n)
+        y, x = d // 4, d % 4
+        msg[d] = jnp.where(y > me, group_m, jnp.where(y < me, group_n, jnp.where(x > at, m, n)))
 
 
 def k4b(m3, own, v, w, fx, ex1, hz1, hz1m, hypp, hzpp, dy2, hx_c, hrx_c, bex, dex,
@@ -456,9 +525,11 @@
         copy.wait()
 
 
-def k5(m4, own, dz2, fy, hxpp, hy_c, hry_c, bey, dey, e_in, h_in, e_o, h_o, ez2_s, hx2_s, sem):
-    me = lax.axis_index("gy")
-    left, right = interface(GY, me, own[0], own[1], lambda j: m4[j], hy_c, hry_c, bey, dey)
+def k5(m4, own, dz2, fy, hxpp, hs_c, hrs_c, hg_c, hrg_c, beg, deg, e_in, h_in, e_o, h_o, ez2_s, hx2_s, sem):
+    at = lax.axis_index("gy") & 3
+    me = lax.axis_index("gy") >> 2
+    al, ga = incoming(4, me, lambda k: m4[4 * k] + m4[4 * k + 1] + m4[4 * k + 2] + m4[4 * k + 3], hs_c, hrs_c)
+    left, right = interface(4, at, own[0], own[1], lambda k: m4[4 * me + k], hg_c, hrg_c, beg, deg, al, ga)
     us = block_solve([dz2[strided(y), :] for y in range(CY)], [fy[y] for y in range(CY)], left, right)
     for y in range(CY):
         ez2_s[strided(y), :] = us[y]
@@ -486,6 +557,16 @@
         compiler_params=pltpu.CompilerParams(vmem_limit_bytes=12 << 20),
         name=kernel.__name__,
     )(*args)
+
+
+def ring_x(message, d):
+    pairs = [(4 * y + x, 4 * y + (x + d) % 4) for y in range(4) for x in range(4)]
+    return lax.ppermute(message, "gy", pairs)
+
+
+def ring_y(message, d):
+    pairs = [(4 * y + x, 4 * ((y + d) % 4) + x) for y in range(4) for x in range(4)]
+    return lax.ppermute(message, "gy", pairs)
 
 
 def exchange(message, axis):
@@ -517,26 +598,35 @@
     (fy, by, g, hyp, dz0, hxpp0, dy20, zx, zy) = call(
         k1b, [LINE, LINE, (3,) + FACE, FIELD, FIELD, FIELD, FIELD, (15,) + FACE, (15,) + FACE],
         (e, h, w, v), scratch=[FIELD, FIELD, FIELD])
-    (msg2, hzp, dx, hz_low, *xstat) = call(
-        k2, [(GY, R2, NZ), FIELD, FIELD, FACE, (GX,) + FACE, (GX,) + FACE, (GX + 1,) + FACE, (GX + 1,) + FACE],
-        (m1, e, h, v, fy, by, g))
-    m2 = exchange(msg2, "gy")
-    (msg3, hyc, hryc, bey, dey, ex1, hz1, hz1m, inj, hxpp, hzpp, dz, dy2, own) = call(
-        k3, [(GX, R3, NZ), (GY,) + FACE, (GY,) + FACE, (GY + 1,) + FACE, (GY + 1,) + FACE,
-             FIELD, FIELD, FACE, FIELD, FIELD, FIELD, FIELD, FIELD, (4,) + FACE],
-        (m2, v, hzp, dx, fy, fx, bx, hz_low, *xstat, hyp, dz0, hxpp0, dy20, zx, zy))
-    ystat = (hyc, hryc, bey, dey)
+    chain = [(4,) + FACE, (4,) + FACE, (5,) + FACE, (5,) + FACE]
+    out = call(
+        k2, [(X_HALO + HALO[d], NZ) for d in (1, 2, 3)] + [
+            (X_HALO, NZ), FIELD, FIELD, FACE, (GX,) + FACE, (GX,) + FACE, (GX + 1,) + FACE, (GX + 1,) + FACE],
+        (m1, e, h, v, fy, by, g), scratch=[(4, 64, NZ)])
+    msgx, (ownx, hzp, dx, hz_low), xstat = out[:3], out[3:7], out[7:]
+    rx = [ring_x(m, d) for d, m in enumerate(msgx, 1)]
+    out = call(
+        k2c, [(Y_HALO + HALO[d], NZ) for d in (1, 2, 3)] + [(Y_HALO, NZ), (4, 80, NZ)] + chain, (ownx, *rx))
+    msgy, owny, blk, zstat = out[:3], out[3], out[4], out[5:]
+    ry = [ring_y(m, d) for d, m in enumerate(msgy, 1)]
+    out = call(
+        k3, [(GX, R3, NZ)] + chain + chain + [(2,) + FACE, FIELD, FIELD, FACE, FIELD, FIELD, FIELD, FIELD, FIELD,
+                                              (4,) + FACE],
+        (owny, *ry, rx[0], rx[2], blk, zstat[0], zstat[1], v, hzp, dx, fy, fx, bx, hz_low, *xstat,
+         hyp, dz0, hxpp0, dy20, zx, zy), scratch=[(4, 80, NZ)])
+    msg3, sstat, gstat, tr = out[0], out[1:5], out[5:9], out[9]
+    ex1, hz1, hz1m, inj, hxpp, hzpp, dz, dy2, own = out[10:]
     m3 = exchange(msg3, "gx")
     msg4, dz2, hypp, own2 = call(
         k4, [(GY, R4, NZ), FIELD, FIELD, (2,) + FACE],
-        (m3, own, v, dz, fx, fy, by, hyp, hxpp, inj, *xstat, *ystat))
+        (m3, own, v, dz, fx, fy, by, hyp, hxpp, inj, *xstat, *zstat, *sstat, *gstat, tr))
     m4 = exchange(msg4, "gy")
     e_out, h_out = call(
         k4b, [(3,) + FIELD, (3,) + FIELD], (m3, own, v, w, fx, ex1, hz1, hz1m, hypp, hzpp, dy2, *xstat),
         scratch=[FIELD] * 5 + [dma((4,))], hbm_out=(0, 1))
     e_out, h_out = call(
-        k5, [(3,) + FIELD, (3,) + FIELD], (m4, own2, dz2, fy, hxpp, *ystat, e_out, h_out),
-        scratch=[FIELD, FIELD, dma((2,))], hbm_in=(9, 10), hbm_out=(0, 1), alias={9: 0, 10: 1})
+        k5, [(3,) + FIELD, (3,) + FIELD], (m4, own2, dz2, fy, hxpp, sstat[0], sstat[1], *gstat, e_out, h_out),
+        scratch=[FIELD, FIELD, dma((2,))], hbm_in=(11, 12), hbm_out=(0, 1), alias={11: 0, 12: 1})
     return e_out.reshape(3, CX, CY, NZ), h_out.reshape(3, CX, CY, NZ)
 
 

time: 66.5 us -> 61.6 us (0.926)
  blocking collectives: 33.9 us -> 9.23 us
  starting transfers between devices: 8.92 us -> 20.6 us
  waiting for transfers between devices: 9.73 us -> 18.6 us
    all_to_all x2 -> x1, blocking collectives: 33.9 us -> 9.23 us  [exchange(): lax.all_to_all(message, axis, split_axis=0, concat_axis=0, tiled=True)]
    ppermute x0 -> x6, starting transfers between devices: none -> 10.4 us  [the longest x3 5.29 us: ring_y(): return lax.ppermute(message, 'gy', pairs)]
    ppermute x0 -> x6, waiting for transfers between devices: none -> 8.15 us  [the longest x3 4.09 us: ring_x(): return lax.ppermute(message, 'gy', pairs)]
    all_to_all x2, starting transfers between devices: 8.92 us -> 10.2 us  [exchange(): lax.all_to_all(message, axis, split_axis=0, concat_axis=0, tiled=True)]
    all_to_all x2, waiting for transfers between devices: 9.73 us -> 10.4 us  [exchange(): lax.all_to_all(message, axis, split_axis=0, concat_axis=0, tiled=True)]
    pallas_call x7 -> x8, Pallas kernels: 12.2 us -> 12.2 us  [call(): pl.pallas_call(kernel, out_shape=[jax.ShapeDtypeStruct(s, F32) for s in s...]
  transfers between devices with their start and end apart: 2 -> 8, of which waited for: 2 -> 4; matrix products, arithmetic and copies ran while one was open for 0% -> 0% of each run, Pallas kernels for 10% -> 11%
where the time goes in v2:
time: 61.6 us; the launch traced here: 61.3 us
  starting transfers between devices  20.6 us (33%)
  waiting for transfers between devices  18.6 us (30%)
  Pallas kernels  12.2 us (20%)
  blocking collectives  9.23 us (15%)
  between operations  0.71 us (1%)
    pallas_call x8, Pallas kernels, call(): pl.pallas_call(kernel, out_shape=[jax.ShapeDtypeStruct(s, F32) for s in s...  12.2 us
    all_to_all x2, waiting for transfers between devices, exchange(): lax.all_to_all(message, axis, split_axis=0, concat_axis=0, tiled=True)  10.4 us
    all_to_all x2, starting transfers between devices, exchange(): lax.all_to_all(message, axis, split_axis=0, concat_axis=0, tiled=True)  10.2 us
    all_to_all x1, blocking collectives, exchange(): lax.all_to_all(message, axis, split_axis=0, concat_axis=0, tiled=True)  9.23 us
    ppermute x3, starting transfers between devices, ring_y(): return lax.ppermute(message, 'gy', pairs)  5.29 us
    ppermute x3, starting transfers between devices, ring_x(): return lax.ppermute(message, 'gy', pairs)  5.12 us
    ppermute x3, waiting for transfers between devices, ring_x(): return lax.ppermute(message, 'gy', pairs)  4.09 us
    ppermute x3, waiting for transfers between devices, ring_y(): return lax.ppermute(message, 'gy', pairs)  4.05 us
  transfers between devices with their start and end apart: 8, of which 4 were waited for; matrix products, arithmetic and copies ran while one was open for 0% of the time, Pallas kernels for 11%

profile of v2, /device:TPU:0, one launch (start us, length us, event | category | flops | bytes accessed | tf_op | source)
XLA Modules:
  0.0 61.3 jit_solution(11202106393225047583)
XLA Ops:
  0.6 2.5 %k1.1 = (f32[8,104,128]{2,1,0:T(8,128)}, f32[256,128]{1,0:T(8,128)S(1)}, f32[256,128]{1,0:T(8,128)S(1)}, f32[16,16,128]{2,1,0:T(8,128)S(1)}, f32[16,16,128]{2,1,0:T(8,128)S(1)}) custom-call(f32[3,256,128]{2,1,0:T(8,128)} %bitcast.10, f32[3,256,128]{2,1,0:T(8,128)} %bitcast.13, s32[256,128]{1,0:T(8,128)} %bitcast.19, f32[8]{0:T(128)} %perm_h.1, f32[8]{0:T(128)} %cond_h.1, ...), custom_call_target="tpu_custom_call" | custom-call | tf_op jit(solution)/shard_map/k1/pallas_call | solution.py:550
  3.2 0.0 copy-start
  3.2 0.0 copy-start.1
  3.2 5.5 %all-to-all-start = ((f32[8,104,128]{2,1,0:T(8,128)}), f32[8,104,128]{2,1,0:T(8,128)S(1)}, u32[]{:S(2)}, u32[]{:S(2)}) async-start(f32[8,104,128]{2,1,0:T(8,128)} %get-tuple-element.63), calls=%async_computation | async-start | bytes 851968 | tf_op jit(solution)/shard_map/all_to_all | solution.py:573
  8.7 0.0 copy-done
  8.7 0.0 copy-done.1
  8.7 3.3 %k1b.1 = (f32[16,16,128]{2,1,0:T(8,128)S(1)}, f32[16,16,128]{2,1,0:T(8,128)S(1)}, f32[3,16,128]{2,1,0:T(8,128)S(1)}, f32[256,128]{1,0:T(8,128)S(1)}, f32[256,128...) custom-call(f32[3,256,128]{2,1,0:T(8,128)S(1)} %bitcast.11, ...), custom_call_target="tpu_custom_call" | custom-call | tf_op jit(solution)/shard_map/k1b/pallas_call | solution.py:550
  12.0 6.0 %all-to-all-done = f32[8,104,128]{2,1,0:T(8,128)S(1)} async-done(((f32[8,104,128]{2,1,0:T(8,128)}), f32[8,104,128]{2,1,0:T(8,128)S(1)}, u32[]{:S(2)}, u32[]{:S(2)}) %all-to-all-start) | async-done | bytes 426016 | tf_op jit(solution)/shard_map/all_to_all | solution.py:573
  18.0 0.2 k2.1
  18.3 1.6 %collective-permute-start = (f32[184,128]{1,0:T(8,128)S(1)}, f32[184,128]{1,0:T(8,128)S(1)}, u32[]{:S(2)}, u32[]{:S(2)}) collective-permute-start(f32[184,128]{1,0:T(8,128)S(1)} %get-tuple-element.70), channel_id=1, source_target_pairs={{0,1},{1,2},{2,3},{3,0},{4,5},{5,6},{6,7},{7,4},{8,9},{9,10},{10,1... | collective-permute-start | bytes 282632 | tf_op jit(solution)/shard_map/ppermute | solution.py:564
  19.8 1.7 %collective-permute-start.2 = (f32[168,128]{1,0:T(8,128)S(1)}, f32[168,128]{1,0:T(8,128)S(1)}, u32[]{:S(2)}, u32[]{:S(2)}) collective-permute-start(f32[168,128]{1,0:T(8,128)S(1)} %get-tuple-element.72), channel_id=1, source_target_pairs={{0,3},{1,0},{2,1},{3,2},{4,7},{5,4},{6,5},{7,6},{8,11},{9,8},{10,9... | collective-permute-start | bytes 258056 | tf_op jit(solution)/shard_map/ppermute | solution.py:564
  21.6 1.8 %collective-permute-start.1 = (f32[152,128]{1,0:T(8,128)S(1)}, f32[152,128]{1,0:T(8,128)S(1)}, u32[]{:S(2)}, u32[]{:S(2)}) collective-permute-start(f32[152,128]{1,0:T(8,128)S(1)} %get-tuple-element.71), channel_id=1, source_target_pairs={{0,2},{1,3},{2,0},{3,1},{4,6},{5,7},{6,4},{7,5},{8,10},{9,11},{10,... | collective-permute-start | bytes 233480 | tf_op jit(solution)/shard_map/ppermute | solution.py:564
  23.4 4.1 %collective-permute-done.1.r2 = f32[152,128]{1,0:T(8,128)S(1)} collective-permute-done((f32[152,128]{1,0:T(8,128)S(1)}, f32[152,128]{1,0:T(8,128)S(1)}, u32[]{:S(2)}, u32[]{:S(2)}) %collective-permute-start.1) | collective-permute-done | bytes 77856 | tf_op jit(solution)/shard_map/ppermute | solution.py:564
  27.5 0.0 collective-permute-done.2.r3
  27.5 0.0 collective-permute-done.r1
  27.5 0.1 k2c.1
  27.6 1.6 %collective-permute-start.3 = (f32[208,128]{1,0:T(8,128)S(1)}, f32[208,128]{1,0:T(8,128)S(1)}, u32[]{:S(2)}, u32[]{:S(2)}) collective-permute-start(f32[208,128]{1,0:T(8,128)S(1)} %get-tuple-element.74), channel_id=1, source_target_pairs={{0,4},{1,5},{2,6},{3,7},{4,8},{5,9},{6,10},{7,11},{8,12},{9,13},{1... | collective-permute-start | bytes 319496 | tf_op jit(solution)/shard_map/ppermute | solution.py:569
  29.2 1.7 %collective-permute-start.5 = (f32[192,128]{1,0:T(8,128)S(1)}, f32[192,128]{1,0:T(8,128)S(1)}, u32[]{:S(2)}, u32[]{:S(2)}) collective-permute-start(f32[192,128]{1,0:T(8,128)S(1)} %get-tuple-element.76), channel_id=1, source_target_pairs={{0,12},{1,13},{2,14},{3,15},{4,0},{5,1},{6,2},{7,3},{8,4},{9,5},{1... | collective-permute-start | bytes 294920 | tf_op jit(solution)/shard_map/ppermute | solution.py:569
  30.9 2.0 %collective-permute-start.4 = (f32[176,128]{1,0:T(8,128)S(1)}, f32[176,128]{1,0:T(8,128)S(1)}, u32[]{:S(2)}, u32[]{:S(2)}) collective-permute-start(f32[176,128]{1,0:T(8,128)S(1)} %get-tuple-element.75), channel_id=1, source_target_pairs={{0,8},{1,9},{2,10},{3,11},{4,12},{5,13},{6,14},{7,15},{8,0},{9,1},... | collective-permute-start | bytes 270344 | tf_op jit(solution)/shard_map/ppermute | solution.py:569
  32.9 4.0 %collective-permute-done.4.s2 = f32[176,128]{1,0:T(8,128)S(1)} collective-permute-done((f32[176,128]{1,0:T(8,128)S(1)}, f32[176,128]{1,0:T(8,128)S(1)}, u32[]{:S(2)}, u32[]{:S(2)}) %collective-permute-start.4) | collective-permute-done | bytes 90144 | tf_op jit(solution)/shard_map/ppermute | solution.py:569
  36.9 0.0 collective-permute-done.5.s3
  36.9 0.0 collective-permute-done.3.s1
  36.9 0.9 %k3.1 = (f32[8,48,128]{2,1,0:T(8,128)S(1)}, f32[4,16,128]{2,1,0:T(8,128)S(1)}, f32[4,16,128]{2,1,0:T(8,128)S(1)}, f32[5,16,128]{2,1,0:T(8,128)S(1)}, f32[5,16,12...) custom-call(f32[176,128]{1,0:T(8,128)S(1)} %get-tuple-element.73.own, ...), custom_call_target="tpu_custom_call" | custom-call | tf_op jit(solution)/shard_map/k3/pallas_call | solution.py:550
  37.8 9.2 %all_to_all.15.m3 = f32[8,48,128]{2,1,0:T(8,128)S(1)} all-to-all(f32[8,48,128]{2,1,0:T(8,128)S(1)} %get-tuple-element.95), channel_id=1, replica_groups=mesh['gx'=8,'gy'=16] {'gx'}, dimensions={0} | all-to-all | bytes 393216 | tf_op jit(solution)/shard_map/all_to_all | solution.py:573
  47.0 0.9 %k4.1 = (f32[16,16,128]{2,1,0:T(8,128)}, f32[256,128]{1,0:T(8,128)S(1)}, f32[256,128]{1,0:T(8,128)S(1)}, f32[2,16,128]{2,1,0:T(8,128)S(1)}) custom-call(f32[8,48,128]{2,1,0:T(8,128)S(1)} %all_to_all.15.m3, f32[4,16,128]{2,1,0:T(8,128)S(1)} %get-tuple-element.96.own, f32[256,128]{1,0:T(8,128)S(1)} %get-tuple-element.64.v, ...), custom_call_target="tpu_custom_call" | custom-call | tf_op jit(solution)/shard_map/k4/pallas_call | solution.py:550
  47.9 4.6 %all-to-all-start.2 = ((f32[16,16,128]{2,1,0:T(8,128)}), f32[16,16,128]{2,1,0:T(8,128)S(1)}, u32[]{:S(2)}, u32[]{:S(2)}) async-start(f32[16,16,128]{2,1,0:T(8,128)} %get-tuple-element.111), calls=%async_computation.2 | async-start | bytes 262144 | tf_op jit(solution)/shard_map/all_to_all | solution.py:573
  52.5 3.5 %k4b.1 = (f32[3,256,128]{2,1,0:T(8,128)}, f32[3,256,128]{2,1,0:T(8,128)}) custom-call(f32[8,48,128]{2,1,0:T(8,128)S(1)} %all_to_all.15.m3, f32[4,16,128]{2,1,0:T(8,128)S(1)} %get-tuple-element.96.own, f32[256,128]{1,0:T(8,128)S(1)} %get-tuple-element.64.v, f32[256,128]{1,0:T(8,128)S(1)} %get-tuple-element.65.w, f32[16,16,128]{2,1,0:T(8,128)S(1)} %get-tuple-element.82.fx, ...), custom_call_target="tpu_custom_call" | custom-call | tf_op jit(solution)/shard_map/k4b/pallas_call | solution.py:550
  56.0 4.4 %all-to-all-done.2.m4 = f32[16,16,128]{2,1,0:T(8,128)S(1)} async-done(((f32[16,16,128]{2,1,0:T(8,128)}), f32[16,16,128]{2,1,0:T(8,128)S(1)}, u32[]{:S(2)}, u32[]{:S(2)}) %all-to-all-start.2) | async-done | bytes 131104 | tf_op jit(solution)/shard_map/all_to_all | solution.py:573
  60.5 0.8 %k5.1 = (f32[3,256,128]{2,1,0:T(8,128)}, f32[3,256,128]{2,1,0:T(8,128)}) custom-call(f32[16,16,128]{2,1,0:T(8,128)S(1)} %all-to-all-done.2.m4, f32[2,16,128]{2,1,0:T(8,128)S(1)} %get-tuple-element.112.own, f32[256,128]{1,0:T(8,128)S(1)} %get-tuple-element.113.dz2, ...), custom_call_target="tpu_custom_call", output_to_operand_aliasing={{0}: (11, {}), {1}: (12, {})} | custom-call | tf_op jit(solution)/shard_map/k5/pallas_call | solution.py:550
Async XLA Ops:
  3.2 5.6 %copy-start = (f32[3,16,16,128]{3,2,1,0:T(8,128)S(1)}, f32[3,16,16,128]{3,2,1,0:T(8,128)}, u32[]{:S(2)}) copy-start(f32[3,16,16,128]{3,2,1,0:T(8,128)} %param.9) | copy-start | bytes 1179652
  3.2 5.6 %copy-start.1 = (f32[3,16,16,128]{3,2,1,0:T(8,128)S(1)}, f32[3,16,16,128]{3,2,1,0:T(8,128)}, u32[]{:S(2)}) copy-start(f32[3,16,16,128]{3,2,1,0:T(8,128)} %param.10) | copy-start | bytes 1179652
  3.2 14.8 %all-to-all-start = ((f32[8,104,128]{2,1,0:T(8,128)}), f32[8,104,128]{2,1,0:T(8,128)S(1)}, u32[]{:S(2)}, u32[]{:S(2)}) async-start(f32[8,104,128]{2,1,0:T(8,128)} %get-tuple-element.63), calls=%async_computation | async-start | bytes 851968 | tf_op jit(solution)/shard_map/all_to_all | solution.py:573
  18.3 9.2 %collective-permute-start = (f32[184,128]{1,0:T(8,128)S(1)}, f32[184,128]{1,0:T(8,128)S(1)}, u32[]{:S(2)}, u32[]{:S(2)}) collective-permute-start(f32[184,128]{1,0:T(8,128)S(1)} %get-tuple-element.70), channel_id=1, source_target_pairs={{0,1},{1,2},{2,3},{3,0},{4,5},{5,6},{6,7},{7,4},{8,9},{9,10},{10,1... | collective-permute-start | bytes 282632 | tf_op jit(solution)/shard_map/ppermute | solution.py:564
  19.8 7.7 %collective-permute-start.2 = (f32[168,128]{1,0:T(8,128)S(1)}, f32[168,128]{1,0:T(8,128)S(1)}, u32[]{:S(2)}, u32[]{:S(2)}) collective-permute-start(f32[168,128]{1,0:T(8,128)S(1)} %get-tuple-element.72), channel_id=1, source_target_pairs={{0,3},{1,0},{2,1},{3,2},{4,7},{5,4},{6,5},{7,6},{8,11},{9,8},{10,9... | collective-permute-start | bytes 258056 | tf_op jit(solution)/shard_map/ppermute | solution.py:564
  21.6 5.9 %collective-permute-start.1 = (f32[152,128]{1,0:T(8,128)S(1)}, f32[152,128]{1,0:T(8,128)S(1)}, u32[]{:S(2)}, u32[]{:S(2)}) collective-permute-start(f32[152,128]{1,0:T(8,128)S(1)} %get-tuple-element.71), channel_id=1, source_target_pairs={{0,2},{1,3},{2,0},{3,1},{4,6},{5,7},{6,4},{7,5},{8,10},{9,11},{10,... | collective-permute-start | bytes 233480 | tf_op jit(solution)/shard_map/ppermute | solution.py:564
  27.6 9.3 %collective-permute-start.3 = (f32[208,128]{1,0:T(8,128)S(1)}, f32[208,128]{1,0:T(8,128)S(1)}, u32[]{:S(2)}, u32[]{:S(2)}) collective-permute-start(f32[208,128]{1,0:T(8,128)S(1)} %get-tuple-element.74), channel_id=1, source_target_pairs={{0,4},{1,5},{2,6},{3,7},{4,8},{5,9},{6,10},{7,11},{8,12},{9,13},{1... | collective-permute-start | bytes 319496 | tf_op jit(solution)/shard_map/ppermute | solution.py:569
  29.2 7.7 %collective-permute-start.5 = (f32[192,128]{1,0:T(8,128)S(1)}, f32[192,128]{1,0:T(8,128)S(1)}, u32[]{:S(2)}, u32[]{:S(2)}) collective-permute-start(f32[192,128]{1,0:T(8,128)S(1)} %get-tuple-element.76), channel_id=1, source_target_pairs={{0,12},{1,13},{2,14},{3,15},{4,0},{5,1},{6,2},{7,3},{8,4},{9,5},{1... | collective-permute-start | bytes 294920 | tf_op jit(solution)/shard_map/ppermute | solution.py:569
  30.9 6.0 %collective-permute-start.4 = (f32[176,128]{1,0:T(8,128)S(1)}, f32[176,128]{1,0:T(8,128)S(1)}, u32[]{:S(2)}, u32[]{:S(2)}) collective-permute-start(f32[176,128]{1,0:T(8,128)S(1)} %get-tuple-element.75), channel_id=1, source_target_pairs={{0,8},{1,9},{2,10},{3,11},{4,12},{5,13},{6,14},{7,15},{8,0},{9,1},... | collective-permute-start | bytes 270344 | tf_op jit(solution)/shard_map/ppermute | solution.py:569
  47.9 12.6 %all-to-all-start.2 = ((f32[16,16,128]{2,1,0:T(8,128)}), f32[16,16,128]{2,1,0:T(8,128)S(1)}, u32[]{:S(2)}, u32[]{:S(2)}) async-start(f32[16,16,128]{2,1,0:T(8,128)} %get-tuple-element.111), calls=%async_computation.2 | async-start | bytes 262144 | tf_op jit(solution)/shard_map/all_to_all | solution.py:573

commit v3 on v2

--- a/solution.py
+++ b/solution.py
@@ -16,11 +16,12 @@
 HS = 16.0
 INV = 1.0 / 256.0
 
-R1_VAL, R1_HALO, R1_G11, R1_G1N, R1_GNN, R1_CODE, R1 = 0, 32, 48, 64, 80, 96, 104
+C_CODE, C_HALO, C_COEF, C_ALL = 256, 264, 296, 344
+Z_CODE, Z_COEF, Z_HALO = 64, 72, 120
 X_CODE, X_BLOCK, X_HALO = 64, 72, 152
 Y_CODE, Y_BLOCK, Y_HALO = 64, 96, 176
 HALO = (0, 32, 0, 16)
-R3_Z, R3_Y, R3_T, R3 = 0, 16, 32, 48
+Z_ROWS = (0, 16, 0, 16)
 R4 = 16
 
 
@@ -179,20 +180,10 @@
     return q2 + h_ref[k] * be_ref[k] * q1, q1 + hr_ref[k] * de_ref[k + 1] * q2
 
 
-def faces(ref, k):
-    return [ref[k, pl.ds(16 * f, 16), :] for f in range(5)]
-
-
 def place(buf, own_at, own, others):
     buf[own_at] = own
     for d, value in enumerate(others, 1):
         buf[(own_at + 4 - d) & 3] = value
-
-
-def to_messages(me, p1, p2, h_ref, hr_ref, be_ref, de_ref):
-    m = p2 + h_ref[me] * be_ref[me] * p1
-    n = p1 + hr_ref[me] * de_ref[me + 1] * p2
-    return m, n
 
 
 def split_dot(sel, values):
@@ -220,7 +211,6 @@
         copy.start()
     for copy in copies[:3]:
         copy.wait()
-    me = lax.axis_index("gx")
     ws = [(perm[k] + 8.0 * cond[k]) * (1.0 / 4096.0) for k in range(8)]
     vs = [(perm[k] - 8.0 * cond[k]) * (1.0 / 4096.0) for k in range(8)]
 
@@ -258,13 +248,32 @@
     code_at = jnp.where(iota((8, 128), 0) == dest_x, (tgt[...] + 1).astype(F32), 0.0).astype(BF16)
     lane_hot = (iota((128, 128), 0) == lane_slot).astype(BF16)
     code = lax.dot_general(code_at, lane_hot, nt, preferred_element_type=F32)
-    for d in range(GX):
-        msg[d, 0:32, :] = vals[d * 32:(d + 1) * 32]
-        msg[d, R1_HALO:R1_HALO + 16, :] = jnp.where(d > me, hz_last[...], ey_first[...])
-        msg[d, R1_G11:R1_G11 + 16, :] = bwd[0]
-        msg[d, R1_G1N:R1_G1N + 16, :] = link
-        msg[d, R1_GNN:R1_GNN + 16, :] = fwd[CX - 1]
-        msg[d, R1_CODE:R1_CODE + 8, :] = jnp.broadcast_to(code[d:d + 1], (8, NZ))
+    msg[0:CELLS, :] = vals
+    msg[C_CODE:C_CODE + 8, :] = code
+    msg[C_HALO:C_HALO + 16, :] = hz_last[...]
+    msg[C_HALO + 16:C_HALO + 32, :] = ey_first[...]
+    for f, face in enumerate((bwd[0], link, fwd[CX - 1])):
+        msg[C_COEF + 16 * f:C_COEF + 16 * f + 16, :] = face
+
+
+def k1c(own, rc, mz1, mz2, mz3, own_o, blk_o, h_o, hr_o, be_o, de_o):
+    gx = lax.axis_index("gx")
+    c = gx & 1
+    z = gx >> 1
+    blk_o[c] = own[C_COEF:C_ALL, :]
+    blk_o[1 - c] = rc[C_COEF:C_ALL, :]
+    static_fold(2, lambda k: blk_o[k, 0:16, :], lambda k: blk_o[k, 16:32, :], lambda k: blk_o[k, 32:48, :],
+                h_o, hr_o, be_o, de_o)
+    for d, ref in enumerate((own_o, mz1, mz2, mz3)):
+        to = ((z + d) & 3) * 2 + c
+        for r, src in enumerate((own, rc)):
+            ref[32 * r:32 * r + 32, :] = src[pl.ds(pl.multiple_of(to * 32, 32), 32), :]
+            ref[Z_CODE + r:Z_CODE + r + 1, :] = src[pl.ds(C_CODE + to, 1), :]
+        ref[Z_CODE + 2:Z_CODE + 8, :] = jnp.zeros((6, NZ), F32)
+        for f, face in enumerate((de_o[0], h_o[0] * h_o[1], be_o[2])):
+            ref[Z_COEF + 16 * f:Z_COEF + 16 * f + 16, :] = face
+    mz1[Z_HALO:Z_HALO + 16, :] = jnp.where(c == 1, own[C_HALO:C_HALO + 16, :], rc[C_HALO:C_HALO + 16, :])
+    mz3[Z_HALO:Z_HALO + 16, :] = jnp.where(c == 0, own[C_HALO + 16:C_HALO + 32, :], rc[C_HALO + 16:C_HALO + 32, :])
 
 
 def k1b(e, h, w, v, fy_o, by_o, g_o, hyp_o, dz_o, hxpp_o, dy2_o, zx_o, zy_o, hxp_s, ey1_s, dy1_s):
@@ -309,13 +318,16 @@
         dy2_o[rows(x), :] = v[rows(x), :] * ey1 + INV * (hx1 - z_down(hx1))
 
 
-def k2(m1, e, h, v, fy, by, g, mx1, mx2, mx3, own_o, hzp_o, dx_o, halo_o, h_o, hr_o, be_o, de_o, vals_s):
+def k2(rc, ownz, z1, z2, z3, blk, e, h, v, fy, by, g, mx1, mx2, mx3, own_o, hzp_o, dx_o, halo_o,
+       h_o, hr_o, be_o, de_o, hg_o, hrg_o, beg_o, deg_o, vals_s, src_s, code_s, grp):
     gx = lax.axis_index("gx")
     me = lax.axis_index("gy")
-    lo = jnp.maximum(gx - 1, 0) * R1 + R1_HALO
-    hi = jnp.minimum(gx + 1, GX - 1) * R1 + R1_HALO
-    hz_low = jnp.where(gx > 0, m1[pl.ds(lo, 16), :], 0.0)
-    ey_high = jnp.where(gx < GX - 1, m1[pl.ds(hi, 16), :], 0.0)
+    c = gx & 1
+    z = gx >> 1
+    hz_low = jnp.where(c == 1, rc[C_HALO:C_HALO + 16, :], z1[Z_HALO:Z_HALO + 16, :])
+    ey_high = jnp.where(c == 0, rc[C_HALO + 16:C_HALO + 32, :], z3[Z_HALO:Z_HALO + 16, :])
+    hz_low = jnp.where(gx > 0, hz_low, 0.0)
+    ey_high = jnp.where(gx < GX - 1, ey_high, 0.0)
     halo_o[...] = hz_low
     for x in range(CX):
         ey = e[1, rows(x), :]
@@ -330,12 +342,15 @@
     p1, p2 = ends([dx_o[strided(y), :] for y in range(CY)], fwd, bwd)
     t = -INV * hzp_o[strided(CY - 1), :]
     p2 = p2 + t
+    for k, ref in enumerate((ownz, z1, z2, z3)):
+        src_s[64 * k:64 * k + 64, :] = ref[0:64, :]
+        code_s[2 * k:2 * k + 2, :] = ref[Z_CODE:Z_CODE + 2, :]
     for to in range(4):
         for r in range(2):
             for y in range(4):
                 at = (r * 4 + y) * 8
-                vals_s[to, at:at + 8, :] = m1[pl.ds(r * GY + 4 * y + to, 8, stride=R1), :]
-    code = m1[pl.ds(R1_CODE, 8, stride=R1), :]
+                vals_s[to, at:at + 8, :] = src_s[pl.ds(r * GY + 4 * y + to, 8, stride=32), :]
+    code = code_s[...]
     for d, ref in enumerate((own_o, mx1, mx2, mx3)):
         ref[0:64, :] = vals_s[(me + d) & 3]
         ref[X_CODE:X_CODE + 8, :] = code
@@ -344,12 +359,11 @@
     mx1[X_HALO:X_HALO + 16, :] = h[0, strided(CY - 1), :]
     mx1[X_HALO + 16:X_HALO + 32, :] = t
     mx3[X_HALO:X_HALO + 16, :] = e[2, strided(0), :]
-    static_fold(
-        GX,
-        lambda j: m1[pl.ds(j * R1 + R1_G11, 16), :],
-        lambda j: m1[pl.ds(j * R1 + R1_G1N, 16), :],
-        lambda j: m1[pl.ds(j * R1 + R1_GNN, 16), :],
-        h_o, hr_o, be_o, de_o)
+    place(grp, z, ownz[Z_COEF:Z_HALO, :], [r[Z_COEF:Z_HALO, :] for r in (z1, z2, z3)])
+    static_fold(4, lambda k: grp[k, 0:16, :], lambda k: grp[k, 16:32, :], lambda k: grp[k, 32:48, :],
+                h_o, hr_o, be_o, de_o)
+    static_fold(2, lambda k: blk[k, 0:16, :], lambda k: blk[k, 16:32, :], lambda k: blk[k, 32:48, :],
+                hg_o, hrg_o, beg_o, deg_o, be_o[z], de_o[z + 1])
 
 
 def k2c(own, r1, r2, r3, my1, my2, my3, own_o, blk_o, h_o, hr_o, be_o, de_o):
@@ -378,11 +392,10 @@
     my3[Y_HALO:Y_HALO + 16, :] = r3[X_HALO:X_HALO + 16, :]
 
 
-def k3(own, s1, s2, s3, r1, r3, blk, h0, hr0, v, hzp, dx, fy, fx, bx, hz_low, hx_c, hrx_c, bex, dex,
+def k3(own, s1, s2, s3, r1, r3, blk, h0, hr0, v, hzp, dx, fy, fx, bx, hz_low,
        hyp, dz0, hxpp0, dy20, zx, zy,
        msg, hs_c, hrs_c, bes, des, hg_c, hrg_c, beg, deg, tr_o, ex1_o, hz1_o, hz1m_o, inj_o, hxpp_o, hzpp_o,
-       dz_o, dy2_o, own_o, grp):
-    gx = lax.axis_index("gx")
+       dz_o, dy2_o, grp):
     gy = lax.axis_index("gy")
     at = gy & 3
     me = gy >> 2
@@ -458,25 +471,52 @@
     bwd = [bx[x] for x in range(CX)]
     tz = -INV * hyp[rows(CX - 1), :]
     p1, p2 = ends([dz_o[rows(x), :] for x in range(CX)], fwd, bwd)
-    mz, nz = to_messages(gx, p1, p2 + tz, hx_c, hrx_c, bex, dex)
     ty = INV * hzpp_o[rows(CX - 1), :]
-    p1, p2 = ends([dy2_o[rows(x), :] for x in range(CX)], fwd, bwd)
-    my, ny = to_messages(gx, p1, p2 + ty, hx_c, hrx_c, bex, dex)
-    own_o[0], own_o[1], own_o[2], own_o[3] = mz, nz, my, ny
-    for d in range(GX):
-        msg[d, 0:16, :] = jnp.where(d > gx, mz, nz)
-        msg[d, 16:32, :] = jnp.where(d > gx, my, ny)
-        msg[d, 32:48, :] = tz
-
-
-def k4(m3, own, v, dz, fx, fy, by, hyp, hxpp, inj, hx_c, hrx_c, bex, dex,
-       h0, hr0, be0, de0, hs_c, hrs_c, bes, des, hg_c, hrg_c, beg, deg, tr, msg, dz2_o, hypp_o, own_o):
+    q1, q2 = ends([dy2_o[rows(x), :] for x in range(CX)], fwd, bwd)
+    for f, face in enumerate((p1, p2 + tz, q1, q2 + ty, tz)):
+        msg[16 * f:16 * f + 16, :] = face
+
+
+def k3b(own, rc, h0, hr0, be0, de0, hs_c, hrs_c, bes, des, mz1, mz2, mz3):
+    gx = lax.axis_index("gx")
+    c = gx & 1
+    z = gx >> 1
+    terms = []
+    for f in range(2):
+        blocks = []
+        for k in range(2):
+            q1 = jnp.where(c == k, own[32 * f:32 * f + 16, :], rc[32 * f:32 * f + 16, :])
+            q2 = jnp.where(c == k, own[32 * f + 16:32 * f + 32, :], rc[32 * f + 16:32 * f + 32, :])
+            blocks.append(pair_terms(k, q1, q2, h0, hr0, be0, de0))
+        last = blocks[1][0] + h0[1] * blocks[0][0]
+        first = blocks[0][1] + hr0[0] * blocks[1][1]
+        terms.append(pair_terms(z, first, last, hs_c, hrs_c, bes, des))
+    for d, ref in enumerate((mz1, mz2, mz3), 1):
+        up = ((z + d) & 3) > z
+        for f in range(2):
+            ref[16 * f:16 * f + 16, :] = jnp.where(up, terms[f][0], terms[f][1])
+    mz1[32:48, :] = jnp.where(c == 1, own[64:80, :], rc[64:80, :])
+
+
+def x_interface(f, own, rc, zs, hs_c, hrs_c, hg_c, hrg_c, beg, deg, buf):
+    gx = lax.axis_index("gx")
+    c = gx & 1
+    z = gx >> 1
+    place(buf, z, zs[0][16 * f:16 * f + 16, :], [r[16 * f:16 * f + 16, :] for r in zs])
+    al, ga = incoming(4, z, lambda k: buf[k], hs_c, hrs_c)
+    own_m, own_n = pair_terms(c, own[32 * f:32 * f + 16, :], own[32 * f + 16:32 * f + 32, :], hg_c, hrg_c, beg, deg)
+    other = pair_terms(1 - c, rc[32 * f:32 * f + 16, :], rc[32 * f + 16:32 * f + 32, :], hg_c, hrg_c, beg, deg)
+    return interface(2, c, own_m, own_n, lambda k: other[k], hg_c, hrg_c, beg, deg, al, ga)
+
+
+def k4(own, rc, z1, z2, z3, hxs, hrxs, hxg, hrxg, bexg, dexg, v, dz, fx, fy, by, hyp, hxpp, inj,
+       h0, hr0, be0, de0, hs_c, hrs_c, bes, des, hg_c, hrg_c, beg, deg, tr, msg, dz2_o, hypp_o, own_o, buf):
     gx = lax.axis_index("gx")
     at = lax.axis_index("gy") & 3
     me = lax.axis_index("gy") >> 2
-    left, right = interface(GX, gx, own[0], own[1], lambda j: m3[j, 0:16, :], hx_c, hrx_c, bex, dex)
+    left, right = x_interface(0, own, rc, (z1, z2, z3), hxs, hrxs, hxg, hrxg, bexg, dexg, buf)
     us = block_solve([dz[rows(x), :] for x in range(CX)], [fx[x] for x in range(CX)], left, right)
-    t = m3[jnp.maximum(gx - 1, 0), 32:48, :]
+    t = jnp.where((gx & 1) == 1, rc[64:80, :], z1[32:48, :])
     prev = jnp.where(gx > 0, HS * (us[0] - left) - 240.0 * t, 0.0)
     for x in range(CX):
         dez = HS * ((us[x + 1] if x < CX - 1 else right) - us[x])
@@ -498,10 +538,9 @@
         msg[d] = jnp.where(y > me, group_m, jnp.where(y < me, group_n, jnp.where(x > at, m, n)))
 
 
-def k4b(m3, own, v, w, fx, ex1, hz1, hz1m, hypp, hzpp, dy2, hx_c, hrx_c, bex, dex,
-        e_o, h_o, ex2_s, ey2_s, hy2_s, hz2_s, dx2_s, sem):
-    gx = lax.axis_index("gx")
-    left, right = interface(GX, gx, own[2], own[3], lambda j: m3[j, 16:32, :], hx_c, hrx_c, bex, dex)
+def k4b(own, rc, z1, z2, z3, hxs, hrxs, hxg, hrxg, bexg, dexg, v, w, fx, ex1, hz1, hz1m, hypp, hzpp, dy2,
+        e_o, h_o, ex2_s, ey2_s, hy2_s, hz2_s, dx2_s, buf, sem):
+    left, right = x_interface(1, own, rc, (z1, z2, z3), hxs, hrxs, hxg, hrxg, bexg, dexg, buf)
     us = block_solve([dy2[rows(x), :] for x in range(CX)], [fx[x] for x in range(CX)], left, right)
     for x in range(CX):
         ey2_s[rows(x), :] = us[x]
@@ -559,6 +598,15 @@
     )(*args)
 
 
+def pair(message):
+    return lax.ppermute(message, "gx", [(x, x ^ 1) for x in range(GX)])
+
+
+def ring_z(message, d):
+    pairs = [(2 * z + c, 2 * ((z + d) % 4) + c) for z in range(4) for c in range(2)]
+    return lax.ppermute(message, "gx", pairs)
+
+
 def ring_x(message, d):
     pairs = [(4 * y + x, 4 * y + (x + d) % 4) for y in range(4) for x in range(4)]
     return lax.ppermute(message, "gy", pairs)
@@ -589,41 +637,47 @@
         e, h, mat, permittivity, conductivity, electrode_cells.reshape(row),
         electrode_dest.reshape(row), target_cells.reshape(row), electrode_gain.reshape(row))]
     msg1, w, v, fx, bx = call(
-        k1, [(GX, R1, NZ), FIELD, FIELD, LINE, LINE],
+        k1, [(C_ALL, NZ), FIELD, FIELD, LINE, LINE],
         hbm,
         scratch=[FIELD, FACE, FACE, pltpu.VMEM(FIELD, jnp.int32), pltpu.SMEM((8,), F32), pltpu.SMEM((8,), F32),
                  pltpu.VMEM(row, jnp.int32), pltpu.VMEM(row, jnp.int32), pltpu.VMEM(row, jnp.int32), row, dma((10,))],
         hbm_in=range(9))
-    m1 = exchange(msg1, "gx").reshape(GX * R1, NZ)
+    chain2 = [(2,) + FACE, (2,) + FACE, (3,) + FACE, (3,) + FACE]
+    chain = [(4,) + FACE, (4,) + FACE, (5,) + FACE, (5,) + FACE]
+    rc = pair(msg1)
+    out = call(k1c, [(Z_HALO + Z_ROWS[d], NZ) for d in (1, 2, 3)] + [(Z_HALO, NZ), (2, 48, NZ)] + chain2, (msg1, rc))
+    msgz, ownz, blkx, pstat = out[:3], out[3], out[4], out[5:]
+    msgz, w1 = lax.optimization_barrier((msgz, w))
+    rz = [ring_z(m, d) for d, m in enumerate(msgz, 1)]
     (fy, by, g, hyp, dz0, hxpp0, dy20, zx, zy) = call(
         k1b, [LINE, LINE, (3,) + FACE, FIELD, FIELD, FIELD, FIELD, (15,) + FACE, (15,) + FACE],
-        (e, h, w, v), scratch=[FIELD, FIELD, FIELD])
-    chain = [(4,) + FACE, (4,) + FACE, (5,) + FACE, (5,) + FACE]
+        (e, h, w1, v), scratch=[FIELD, FIELD, FIELD])
     out = call(
         k2, [(X_HALO + HALO[d], NZ) for d in (1, 2, 3)] + [
-            (X_HALO, NZ), FIELD, FIELD, FACE, (GX,) + FACE, (GX,) + FACE, (GX + 1,) + FACE, (GX + 1,) + FACE],
-        (m1, e, h, v, fy, by, g), scratch=[(4, 64, NZ)])
-    msgx, (ownx, hzp, dx, hz_low), xstat = out[:3], out[3:7], out[7:]
+            (X_HALO, NZ), FIELD, FIELD, FACE] + chain + chain2,
+        (rc, ownz, *rz, blkx, e, h, v, fy, by, g), scratch=[(4, 64, NZ), FIELD, (8, NZ), (4, 48, NZ)])
+    msgx, (ownx, hzp, dx, hz_low), xsup, xgrp = out[:3], out[3:7], out[7:11], out[11:]
     rx = [ring_x(m, d) for d, m in enumerate(msgx, 1)]
     out = call(
         k2c, [(Y_HALO + HALO[d], NZ) for d in (1, 2, 3)] + [(Y_HALO, NZ), (4, 80, NZ)] + chain, (ownx, *rx))
     msgy, owny, blk, zstat = out[:3], out[3], out[4], out[5:]
     ry = [ring_y(m, d) for d, m in enumerate(msgy, 1)]
     out = call(
-        k3, [(GX, R3, NZ)] + chain + chain + [(2,) + FACE, FIELD, FIELD, FACE, FIELD, FIELD, FIELD, FIELD, FIELD,
-                                              (4,) + FACE],
-        (owny, *ry, rx[0], rx[2], blk, zstat[0], zstat[1], v, hzp, dx, fy, fx, bx, hz_low, *xstat,
+        k3, [(80, NZ)] + chain + chain + [(2,) + FACE, FIELD, FIELD, FACE, FIELD, FIELD, FIELD, FIELD, FIELD],
+        (owny, *ry, rx[0], rx[2], blk, zstat[0], zstat[1], v, hzp, dx, fy, fx, bx, hz_low,
          hyp, dz0, hxpp0, dy20, zx, zy), scratch=[(4, 80, NZ)])
     msg3, sstat, gstat, tr = out[0], out[1:5], out[5:9], out[9]
-    ex1, hz1, hz1m, inj, hxpp, hzpp, dz, dy2, own = out[10:]
-    m3 = exchange(msg3, "gx")
+    ex1, hz1, hz1m, inj, hxpp, hzpp, dz, dy2 = out[10:]
+    rc3 = pair(msg3)
+    msgz3 = call(k3b, [(48, NZ), (32, NZ), (32, NZ)], (msg3, rc3, *pstat, *xsup))
+    got3 = (msg3, rc3, *[ring_z(m, d) for d, m in enumerate(msgz3, 1)], xsup[0], xsup[1], *xgrp)
     msg4, dz2, hypp, own2 = call(
         k4, [(GY, R4, NZ), FIELD, FIELD, (2,) + FACE],
-        (m3, own, v, dz, fx, fy, by, hyp, hxpp, inj, *xstat, *zstat, *sstat, *gstat, tr))
+        (*got3, v, dz, fx, fy, by, hyp, hxpp, inj, *zstat, *sstat, *gstat, tr), scratch=[(4,) + FACE])
     m4 = exchange(msg4, "gy")
     e_out, h_out = call(
-        k4b, [(3,) + FIELD, (3,) + FIELD], (m3, own, v, w, fx, ex1, hz1, hz1m, hypp, hzpp, dy2, *xstat),
-        scratch=[FIELD] * 5 + [dma((4,))], hbm_out=(0, 1))
+        k4b, [(3,) + FIELD, (3,) + FIELD], (*got3, v, w, fx, ex1, hz1, hz1m, hypp, hzpp, dy2),
+        scratch=[FIELD] * 5 + [(4,) + FACE, dma((4,))], hbm_out=(0, 1))
     e_out, h_out = call(
         k5, [(3,) + FIELD, (3,) + FIELD], (m4, own2, dz2, fy, hxpp, sstat[0], sstat[1], *gstat, e_out, h_out),
         scratch=[FIELD, FIELD, dma((2,))], hbm_in=(11, 12), hbm_out=(0, 1), alias={11: 0, 12: 1})

time: 61.6 us -> 56.9 us (0.924)
  blocking collectives: 9.23 us -> 0 us
  starting transfers between devices: 20.6 us -> 25.7 us
    ppermute x0 -> x8, starting transfers between devices: none -> 10.7 us  [the longest x6 10.5 us: ring_z(): return lax.ppermute(message, 'gx', pairs)]
    all_to_all x1 -> x0, blocking collectives: 9.23 us -> none  [exchange(): lax.all_to_all(message, axis, split_axis=0, concat_axis=0, tiled=True)]
    all_to_all x2 -> x1, waiting for transfers between devices: 10.4 us -> 4.43 us  [exchange(): lax.all_to_all(message, axis, split_axis=0, concat_axis=0, tiled=True)]
    ppermute x0 -> x8, waiting for transfers between devices: none -> 5.96 us  [the longest x6 3.36 us: ring_z(): return lax.ppermute(message, 'gx', pairs)]
    all_to_all x2 -> x1, starting transfers between devices: 10.2 us -> 4.61 us  [exchange(): lax.all_to_all(message, axis, split_axis=0, concat_axis=0, tiled=True)]
    pallas_call x8 -> x10, Pallas kernels: 12.2 us -> 11.7 us  [call(): pl.pallas_call(kernel, out_shape=[jax.ShapeDtypeStruct(s, F32) for s in s...]
  transfers between devices with their start and end apart: 8 -> 15, of which waited for: 4 -> 8; matrix products, arithmetic and copies ran while one was open for 0% -> 0% of each run, Pallas kernels for 11% -> 12%
where the time goes in v3:
time: 56.9 us; the launch traced here: 56.7 us
  starting transfers between devices  25.7 us (45%)
  waiting for transfers between devices  18.5 us (33%)
  Pallas kernels  11.7 us (21%)
  between operations  0.74 us (1%)
    pallas_call x10, Pallas kernels, call(): pl.pallas_call(kernel, out_shape=[jax.ShapeDtypeStruct(s, F32) for s in s...  11.7 us
    ppermute x6, starting transfers between devices, ring_z(): return lax.ppermute(message, 'gx', pairs)  10.5 us
    ppermute x3, starting transfers between devices, ring_y(): return lax.ppermute(message, 'gy', pairs)  5.29 us
    ppermute x3, starting transfers between devices, ring_x(): return lax.ppermute(message, 'gy', pairs)  5.12 us
    all_to_all x1, starting transfers between devices, exchange(): lax.all_to_all(message, axis, split_axis=0, concat_axis=0, tiled=True)  4.61 us
    all_to_all x1, waiting for transfers between devices, exchange(): lax.all_to_all(message, axis, split_axis=0, concat_axis=0, tiled=True)  4.43 us
    ppermute x3, waiting for transfers between devices, ring_x(): return lax.ppermute(message, 'gy', pairs)  4.09 us
    ppermute x3, waiting for transfers between devices, ring_y(): return lax.ppermute(message, 'gy', pairs)  4.05 us
  transfers between devices with their start and end apart: 15, of which 8 were waited for; matrix products, arithmetic and copies ran while one was open for 0% of the time, Pallas kernels for 12%

profile of v3, /device:TPU:0, one launch (start us, length us, event | category | flops | bytes accessed | tf_op | source)
XLA Modules:
  0.0 56.7 jit_solution(2988183370010910640)
XLA Ops:
  0.7 1.8 %k1.1 = (f32[344,128]{1,0:T(8,128)S(1)}, f32[256,128]{1,0:T(8,128)S(1)}, f32[256,128]{1,0:T(8,128)S(1)}, f32[16,16,128]{2,1,0:T(8,128)S(1)}, f32[16,16,128]{2,1,0:T(8,128)S(1)}) custom-call(f32[3,256,128]{2,1,0:T(8,128)} %bitcast.9, f32[3,256,128]{2,1,0:T(8,128)} %bitcast.12, s32[256,128]{1,0:T(8,128)} %bitcast.17, f32[8]{0:T(128)} %perm_h.1, f32[8]{0:T(128)} %cond_h.1, ...), custom_call_target="tpu_custom_call" | custom-call | tf_op jit(solution)/shard_map/k1/pallas_call | solution.py:589
  2.5 0.1 collective-permute-start
  2.6 1.4 %collective-permute-done.rc = f32[344,128]{1,0:T(8,128)S(1)} collective-permute-done((f32[344,128]{1,0:T(8,128)S(1)}, f32[344,128]{1,0:T(8,128)S(1)}, u32[]{:S(2)}, u32[]{:S(2)}) %collective-permute-start) | collective-permute-done | bytes 176160 | tf_op jit(solution)/shard_map/ppermute | solution.py:602
  4.0 2.1 %collective-permute-start.1 = (f32[136,128]{1,0:T(8,128)S(1)}, f32[136,128]{1,0:T(8,128)S(1)}, u32[]{:S(2)}, u32[]{:S(2)}) collective-permute-start(f32[136,128]{1,0:T(8,128)S(1)} %get-tuple-element.88), channel_id=1, source_target_pairs={{0,32},{16,48},{32,64},{48,80},{64,96},{80,112},{96,0},{112,16},{1... | collective-permute-start | bytes 208904 | tf_op jit(solution)/shard_map/ppermute | solution.py:607
  6.1 2.2 %collective-permute-start.3 = (f32[136,128]{1,0:T(8,128)S(1)}, f32[136,128]{1,0:T(8,128)S(1)}, u32[]{:S(2)}, u32[]{:S(2)}) collective-permute-start(f32[136,128]{1,0:T(8,128)S(1)} %get-tuple-element.90), channel_id=1, source_target_pairs={{0,96},{16,112},{32,0},{48,16},{64,32},{80,48},{96,64},{112,80},{1... | collective-permute-start | bytes 208904 | tf_op jit(solution)/shard_map/ppermute | solution.py:607
  8.3 1.8 %collective-permute-start.2 = (f32[120,128]{1,0:T(8,128)S(1)}, f32[120,128]{1,0:T(8,128)S(1)}, u32[]{:S(2)}, u32[]{:S(2)}) collective-permute-start(f32[120,128]{1,0:T(8,128)S(1)} %get-tuple-element.89), channel_id=1, source_target_pairs={{0,64},{16,80},{32,96},{48,112},{64,0},{80,16},{96,32},{112,48},{1... | collective-permute-start | bytes 184328 | tf_op jit(solution)/shard_map/ppermute | solution.py:607
  10.1 3.3 %k1b.1 = (f32[16,16,128]{2,1,0:T(8,128)S(1)}, f32[16,16,128]{2,1,0:T(8,128)S(1)}, f32[3,16,128]{2,1,0:T(8,128)S(1)}, f32[256,128]{1,0:T(8,128)S(1)}, f32[256,128...) custom-call(f32[3,256,128]{2,1,0:T(8,128)S(1)} %bitcast.10, ...), custom_call_target="tpu_custom_call" | custom-call | tf_op jit(solution)/shard_map/k1b/pallas_call | solution.py:589
  13.4 0.6 %collective-permute-done.2.z2 = f32[120,128]{1,0:T(8,128)S(1)} collective-permute-done((f32[120,128]{1,0:T(8,128)S(1)}, f32[120,128]{1,0:T(8,128)S(1)}, u32[]{:S(2)}, u32[]{:S(2)}) %collective-permute-start.2) | collective-permute-done | bytes 61472 | tf_op jit(solution)/shard_map/ppermute | solution.py:607
  14.0 0.0 collective-permute-done.3.z3
  14.0 0.3 k2.1
  14.3 1.6 %collective-permute-start.4 = (f32[184,128]{1,0:T(8,128)S(1)}, f32[184,128]{1,0:T(8,128)S(1)}, u32[]{:S(2)}, u32[]{:S(2)}) collective-permute-start(f32[184,128]{1,0:T(8,128)S(1)} %get-tuple-element.98), channel_id=1, source_target_pairs={{0,1},{1,2},{2,3},{3,0},{4,5},{5,6},{6,7},{7,4},{8,9},{9,10},{10,1... | collective-permute-start | bytes 282632 | tf_op jit(solution)/shard_map/ppermute | solution.py:612
  15.9 1.7 %collective-permute-start.6 = (f32[168,128]{1,0:T(8,128)S(1)}, f32[168,128]{1,0:T(8,128)S(1)}, u32[]{:S(2)}, u32[]{:S(2)}) collective-permute-start(f32[168,128]{1,0:T(8,128)S(1)} %get-tuple-element.100), channel_id=1, source_target_pairs={{0,3},{1,0},{2,1},{3,2},{4,7},{5,4},{6,5},{7,6},{8,11},{9,8},{10,9... | collective-permute-start | bytes 258056 | tf_op jit(solution)/shard_map/ppermute | solution.py:612
  17.6 1.8 %collective-permute-start.5 = (f32[152,128]{1,0:T(8,128)S(1)}, f32[152,128]{1,0:T(8,128)S(1)}, u32[]{:S(2)}, u32[]{:S(2)}) collective-permute-start(f32[152,128]{1,0:T(8,128)S(1)} %get-tuple-element.99), channel_id=1, source_target_pairs={{0,2},{1,3},{2,0},{3,1},{4,6},{5,7},{6,4},{7,5},{8,10},{9,11},{10,... | collective-permute-start | bytes 233480 | tf_op jit(solution)/shard_map/ppermute | solution.py:612
  19.5 4.1 %collective-permute-done.5.r2 = f32[152,128]{1,0:T(8,128)S(1)} collective-permute-done((f32[152,128]{1,0:T(8,128)S(1)}, f32[152,128]{1,0:T(8,128)S(1)}, u32[]{:S(2)}, u32[]{:S(2)}) %collective-permute-start.5) | collective-permute-done | bytes 77856 | tf_op jit(solution)/shard_map/ppermute | solution.py:612
  23.6 0.1 k2c.1
  23.6 1.6 %collective-permute-start.7 = (f32[208,128]{1,0:T(8,128)S(1)}, f32[208,128]{1,0:T(8,128)S(1)}, u32[]{:S(2)}, u32[]{:S(2)}) collective-permute-start(f32[208,128]{1,0:T(8,128)S(1)} %get-tuple-element.102), channel_id=1, source_target_pairs={{0,4},{1,5},{2,6},{3,7},{4,8},{5,9},{6,10},{7,11},{8,12},{9,13},{1... | collective-permute-start | bytes 319496 | tf_op jit(solution)/shard_map/ppermute | solution.py:617
  25.3 1.7 %collective-permute-start.9 = (f32[192,128]{1,0:T(8,128)S(1)}, f32[192,128]{1,0:T(8,128)S(1)}, u32[]{:S(2)}, u32[]{:S(2)}) collective-permute-start(f32[192,128]{1,0:T(8,128)S(1)} %get-tuple-element.104), channel_id=1, source_target_pairs={{0,12},{1,13},{2,14},{3,15},{4,0},{5,1},{6,2},{7,3},{8,4},{9,5},{1... | collective-permute-start | bytes 294920 | tf_op jit(solution)/shard_map/ppermute | solution.py:617
  26.9 2.0 %collective-permute-start.8 = (f32[176,128]{1,0:T(8,128)S(1)}, f32[176,128]{1,0:T(8,128)S(1)}, u32[]{:S(2)}, u32[]{:S(2)}) collective-permute-start(f32[176,128]{1,0:T(8,128)S(1)} %get-tuple-element.103), channel_id=1, source_target_pairs={{0,8},{1,9},{2,10},{3,11},{4,12},{5,13},{6,14},{7,15},{8,0},{9,1},... | collective-permute-start | bytes 270344 | tf_op jit(solution)/shard_map/ppermute | solution.py:617
  28.9 4.0 %collective-permute-done.8.s2 = f32[176,128]{1,0:T(8,128)S(1)} collective-permute-done((f32[176,128]{1,0:T(8,128)S(1)}, f32[176,128]{1,0:T(8,128)S(1)}, u32[]{:S(2)}, u32[]{:S(2)}) %collective-permute-start.8) | collective-permute-done | bytes 90144 | tf_op jit(solution)/shard_map/ppermute | solution.py:617
  33.0 0.9 %k3.1 = (f32[80,128]{1,0:T(8,128)S(1)}, f32[4,16,128]{2,1,0:T(8,128)S(1)}, f32[4,16,128]{2,1,0:T(8,128)S(1)}, f32[5,16,128]{2,1,0:T(8,128)S(1)}, f32[5,16,128]{2...) custom-call(f32[176,128]{1,0:T(8,128)S(1)} %get-tuple-element.101.ow, ...), custom_call_target="tpu_custom_call" | custom-call | tf_op jit(solution)/shard_map/k3/pallas_call | solution.py:589
  33.8 0.1 collective-permute-start.10
  33.9 1.2 %collective-permute-done.10.rc = f32[80,128]{1,0:T(8,128)S(1)} collective-permute-done((f32[80,128]{1,0:T(8,128)S(1)}, f32[80,128]{1,0:T(8,128)S(1)}, u32[]{:S(2)}, u32[]{:S(2)}) %collective-permute-start.10) | collective-permute-done | bytes 40992 | tf_op jit(solution)/shard_map/ppermute | solution.py:602
  35.2 0.5 collective-permute-start.11
  35.7 3.0 %collective-permute-start.12 = (f32[32,128]{1,0:T(8,128)S(1)}, f32[32,128]{1,0:T(8,128)S(1)}, u32[]{:S(2)}, u32[]{:S(2)}) collective-permute-start(f32[32,128]{1,0:T(8,128)S(1)} %get-tuple-element.129), channel_id=1, source_target_pairs={{0,64},{16,80},{32,96},{48,112},{64,0},{80,16},{96,32},{112,48},{1... | collective-permute-start | bytes 49160 | tf_op jit(solution)/shard_map/ppermute | solution.py:607
  38.7 1.0 %collective-permute-start.13 = (f32[32,128]{1,0:T(8,128)S(1)}, f32[32,128]{1,0:T(8,128)S(1)}, u32[]{:S(2)}, u32[]{:S(2)}) collective-permute-start(f32[32,128]{1,0:T(8,128)S(1)} %get-tuple-element.130), channel_id=1, source_target_pairs={{0,96},{16,112},{32,0},{48,16},{64,32},{80,48},{96,64},{112,80},{1... | collective-permute-start | bytes 49160 | tf_op jit(solution)/shard_map/ppermute | solution.py:607
  39.7 1.2 %collective-permute-done.12.z2 = f32[32,128]{1,0:T(8,128)S(1)} collective-permute-done((f32[32,128]{1,0:T(8,128)S(1)}, f32[32,128]{1,0:T(8,128)S(1)}, u32[]{:S(2)}, u32[]{:S(2)}) %collective-permute-start.12) | collective-permute-done | bytes 16416 | tf_op jit(solution)/shard_map/ppermute | solution.py:607
  40.9 1.5 %collective-permute-done.13.z3 = f32[32,128]{1,0:T(8,128)S(1)} collective-permute-done((f32[32,128]{1,0:T(8,128)S(1)}, f32[32,128]{1,0:T(8,128)S(1)}, u32[]{:S(2)}, u32[]{:S(2)}) %collective-permute-start.13) | collective-permute-done | bytes 16416 | tf_op jit(solution)/shard_map/ppermute | solution.py:607
  42.4 0.9 %k4.1 = (f32[16,16,128]{2,1,0:T(8,128)}, f32[256,128]{1,0:T(8,128)S(1)}, f32[256,128]{1,0:T(8,128)S(1)}, f32[2,16,128]{2,1,0:T(8,128)S(1)}) custom-call(f32[80,128]{1,0:T(8,128)S(1)} %get-tuple-element.119.own, f32[80,128]{1,0:T(8,128)S(1)} %collective-permute-done.10.rc, f32[48,128]{1,0:T(8,128)S(1)} %collective-permute-done.11.z1, ...), custom_call_target="tpu_custom_call" | custom-call | tf_op jit(solution)/shard_map/k4/pallas_call | solution.py:589
  43.3 4.6 %all-to-all-start = ((f32[16,16,128]{2,1,0:T(8,128)}), f32[16,16,128]{2,1,0:T(8,128)S(1)}, u32[]{:S(2)}, u32[]{:S(2)}) async-start(f32[16,16,128]{2,1,0:T(8,128)} %get-tuple-element.149), calls=%async_computation | async-start | bytes 262144 | tf_op jit(solution)/shard_map/all_to_all | solution.py:621
  47.9 3.6 %k4b.1 = (f32[3,256,128]{2,1,0:T(8,128)}, f32[3,256,128]{2,1,0:T(8,128)}) custom-call(f32[80,128]{1,0:T(8,128)S(1)} %get-tuple-element.119.own, f32[80,128]{1,0:T(8,128)S(1)} %collective-permute-done.10.rc, f32[48,128]{1,0:T(8,128)S(1)} %collective-permute-done.11.z1, f32[32,128]{1,0:T(8,128)S(1)} %collective-permute-done.12.z2, ...), custom_call_target="tpu_custom_call" | custom-call | tf_op jit(solution)/shard_map/k4b/pallas_call | solution.py:589
  51.4 4.4 %all-to-all-done.m4 = f32[16,16,128]{2,1,0:T(8,128)S(1)} async-done(((f32[16,16,128]{2,1,0:T(8,128)}), f32[16,16,128]{2,1,0:T(8,128)S(1)}, u32[]{:S(2)}, u32[]{:S(2)}) %all-to-all-start) | async-done | bytes 131104 | tf_op jit(solution)/shard_map/all_to_all | solution.py:621
  55.9 0.8 %k5.1 = (f32[3,256,128]{2,1,0:T(8,128)}, f32[3,256,128]{2,1,0:T(8,128)}) custom-call(f32[16,16,128]{2,1,0:T(8,128)S(1)} %all-to-all-done.m4, f32[2,16,128]{2,1,0:T(8,128)S(1)} %get-tuple-element.150.own, f32[256,128]{1,0:T(8,128)S(1)} %get-tuple-element.151.dz2, ...), custom_call_target="tpu_custom_call", output_to_operand_aliasing={{0}: (11, {}), {1}: (12, {})} | custom-call | tf_op jit(solution)/shard_map/k5/pallas_call | solution.py:589
  (12 shorter events, 0.1 us)
Async XLA Ops:
  0.6 9.5 %copy-start = (f32[3,16,16,128]{3,2,1,0:T(8,128)S(1)}, f32[3,16,16,128]{3,2,1,0:T(8,128)}, u32[]{:S(2)}) copy-start(f32[3,16,16,128]{3,2,1,0:T(8,128)} %param.9) | copy-start | bytes 1179652
  0.6 9.5 %copy-start.1 = (f32[3,16,16,128]{3,2,1,0:T(8,128)S(1)}, f32[3,16,16,128]{3,2,1,0:T(8,128)}, u32[]{:S(2)}) copy-start(f32[3,16,16,128]{3,2,1,0:T(8,128)} %param.10) | copy-start | bytes 1179652
  2.5 1.5 %collective-permute-start = (f32[344,128]{1,0:T(8,128)S(1)}, f32[344,128]{1,0:T(8,128)S(1)}, u32[]{:S(2)}, u32[]{:S(2)}) collective-permute-start(f32[344,128]{1,0:T(8,128)S(1)} %get-tuple-element.82.own), channel_id=1, source_target_pairs={{0,16},{16,0},{32,48},{48,32},{64,80},{80,64},{96,112},{112,96},{1... | collective-permute-start | bytes 528392 | tf_op jit(solution)/shard_map/ppermute | solution.py:602
  4.0 10.0 %collective-permute-start.1 = (f32[136,128]{1,0:T(8,128)S(1)}, f32[136,128]{1,0:T(8,128)S(1)}, u32[]{:S(2)}, u32[]{:S(2)}) collective-permute-start(f32[136,128]{1,0:T(8,128)S(1)} %get-tuple-element.88), channel_id=1, source_target_pairs={{0,32},{16,48},{32,64},{48,80},{64,96},{80,112},{96,0},{112,16},{1... | collective-permute-start | bytes 208904 | tf_op jit(solution)/shard_map/ppermute | solution.py:607
  6.1 7.9 %collective-permute-start.3 = (f32[136,128]{1,0:T(8,128)S(1)}, f32[136,128]{1,0:T(8,128)S(1)}, u32[]{:S(2)}, u32[]{:S(2)}) collective-permute-start(f32[136,128]{1,0:T(8,128)S(1)} %get-tuple-element.90), channel_id=1, source_target_pairs={{0,96},{16,112},{32,0},{48,16},{64,32},{80,48},{96,64},{112,80},{1... | collective-permute-start | bytes 208904 | tf_op jit(solution)/shard_map/ppermute | solution.py:607
  8.3 5.7 %collective-permute-start.2 = (f32[120,128]{1,0:T(8,128)S(1)}, f32[120,128]{1,0:T(8,128)S(1)}, u32[]{:S(2)}, u32[]{:S(2)}) collective-permute-start(f32[120,128]{1,0:T(8,128)S(1)} %get-tuple-element.89), channel_id=1, source_target_pairs={{0,64},{16,80},{32,96},{48,112},{64,0},{80,16},{96,32},{112,48},{1... | collective-permute-start | bytes 184328 | tf_op jit(solution)/shard_map/ppermute | solution.py:607
  14.3 9.2 %collective-permute-start.4 = (f32[184,128]{1,0:T(8,128)S(1)}, f32[184,128]{1,0:T(8,128)S(1)}, u32[]{:S(2)}, u32[]{:S(2)}) collective-permute-start(f32[184,128]{1,0:T(8,128)S(1)} %get-tuple-element.98), channel_id=1, source_target_pairs={{0,1},{1,2},{2,3},{3,0},{4,5},{5,6},{6,7},{7,4},{8,9},{9,10},{10,1... | collective-permute-start | bytes 282632 | tf_op jit(solution)/shard_map/ppermute | solution.py:612
  15.9 7.7 %collective-permute-start.6 = (f32[168,128]{1,0:T(8,128)S(1)}, f32[168,128]{1,0:T(8,128)S(1)}, u32[]{:S(2)}, u32[]{:S(2)}) collective-permute-start(f32[168,128]{1,0:T(8,128)S(1)} %get-tuple-element.100), channel_id=1, source_target_pairs={{0,3},{1,0},{2,1},{3,2},{4,7},{5,4},{6,5},{7,6},{8,11},{9,8},{10,9... | collective-permute-start | bytes 258056 | tf_op jit(solution)/shard_map/ppermute | solution.py:612
  17.6 5.9 %collective-permute-start.5 = (f32[152,128]{1,0:T(8,128)S(1)}, f32[152,128]{1,0:T(8,128)S(1)}, u32[]{:S(2)}, u32[]{:S(2)}) collective-permute-start(f32[152,128]{1,0:T(8,128)S(1)} %get-tuple-element.99), channel_id=1, source_target_pairs={{0,2},{1,3},{2,0},{3,1},{4,6},{5,7},{6,4},{7,5},{8,10},{9,11},{10,... | collective-permute-start | bytes 233480 | tf_op jit(solution)/shard_map/ppermute | solution.py:612
  23.6 9.3 %collective-permute-start.7 = (f32[208,128]{1,0:T(8,128)S(1)}, f32[208,128]{1,0:T(8,128)S(1)}, u32[]{:S(2)}, u32[]{:S(2)}) collective-permute-start(f32[208,128]{1,0:T(8,128)S(1)} %get-tuple-element.102), channel_id=1, source_target_pairs={{0,4},{1,5},{2,6},{3,7},{4,8},{5,9},{6,10},{7,11},{8,12},{9,13},{1... | collective-permute-start | bytes 319496 | tf_op jit(solution)/shard_map/ppermute | solution.py:617
  25.3 7.7 %collective-permute-start.9 = (f32[192,128]{1,0:T(8,128)S(1)}, f32[192,128]{1,0:T(8,128)S(1)}, u32[]{:S(2)}, u32[]{:S(2)}) collective-permute-start(f32[192,128]{1,0:T(8,128)S(1)} %get-tuple-element.104), channel_id=1, source_target_pairs={{0,12},{1,13},{2,14},{3,15},{4,0},{5,1},{6,2},{7,3},{8,4},{9,5},{1... | collective-permute-start | bytes 294920 | tf_op jit(solution)/shard_map/ppermute | solution.py:617
  26.9 6.0 %collective-permute-start.8 = (f32[176,128]{1,0:T(8,128)S(1)}, f32[176,128]{1,0:T(8,128)S(1)}, u32[]{:S(2)}, u32[]{:S(2)}) collective-permute-start(f32[176,128]{1,0:T(8,128)S(1)} %get-tuple-element.103), channel_id=1, source_target_pairs={{0,8},{1,9},{2,10},{3,11},{4,12},{5,13},{6,14},{7,15},{8,0},{9,1},... | collective-permute-start | bytes 270344 | tf_op jit(solution)/shard_map/ppermute | solution.py:617
  33.8 1.3 %collective-permute-start.10 = (f32[80,128]{1,0:T(8,128)S(1)}, f32[80,128]{1,0:T(8,128)S(1)}, u32[]{:S(2)}, u32[]{:S(2)}) collective-permute-start(f32[80,128]{1,0:T(8,128)S(1)} %get-tuple-element.119.own), channel_id=1, source_target_pairs={{0,16},{16,0},{32,48},{48,32},{64,80},{80,64},{96,112},{112,96},{1... | collective-permute-start | bytes 122888 | tf_op jit(solution)/shard_map/ppermute | solution.py:602
  35.2 7.2 %collective-permute-start.11 = (f32[48,128]{1,0:T(8,128)S(1)}, f32[48,128]{1,0:T(8,128)S(1)}, u32[]{:S(2)}, u32[]{:S(2)}) collective-permute-start(f32[48,128]{1,0:T(8,128)S(1)} %get-tuple-element.128), channel_id=1, source_target_pairs={{0,32},{16,48},{32,64},{48,80},{64,96},{80,112},{96,0},{112,16},{1... | collective-permute-start | bytes 73736 | tf_op jit(solution)/shard_map/ppermute | solution.py:607
  35.7 5.2 %collective-permute-start.12 = (f32[32,128]{1,0:T(8,128)S(1)}, f32[32,128]{1,0:T(8,128)S(1)}, u32[]{:S(2)}, u32[]{:S(2)}) collective-permute-start(f32[32,128]{1,0:T(8,128)S(1)} %get-tuple-element.129), channel_id=1, source_target_pairs={{0,64},{16,80},{32,96},{48,112},{64,0},{80,16},{96,32},{112,48},{1... | collective-permute-start | bytes 49160 | tf_op jit(solution)/shard_map/ppermute | solution.py:607
  38.7 3.7 %collective-permute-start.13 = (f32[32,128]{1,0:T(8,128)S(1)}, f32[32,128]{1,0:T(8,128)S(1)}, u32[]{:S(2)}, u32[]{:S(2)}) collective-permute-start(f32[32,128]{1,0:T(8,128)S(1)} %get-tuple-element.130), channel_id=1, source_target_pairs={{0,96},{16,112},{32,0},{48,16},{64,32},{80,48},{96,64},{112,80},{1... | collective-permute-start | bytes 49160 | tf_op jit(solution)/shard_map/ppermute | solution.py:607
  43.3 12.6 %all-to-all-start = ((f32[16,16,128]{2,1,0:T(8,128)}), f32[16,16,128]{2,1,0:T(8,128)S(1)}, u32[]{:S(2)}, u32[]{:S(2)}) async-start(f32[16,16,128]{2,1,0:T(8,128)} %get-tuple-element.149), calls=%async_computation | async-start | bytes 262144 | tf_op jit(solution)/shard_map/all_to_all | solution.py:621

commit v4 on v3

--- a/solution.py
+++ b/solution.py
@@ -71,7 +71,8 @@
     return d / e
 
 
-def z_factors(w, out):
+def z_factors(w_ref, out, part):
+    w = w_ref[part, :]
     lane = iota(w.shape, 1)
     a = jnp.where(lane == 0, 0.0, 1.0)
     c = jnp.where(lane == NZ - 1, 0.0, 1.0)
@@ -81,18 +82,18 @@
         rb = 1.0 / (e + a + c)
         low = a * pltpu.roll(rb, step, 1)
         high = c * pltpu.roll(rb, NZ - step, 1)
-        out[2 * k], out[2 * k + 1] = low, high
+        out[2 * k, part, :], out[2 * k + 1, part, :] = low, high
         e = e + low * pltpu.roll(e, step, 1) + high * pltpu.roll(e, NZ - step, 1)
         if k < 6:
             a, c = low * pltpu.roll(a, step, 1), high * pltpu.roll(c, NZ - step, 1)
-    out[14] = 1.0 / e
-
-
-def z_apply(d, f):
+    out[14, part, :] = 1.0 / e
+
+
+def z_apply(d, f, part):
     for k in range(7):
         step = 1 << k
-        d = d + f[2 * k] * pltpu.roll(d, step, 1) + f[2 * k + 1] * pltpu.roll(d, NZ - step, 1)
-    return d * f[14]
+        d = d + f[2 * k, part, :] * pltpu.roll(d, step, 1) + f[2 * k + 1, part, :] * pltpu.roll(d, NZ - step, 1)
+    return d * f[14, part, :]
 
 
 def pivots(ws):
@@ -209,7 +210,7 @@
     ]
     for copy in copies:
         copy.start()
-    for copy in copies[:3]:
+    for copy in copies:
         copy.wait()
     ws = [(perm[k] + 8.0 * cond[k]) * (1.0 / 4096.0) for k in range(8)]
     vs = [(perm[k] - 8.0 * cond[k]) * (1.0 / 4096.0) for k in range(8)]
@@ -231,8 +232,6 @@
     for x in range(CX):
         fx_o[x] = fwd[x]
         bx_o[x] = bwd[x]
-    for copy in copies[3:]:
-        copy.wait()
     to = dest[...]
     to_b = jnp.broadcast_to(to, (128, 128))
     same = (to_b.T == to_b) & (iota((128, 128), 0) < iota((128, 128), 1))
@@ -276,7 +275,7 @@
     mz3[Z_HALO:Z_HALO + 16, :] = jnp.where(c == 0, own[C_HALO + 16:C_HALO + 32, :], rc[C_HALO + 16:C_HALO + 32, :])
 
 
-def k1b(e, h, w, v, fy_o, by_o, g_o, hyp_o, dz_o, hxpp_o, dy2_o, zx_o, zy_o, hxp_s, ey1_s, dy1_s):
+def k1b(e, h, w, fy_o, by_o, g_o):
     ws = [w[strided(y), :] for y in range(CY)]
     fwd, bwd, link = pivots(ws)
     for y in range(CY):
@@ -285,8 +284,9 @@
     g_o[0] = bwd[0]
     g_o[1] = link
     g_o[2] = fwd[CY - 1]
-    z_factors(w[rows(0), :], zx_o)
-    z_factors(w[strided(CY - 1), :], zy_o)
+
+
+def k2a(e, h, w, v, hyp_o, dz_o, hxp_o, dy1_o, zf_o):
     prev_hyp = None
     prev_hz = None
     for x in range(CX):
@@ -295,7 +295,7 @@
         ex = e[0, rows(x), :]
         hz = h[2, rows(x), :]
         hxp = hx - HS * (y_up(ez, 0.0) - ez)
-        hxp_s[rows(x), :] = hxp
+        hxp_o[rows(x), :] = hxp
         hyp = h[1, rows(x), :] - HS * (z_up(ex) - ex)
         hyp_o[rows(x), :] = hyp
         curl_z = hyp - (hx - y_down(hx, 0.0))
@@ -306,14 +306,19 @@
         prev_hyp = hyp
         prev_hz = hz
         dz_o[rows(x), :] = v[rows(x), :] * ez + INV * curl_z
-        dy1_s[rows(x), :] = v[rows(x), :] * e[1, rows(x), :] + INV * curl_y
+        dy1_o[rows(x), :] = v[rows(x), :] * e[1, rows(x), :] + INV * curl_y
+    for q in range(4):
+        z_factors(w, zf_o, pl.ds(q * 64, 64))
+
+
+def k2b(v, hxp, dy1, zf, hxpp_o, dy2_o, ey1_s):
     for q in range(4):
         part = pl.ds(q * 64, 64)
-        ey1_s[part, :] = z_solve(w[part, :], dy1_s[part, :])
+        ey1_s[part, :] = z_apply(dy1[part, :], zf, part)
     for x in range(CX):
         ey1 = ey1_s[rows(x), :]
         dey1 = HS * (z_up(ey1) - ey1)
-        hx1 = hxp_s[rows(x), :] + dey1
+        hx1 = hxp[rows(x), :] + dey1
         hxpp_o[rows(x), :] = hx1 + dey1
         dy2_o[rows(x), :] = v[rows(x), :] * ey1 + INV * (hx1 - z_down(hx1))
 
@@ -393,7 +398,7 @@
 
 
 def k3(own, s1, s2, s3, r1, r3, blk, h0, hr0, v, hzp, dx, fy, fx, bx, hz_low,
-       hyp, dz0, hxpp0, dy20, zx, zy,
+       hyp, dz0, hxpp0, dy20, zf,
        msg, hs_c, hrs_c, bes, des, hg_c, hrg_c, beg, deg, tr_o, ex1_o, hz1_o, hz1m_o, inj_o, hxpp_o, hzpp_o,
        dz_o, dy2_o, grp):
     gy = lax.axis_index("gy")
@@ -446,10 +451,10 @@
     dz_o[...] = dz0[...] - INV * inj
     dz_o[strided(0), :] = dz_o[strided(0), :] + INV * hx_low
     c_h = -HS * ez_high
-    c_e = z_apply(INV * (c_h - z_down(c_h)), zy)
+    c_e = z_apply(INV * (c_h - z_down(c_h)), zf, strided(CY - 1))
     c_d = HS * (z_up(c_e) - c_e)
     c_1 = c_h + c_d
-    b_e = z_apply(INV * hz_low[...], zx)
+    b_e = z_apply(INV * hz_low[...], zf, rows(0))
     b_d = HS * (z_up(b_e) - b_e)
     hxpp_o[...] = hxpp0[...]
     hxpp_o[rows(0), :] = hxpp_o[rows(0), :] + (b_d + b_d)
@@ -649,23 +654,25 @@
     msgz, ownz, blkx, pstat = out[:3], out[3], out[4], out[5:]
     msgz, w1 = lax.optimization_barrier((msgz, w))
     rz = [ring_z(m, d) for d, m in enumerate(msgz, 1)]
-    (fy, by, g, hyp, dz0, hxpp0, dy20, zx, zy) = call(
-        k1b, [LINE, LINE, (3,) + FACE, FIELD, FIELD, FIELD, FIELD, (15,) + FACE, (15,) + FACE],
-        (e, h, w1, v), scratch=[FIELD, FIELD, FIELD])
+    fy, by, g = call(k1b, [LINE, LINE, (3,) + FACE], (e, h, w1))
     out = call(
         k2, [(X_HALO + HALO[d], NZ) for d in (1, 2, 3)] + [
             (X_HALO, NZ), FIELD, FIELD, FACE] + chain + chain2,
         (rc, ownz, *rz, blkx, e, h, v, fy, by, g), scratch=[(4, 64, NZ), FIELD, (8, NZ), (4, 48, NZ)])
     msgx, (ownx, hzp, dx, hz_low), xsup, xgrp = out[:3], out[3:7], out[7:11], out[11:]
+    msgx, w2 = lax.optimization_barrier((msgx, w))
     rx = [ring_x(m, d) for d, m in enumerate(msgx, 1)]
+    hyp, dz0, hxp, dy1, zf = call(k2a, [FIELD] * 4 + [(15,) + FIELD], (e, h, w2, v))
     out = call(
         k2c, [(Y_HALO + HALO[d], NZ) for d in (1, 2, 3)] + [(Y_HALO, NZ), (4, 80, NZ)] + chain, (ownx, *rx))
     msgy, owny, blk, zstat = out[:3], out[3], out[4], out[5:]
+    msgy, zf1 = lax.optimization_barrier((msgy, zf))
     ry = [ring_y(m, d) for d, m in enumerate(msgy, 1)]
+    hxpp0, dy20 = call(k2b, [FIELD, FIELD], (v, hxp, dy1, zf1), scratch=[FIELD])
     out = call(
         k3, [(80, NZ)] + chain + chain + [(2,) + FACE, FIELD, FIELD, FACE, FIELD, FIELD, FIELD, FIELD, FIELD],
         (owny, *ry, rx[0], rx[2], blk, zstat[0], zstat[1], v, hzp, dx, fy, fx, bx, hz_low,
-         hyp, dz0, hxpp0, dy20, zx, zy), scratch=[(4, 80, NZ)])
+         hyp, dz0, hxpp0, dy20, zf), scratch=[(4, 80, NZ)])
     msg3, sstat, gstat, tr = out[0], out[1:5], out[5:9], out[9]
     ex1, hz1, hz1m, inj, hxpp, hzpp, dz, dy2 = out[10:]
     rc3 = pair(msg3)

time: 56.9 us -> 56.8 us (level)
  waiting for transfers between devices: 18.5 us -> 16 us
  local copies, waits for them, and re-layouts: 0.01 us -> 1.99 us
    ppermute x3, waiting for transfers between devices: 4.09 us -> 1.37 us  [ring_x(): return lax.ppermute(message, 'gy', pairs)]
    unnamed x4, local copies, waits for them, and re-layouts: 0.01 us -> 1.99 us
    ppermute x6, waiting for transfers between devices: 3.36 us -> 4.52 us  [ring_z(): return lax.ppermute(message, 'gx', pairs)]
    ppermute x3, waiting for transfers between devices: 4.05 us -> 3.1 us  [ring_y(): return lax.ppermute(message, 'gy', pairs)]
    pallas_call x10 -> x12, Pallas kernels: 11.7 us -> 12 us  [call(): pl.pallas_call(kernel, out_shape=[jax.ShapeDtypeStruct(s, F32) for s in s...]
  transfers between devices with their start and end apart: 15 -> 15, of which waited for: 8 -> 8; matrix products, arithmetic and copies ran while one was open for 0% -> 0% of each run, Pallas kernels for 12% -> 13%
where the time goes in v4:
time: 56.8 us; the launch traced here: 56.5 us
  starting transfers between devices  25.7 us (45%)
  waiting for transfers between devices  16 us (28%)
  Pallas kernels  12 us (21%)
  local copies, waits for them, and re-layouts  1.99 us (4%)
  between operations  0.74 us (1%)
    pallas_call x12, Pallas kernels, call(): pl.pallas_call(kernel, out_shape=[jax.ShapeDtypeStruct(s, F32) for s in s...  12 us
    ppermute x6, starting transfers between devices, ring_z(): return lax.ppermute(message, 'gx', pairs)  10.5 us
    ppermute x3, starting transfers between devices, ring_y(): return lax.ppermute(message, 'gy', pairs)  5.29 us
    ppermute x3, starting transfers between devices, ring_x(): return lax.ppermute(message, 'gy', pairs)  5.12 us
    all_to_all x1, starting transfers between devices, exchange(): lax.all_to_all(message, axis, split_axis=0, concat_axis=0, tiled=True)  4.62 us
    ppermute x6, waiting for transfers between devices, ring_z(): return lax.ppermute(message, 'gx', pairs)  4.52 us
    all_to_all x1, waiting for transfers between devices, exchange(): lax.all_to_all(message, axis, split_axis=0, concat_axis=0, tiled=True)  4.43 us
    ppermute x3, waiting for transfers between devices, ring_y(): return lax.ppermute(message, 'gy', pairs)  3.1 us
  transfers between devices with their start and end apart: 15, of which 8 were waited for; matrix products, arithmetic and copies ran while one was open for 0% of the time, Pallas kernels for 13%

profile of v4, /device:TPU:0, one launch (start us, length us, event | category | flops | bytes accessed | tf_op | source)
XLA Modules:
  0.0 56.5 jit_solution(2588078251053287245)
XLA Ops:
  0.6 1.7 %k1.1 = (f32[344,128]{1,0:T(8,128)S(1)}, f32[256,128]{1,0:T(8,128)S(1)}, f32[256,128]{1,0:T(8,128)S(1)}, f32[16,16,128]{2,1,0:T(8,128)S(1)}, f32[16,16,128]{2,1,0:T(8,128)S(1)}) custom-call(f32[3,256,128]{2,1,0:T(8,128)} %bitcast.9, f32[3,256,128]{2,1,0:T(8,128)} %bitcast.13, s32[256,128]{1,0:T(8,128)} %bitcast.19, f32[8]{0:T(128)} %perm_h.1, f32[8]{0:T(128)} %cond_h.1, ...), custom_call_target="tpu_custom_call" | custom-call | tf_op jit(solution)/shard_map/k1/pallas_call | solution.py:594
  2.4 1.4 %collective-permute-done.rc = f32[344,128]{1,0:T(8,128)S(1)} collective-permute-done((f32[344,128]{1,0:T(8,128)S(1)}, f32[344,128]{1,0:T(8,128)S(1)}, u32[]{:S(2)}, u32[]{:S(2)}) %collective-permute-start) | collective-permute-done | bytes 176160 | tf_op jit(solution)/shard_map/ppermute | solution.py:607
  3.8 2.1 %collective-permute-start.1 = (f32[136,128]{1,0:T(8,128)S(1)}, f32[136,128]{1,0:T(8,128)S(1)}, u32[]{:S(2)}, u32[]{:S(2)}) collective-permute-start(f32[136,128]{1,0:T(8,128)S(1)} %get-tuple-element.97), channel_id=1, source_target_pairs={{0,32},{16,48},{32,64},{48,80},{64,96},{80,112},{96,0},{112,16},{1... | collective-permute-start | bytes 208904 | tf_op jit(solution)/shard_map/ppermute | solution.py:612
  5.9 2.2 %collective-permute-start.3 = (f32[136,128]{1,0:T(8,128)S(1)}, f32[136,128]{1,0:T(8,128)S(1)}, u32[]{:S(2)}, u32[]{:S(2)}) collective-permute-start(f32[136,128]{1,0:T(8,128)S(1)} %get-tuple-element.99), channel_id=1, source_target_pairs={{0,96},{16,112},{32,0},{48,16},{64,32},{80,48},{96,64},{112,80},{1... | collective-permute-start | bytes 208904 | tf_op jit(solution)/shard_map/ppermute | solution.py:612
  8.1 1.8 %collective-permute-start.2 = (f32[120,128]{1,0:T(8,128)S(1)}, f32[120,128]{1,0:T(8,128)S(1)}, u32[]{:S(2)}, u32[]{:S(2)}) collective-permute-start(f32[120,128]{1,0:T(8,128)S(1)} %get-tuple-element.98), channel_id=1, source_target_pairs={{0,64},{16,80},{32,96},{48,112},{64,0},{80,16},{96,32},{112,48},{1... | collective-permute-start | bytes 184328 | tf_op jit(solution)/shard_map/ppermute | solution.py:612
  9.9 1.0 %copy-done = f32[3,16,16,128]{3,2,1,0:T(8,128)S(1)} copy-done((f32[3,16,16,128]{3,2,1,0:T(8,128)S(1)}, f32[3,16,16,128]{3,2,1,0:T(8,128)}, u32[]{:S(2)}) %copy-start) | copy-done | bytes 393240
  10.9 1.0 %copy-done.1 = f32[3,16,16,128]{3,2,1,0:T(8,128)S(1)} copy-done((f32[3,16,16,128]{3,2,1,0:T(8,128)S(1)}, f32[3,16,16,128]{3,2,1,0:T(8,128)}, u32[]{:S(2)}) %copy-start.1) | copy-done | bytes 393240
  11.9 0.2 k1b.1
  12.0 1.8 %collective-permute-done.2.z2 = f32[120,128]{1,0:T(8,128)S(1)} collective-permute-done((f32[120,128]{1,0:T(8,128)S(1)}, f32[120,128]{1,0:T(8,128)S(1)}, u32[]{:S(2)}, u32[]{:S(2)}) %collective-permute-start.2) | collective-permute-done | bytes 61472 | tf_op jit(solution)/shard_map/ppermute | solution.py:612
  13.8 0.3 k2.1
  14.1 1.6 %collective-permute-start.4 = (f32[184,128]{1,0:T(8,128)S(1)}, f32[184,128]{1,0:T(8,128)S(1)}, u32[]{:S(2)}, u32[]{:S(2)}) collective-permute-start(f32[184,128]{1,0:T(8,128)S(1)} %get-tuple-element.110), channel_id=1, source_target_pairs={{0,1},{1,2},{2,3},{3,0},{4,5},{5,6},{6,7},{7,4},{8,9},{9,10},{10,1... | collective-permute-start | bytes 282632 | tf_op jit(solution)/shard_map/ppermute | solution.py:617
  15.7 1.7 %collective-permute-start.6 = (f32[168,128]{1,0:T(8,128)S(1)}, f32[168,128]{1,0:T(8,128)S(1)}, u32[]{:S(2)}, u32[]{:S(2)}) collective-permute-start(f32[168,128]{1,0:T(8,128)S(1)} %get-tuple-element.112), channel_id=1, source_target_pairs={{0,3},{1,0},{2,1},{3,2},{4,7},{5,4},{6,5},{7,6},{8,11},{9,8},{10,9... | collective-permute-start | bytes 258056 | tf_op jit(solution)/shard_map/ppermute | solution.py:617
  17.4 1.8 %collective-permute-start.5 = (f32[152,128]{1,0:T(8,128)S(1)}, f32[152,128]{1,0:T(8,128)S(1)}, u32[]{:S(2)}, u32[]{:S(2)}) collective-permute-start(f32[152,128]{1,0:T(8,128)S(1)} %get-tuple-element.111), channel_id=1, source_target_pairs={{0,2},{1,3},{2,0},{3,1},{4,6},{5,7},{6,4},{7,5},{8,10},{9,11},{10,... | collective-permute-start | bytes 233480 | tf_op jit(solution)/shard_map/ppermute | solution.py:617
  19.2 2.7 %k2a.1 = (f32[256,128]{1,0:T(8,128)S(1)}, f32[256,128]{1,0:T(8,128)S(1)}, f32[256,128]{1,0:T(8,128)S(1)}, f32[256,128]{1,0:T(8,128)S(1)}, f32[15,256,128]{2,1,0:T(8,128)S(1)}) custom-call(f32[3,256,128]{2,1,0:T(8,128)S(1)} %bitcast.12, f32[3,256,128]{2,1,0:T(8,128)S(1)} %bitcast.16, f32[256,128]{1,0:T(8,128)S(1)} %get-tuple-element.117.w, ...), custom_call_target="tpu_custom_call" | custom-call | tf_op jit(solution)/shard_map/k2a/pallas_call | solution.py:594
  22.0 1.4 %collective-permute-done.5.r2 = f32[152,128]{1,0:T(8,128)S(1)} collective-permute-done((f32[152,128]{1,0:T(8,128)S(1)}, f32[152,128]{1,0:T(8,128)S(1)}, u32[]{:S(2)}, u32[]{:S(2)}) %collective-permute-start.5) | collective-permute-done | bytes 77856 | tf_op jit(solution)/shard_map/ppermute | solution.py:617
  23.4 1.6 %collective-permute-start.7 = (f32[208,128]{1,0:T(8,128)S(1)}, f32[208,128]{1,0:T(8,128)S(1)}, u32[]{:S(2)}, u32[]{:S(2)}) collective-permute-start(f32[208,128]{1,0:T(8,128)S(1)} %get-tuple-element.119), channel_id=1, source_target_pairs={{0,4},{1,5},{2,6},{3,7},{4,8},{5,9},{6,10},{7,11},{8,12},{9,13},{1... | collective-permute-start | bytes 319496 | tf_op jit(solution)/shard_map/ppermute | solution.py:622
  25.1 1.7 %collective-permute-start.9 = (f32[192,128]{1,0:T(8,128)S(1)}, f32[192,128]{1,0:T(8,128)S(1)}, u32[]{:S(2)}, u32[]{:S(2)}) collective-permute-start(f32[192,128]{1,0:T(8,128)S(1)} %get-tuple-element.121), channel_id=1, source_target_pairs={{0,12},{1,13},{2,14},{3,15},{4,0},{5,1},{6,2},{7,3},{8,4},{9,5},{1... | collective-permute-start | bytes 294920 | tf_op jit(solution)/shard_map/ppermute | solution.py:622
  26.7 2.0 %collective-permute-start.8 = (f32[176,128]{1,0:T(8,128)S(1)}, f32[176,128]{1,0:T(8,128)S(1)}, u32[]{:S(2)}, u32[]{:S(2)}) collective-permute-start(f32[176,128]{1,0:T(8,128)S(1)} %get-tuple-element.120), channel_id=1, source_target_pairs={{0,8},{1,9},{2,10},{3,11},{4,12},{5,13},{6,14},{7,15},{8,0},{9,1},... | collective-permute-start | bytes 270344 | tf_op jit(solution)/shard_map/ppermute | solution.py:622
  28.7 0.9 %k2b.1 = (f32[256,128]{1,0:T(8,128)S(1)}, f32[256,128]{1,0:T(8,128)S(1)}) custom-call(f32[256,128]{1,0:T(8,128)S(1)} %get-tuple-element.101.v, f32[256,128]{1,0:T(8,128)S(1)} %get-tuple-element.132.hxp, f32[256,128]{1,0:T(8,128)S(1)} %get-tuple-element.133.dy1, f32[15,256,128]{2,1,0:T(8,128)S(1)} %get-tuple-element.134.zf), custom_call_target="tpu_custom_call" | custom-call | tf_op jit(solution)/shard_map/k2b/pallas_call | solution.py:594
  29.7 3.1 %collective-permute-done.8.s2 = f32[176,128]{1,0:T(8,128)S(1)} collective-permute-done((f32[176,128]{1,0:T(8,128)S(1)}, f32[176,128]{1,0:T(8,128)S(1)}, u32[]{:S(2)}, u32[]{:S(2)}) %collective-permute-start.8) | collective-permute-done | bytes 90144 | tf_op jit(solution)/shard_map/ppermute | solution.py:622
  32.8 0.9 %k3.1 = (f32[80,128]{1,0:T(8,128)S(1)}, f32[4,16,128]{2,1,0:T(8,128)S(1)}, f32[4,16,128]{2,1,0:T(8,128)S(1)}, f32[5,16,128]{2,1,0:T(8,128)S(1)}, f32[5,16,128]{2...) custom-call(f32[176,128]{1,0:T(8,128)S(1)} %get-tuple-element.113.ow, ...), custom_call_target="tpu_custom_call" | custom-call | tf_op jit(solution)/shard_map/k3/pallas_call | solution.py:594
  33.7 1.2 %collective-permute-done.10.rc = f32[80,128]{1,0:T(8,128)S(1)} collective-permute-done((f32[80,128]{1,0:T(8,128)S(1)}, f32[80,128]{1,0:T(8,128)S(1)}, u32[]{:S(2)}, u32[]{:S(2)}) %collective-permute-start.10) | collective-permute-done | bytes 40992 | tf_op jit(solution)/shard_map/ppermute | solution.py:607
  35.0 0.4 collective-permute-start.11
  35.4 3.1 %collective-permute-start.12 = (f32[32,128]{1,0:T(8,128)S(1)}, f32[32,128]{1,0:T(8,128)S(1)}, u32[]{:S(2)}, u32[]{:S(2)}) collective-permute-start(f32[32,128]{1,0:T(8,128)S(1)} %get-tuple-element.147), channel_id=1, source_target_pairs={{0,64},{16,80},{32,96},{48,112},{64,0},{80,16},{96,32},{112,48},{1... | collective-permute-start | bytes 49160 | tf_op jit(solution)/shard_map/ppermute | solution.py:612
  38.5 1.0 %collective-permute-start.13 = (f32[32,128]{1,0:T(8,128)S(1)}, f32[32,128]{1,0:T(8,128)S(1)}, u32[]{:S(2)}, u32[]{:S(2)}) collective-permute-start(f32[32,128]{1,0:T(8,128)S(1)} %get-tuple-element.148), channel_id=1, source_target_pairs={{0,96},{16,112},{32,0},{48,16},{64,32},{80,48},{96,64},{112,80},{1... | collective-permute-start | bytes 49160 | tf_op jit(solution)/shard_map/ppermute | solution.py:612
  39.5 1.1 %collective-permute-done.12.z2 = f32[32,128]{1,0:T(8,128)S(1)} collective-permute-done((f32[32,128]{1,0:T(8,128)S(1)}, f32[32,128]{1,0:T(8,128)S(1)}, u32[]{:S(2)}, u32[]{:S(2)}) %collective-permute-start.12) | collective-permute-done | bytes 16416 | tf_op jit(solution)/shard_map/ppermute | solution.py:612
  40.6 1.6 %collective-permute-done.13.z3 = f32[32,128]{1,0:T(8,128)S(1)} collective-permute-done((f32[32,128]{1,0:T(8,128)S(1)}, f32[32,128]{1,0:T(8,128)S(1)}, u32[]{:S(2)}, u32[]{:S(2)}) %collective-permute-start.13) | collective-permute-done | bytes 16416 | tf_op jit(solution)/shard_map/ppermute | solution.py:612
  42.2 0.9 %k4.1 = (f32[16,16,128]{2,1,0:T(8,128)}, f32[256,128]{1,0:T(8,128)S(1)}, f32[256,128]{1,0:T(8,128)S(1)}, f32[2,16,128]{2,1,0:T(8,128)S(1)}) custom-call(f32[80,128]{1,0:T(8,128)S(1)} %get-tuple-element.137.own, f32[80,128]{1,0:T(8,128)S(1)} %collective-permute-done.10.rc, f32[48,128]{1,0:T(8,128)S(1)} %collective-permute-done.11.z1, ...), custom_call_target="tpu_custom_call" | custom-call | tf_op jit(solution)/shard_map/k4/pallas_call | solution.py:594
  43.1 4.6 %all-to-all-start = ((f32[16,16,128]{2,1,0:T(8,128)}), f32[16,16,128]{2,1,0:T(8,128)S(1)}, u32[]{:S(2)}, u32[]{:S(2)}) async-start(f32[16,16,128]{2,1,0:T(8,128)} %get-tuple-element.167), calls=%async_computation | async-start | bytes 262144 | tf_op jit(solution)/shard_map/all_to_all | solution.py:626
  47.7 3.6 %k4b.1 = (f32[3,256,128]{2,1,0:T(8,128)}, f32[3,256,128]{2,1,0:T(8,128)}) custom-call(f32[80,128]{1,0:T(8,128)S(1)} %get-tuple-element.137.own, f32[80,128]{1,0:T(8,128)S(1)} %collective-permute-done.10.rc, f32[48,128]{1,0:T(8,128)S(1)} %collective-permute-done.11.z1, f32[32,128]{1,0:T(8,128)S(1)} %collective-permute-done.12.z2, ...), custom_call_target="tpu_custom_call" | custom-call | tf_op jit(solution)/shard_map/k4b/pallas_call | solution.py:594
  51.2 4.4 %all-to-all-done.m4 = f32[16,16,128]{2,1,0:T(8,128)S(1)} async-done(((f32[16,16,128]{2,1,0:T(8,128)}), f32[16,16,128]{2,1,0:T(8,128)S(1)}, u32[]{:S(2)}, u32[]{:S(2)}) %all-to-all-start) | async-done | bytes 131104 | tf_op jit(solution)/shard_map/all_to_all | solution.py:626
  55.7 0.8 %k5.1 = (f32[3,256,128]{2,1,0:T(8,128)}, f32[3,256,128]{2,1,0:T(8,128)}) custom-call(f32[16,16,128]{2,1,0:T(8,128)S(1)} %all-to-all-done.m4, f32[2,16,128]{2,1,0:T(8,128)S(1)} %get-tuple-element.168.own, f32[256,128]{1,0:T(8,128)S(1)} %get-tuple-element.169.dz2, ...), custom_call_target="tpu_custom_call", output_to_operand_aliasing={{0}: (11, {}), {1}: (12, {})} | custom-call | tf_op jit(solution)/shard_map/k5/pallas_call | solution.py:594
  (14 shorter events, 0.3 us)
Async XLA Ops:
  2.3 1.5 %collective-permute-start = (f32[344,128]{1,0:T(8,128)S(1)}, f32[344,128]{1,0:T(8,128)S(1)}, u32[]{:S(2)}, u32[]{:S(2)}) collective-permute-start(f32[344,128]{1,0:T(8,128)S(1)} %get-tuple-element.91.own), channel_id=1, source_target_pairs={{0,16},{16,0},{32,48},{48,32},{64,80},{80,64},{96,112},{112,96},{1... | collective-permute-start | bytes 528392 | tf_op jit(solution)/shard_map/ppermute | solution.py:607
  3.8 10.0 %collective-permute-start.1 = (f32[136,128]{1,0:T(8,128)S(1)}, f32[136,128]{1,0:T(8,128)S(1)}, u32[]{:S(2)}, u32[]{:S(2)}) collective-permute-start(f32[136,128]{1,0:T(8,128)S(1)} %get-tuple-element.97), channel_id=1, source_target_pairs={{0,32},{16,48},{32,64},{48,80},{64,96},{80,112},{96,0},{112,16},{1... | collective-permute-start | bytes 208904 | tf_op jit(solution)/shard_map/ppermute | solution.py:612
  5.9 7.9 %collective-permute-start.3 = (f32[136,128]{1,0:T(8,128)S(1)}, f32[136,128]{1,0:T(8,128)S(1)}, u32[]{:S(2)}, u32[]{:S(2)}) collective-permute-start(f32[136,128]{1,0:T(8,128)S(1)} %get-tuple-element.99), channel_id=1, source_target_pairs={{0,96},{16,112},{32,0},{48,16},{64,32},{80,48},{96,64},{112,80},{1... | collective-permute-start | bytes 208904 | tf_op jit(solution)/shard_map/ppermute | solution.py:612
  8.1 5.7 %collective-permute-start.2 = (f32[120,128]{1,0:T(8,128)S(1)}, f32[120,128]{1,0:T(8,128)S(1)}, u32[]{:S(2)}, u32[]{:S(2)}) collective-permute-start(f32[120,128]{1,0:T(8,128)S(1)} %get-tuple-element.98), channel_id=1, source_target_pairs={{0,64},{16,80},{32,96},{48,112},{64,0},{80,16},{96,32},{112,48},{1... | collective-permute-start | bytes 184328 | tf_op jit(solution)/shard_map/ppermute | solution.py:612
  9.9 1.0 %copy-start = (f32[3,16,16,128]{3,2,1,0:T(8,128)S(1)}, f32[3,16,16,128]{3,2,1,0:T(8,128)}, u32[]{:S(2)}) copy-start(f32[3,16,16,128]{3,2,1,0:T(8,128)} %param.9) | copy-start | bytes 1179652
  10.9 1.0 %copy-start.1 = (f32[3,16,16,128]{3,2,1,0:T(8,128)S(1)}, f32[3,16,16,128]{3,2,1,0:T(8,128)}, u32[]{:S(2)}) copy-start(f32[3,16,16,128]{3,2,1,0:T(8,128)} %param.10) | copy-start | bytes 1179652
  14.1 9.2 %collective-permute-start.4 = (f32[184,128]{1,0:T(8,128)S(1)}, f32[184,128]{1,0:T(8,128)S(1)}, u32[]{:S(2)}, u32[]{:S(2)}) collective-permute-start(f32[184,128]{1,0:T(8,128)S(1)} %get-tuple-element.110), channel_id=1, source_target_pairs={{0,1},{1,2},{2,3},{3,0},{4,5},{5,6},{6,7},{7,4},{8,9},{9,10},{10,1... | collective-permute-start | bytes 282632 | tf_op jit(solution)/shard_map/ppermute | solution.py:617
  15.7 7.7 %collective-permute-start.6 = (f32[168,128]{1,0:T(8,128)S(1)}, f32[168,128]{1,0:T(8,128)S(1)}, u32[]{:S(2)}, u32[]{:S(2)}) collective-permute-start(f32[168,128]{1,0:T(8,128)S(1)} %get-tuple-element.112), channel_id=1, source_target_pairs={{0,3},{1,0},{2,1},{3,2},{4,7},{5,4},{6,5},{7,6},{8,11},{9,8},{10,9... | collective-permute-start | bytes 258056 | tf_op jit(solution)/shard_map/ppermute | solution.py:617
  17.4 5.9 %collective-permute-start.5 = (f32[152,128]{1,0:T(8,128)S(1)}, f32[152,128]{1,0:T(8,128)S(1)}, u32[]{:S(2)}, u32[]{:S(2)}) collective-permute-start(f32[152,128]{1,0:T(8,128)S(1)} %get-tuple-element.111), channel_id=1, source_target_pairs={{0,2},{1,3},{2,0},{3,1},{4,6},{5,7},{6,4},{7,5},{8,10},{9,11},{10,... | collective-permute-start | bytes 233480 | tf_op jit(solution)/shard_map/ppermute | solution.py:617
  23.4 9.3 %collective-permute-start.7 = (f32[208,128]{1,0:T(8,128)S(1)}, f32[208,128]{1,0:T(8,128)S(1)}, u32[]{:S(2)}, u32[]{:S(2)}) collective-permute-start(f32[208,128]{1,0:T(8,128)S(1)} %get-tuple-element.119), channel_id=1, source_target_pairs={{0,4},{1,5},{2,6},{3,7},{4,8},{5,9},{6,10},{7,11},{8,12},{9,13},{1... | collective-permute-start | bytes 319496 | tf_op jit(solution)/shard_map/ppermute | solution.py:622
  25.1 7.7 %collective-permute-start.9 = (f32[192,128]{1,0:T(8,128)S(1)}, f32[192,128]{1,0:T(8,128)S(1)}, u32[]{:S(2)}, u32[]{:S(2)}) collective-permute-start(f32[192,128]{1,0:T(8,128)S(1)} %get-tuple-element.121), channel_id=1, source_target_pairs={{0,12},{1,13},{2,14},{3,15},{4,0},{5,1},{6,2},{7,3},{8,4},{9,5},{1... | collective-permute-start | bytes 294920 | tf_op jit(solution)/shard_map/ppermute | solution.py:622
  26.7 6.0 %collective-permute-start.8 = (f32[176,128]{1,0:T(8,128)S(1)}, f32[176,128]{1,0:T(8,128)S(1)}, u32[]{:S(2)}, u32[]{:S(2)}) collective-permute-start(f32[176,128]{1,0:T(8,128)S(1)} %get-tuple-element.120), channel_id=1, source_target_pairs={{0,8},{1,9},{2,10},{3,11},{4,12},{5,13},{6,14},{7,15},{8,0},{9,1},... | collective-permute-start | bytes 270344 | tf_op jit(solution)/shard_map/ppermute | solution.py:622
  33.6 1.3 %collective-permute-start.10 = (f32[80,128]{1,0:T(8,128)S(1)}, f32[80,128]{1,0:T(8,128)S(1)}, u32[]{:S(2)}, u32[]{:S(2)}) collective-permute-start(f32[80,128]{1,0:T(8,128)S(1)} %get-tuple-element.137.own), channel_id=1, source_target_pairs={{0,16},{16,0},{32,48},{48,32},{64,80},{80,64},{96,112},{112,96},{1... | collective-permute-start | bytes 122888 | tf_op jit(solution)/shard_map/ppermute | solution.py:607
  35.0 7.2 %collective-permute-start.11 = (f32[48,128]{1,0:T(8,128)S(1)}, f32[48,128]{1,0:T(8,128)S(1)}, u32[]{:S(2)}, u32[]{:S(2)}) collective-permute-start(f32[48,128]{1,0:T(8,128)S(1)} %get-tuple-element.146), channel_id=1, source_target_pairs={{0,32},{16,48},{32,64},{48,80},{64,96},{80,112},{96,0},{112,16},{1... | collective-permute-start | bytes 73736 | tf_op jit(solution)/shard_map/ppermute | solution.py:612
  35.4 5.2 %collective-permute-start.12 = (f32[32,128]{1,0:T(8,128)S(1)}, f32[32,128]{1,0:T(8,128)S(1)}, u32[]{:S(2)}, u32[]{:S(2)}) collective-permute-start(f32[32,128]{1,0:T(8,128)S(1)} %get-tuple-element.147), channel_id=1, source_target_pairs={{0,64},{16,80},{32,96},{48,112},{64,0},{80,16},{96,32},{112,48},{1... | collective-permute-start | bytes 49160 | tf_op jit(solution)/shard_map/ppermute | solution.py:612
  38.5 3.7 %collective-permute-start.13 = (f32[32,128]{1,0:T(8,128)S(1)}, f32[32,128]{1,0:T(8,128)S(1)}, u32[]{:S(2)}, u32[]{:S(2)}) collective-permute-start(f32[32,128]{1,0:T(8,128)S(1)} %get-tuple-element.148), channel_id=1, source_target_pairs={{0,96},{16,112},{32,0},{48,16},{64,32},{80,48},{96,64},{112,80},{1... | collective-permute-start | bytes 49160 | tf_op jit(solution)/shard_map/ppermute | solution.py:612
  43.1 12.6 %all-to-all-start = ((f32[16,16,128]{2,1,0:T(8,128)}), f32[16,16,128]{2,1,0:T(8,128)S(1)}, u32[]{:S(2)}, u32[]{:S(2)}) async-start(f32[16,16,128]{2,1,0:T(8,128)} %get-tuple-element.167), calls=%async_computation | async-start | bytes 262144 | tf_op jit(solution)/shard_map/all_to_all | solution.py:626

commit v5 on v4

--- a/solution.py
+++ b/solution.py
@@ -200,7 +200,7 @@
     return part(hi) + part(mid) + part(low)
 
 
-def k1(e_h, h_h, mat_h, perm_h, cond_h, cells_h, dest_h, tgt_h, gain_h, msg, w_o, v_o, fx_o, bx_o,
+def k1(e_h, h_h, mat_h, perm_h, cond_h, cells_h, dest_h, tgt_h, gain_h, msg, w_o, v_o, fx_o, bx_o, e_o, h_o,
        ez, ey_first, hz_last, mat, perm, cond, cells, dest, tgt, gain, sem):
     copies = [
         pltpu.make_async_copy(src, dst, sem.at[k])
@@ -208,7 +208,8 @@
             (perm_h, perm), (cond_h, cond), (mat_h, mat), (dest_h, dest), (cells_h, cells), (tgt_h, tgt),
             (gain_h, gain), (e_h.at[2], ez), (e_h.at[1, rows(0)], ey_first), (h_h.at[2, rows(CX - 1)], hz_last)])
     ]
-    for copy in copies:
+    whole = [pltpu.make_async_copy(e_h, e_o, sem.at[10]), pltpu.make_async_copy(h_h, h_o, sem.at[11])]
+    for copy in copies + whole:
         copy.start()
     for copy in copies:
         copy.wait()
@@ -253,6 +254,8 @@
     msg[C_HALO + 16:C_HALO + 32, :] = ey_first[...]
     for f, face in enumerate((bwd[0], link, fwd[CX - 1])):
         msg[C_COEF + 16 * f:C_COEF + 16 * f + 16, :] = face
+    for copy in whole:
+        copy.wait()
 
 
 def k1c(own, rc, mz1, mz2, mz3, own_o, blk_o, h_o, hr_o, be_o, de_o):
@@ -275,7 +278,7 @@
     mz3[Z_HALO:Z_HALO + 16, :] = jnp.where(c == 0, own[C_HALO + 16:C_HALO + 32, :], rc[C_HALO + 16:C_HALO + 32, :])
 
 
-def k1b(e, h, w, fy_o, by_o, g_o):
+def k1b(w, fy_o, by_o, g_o):
     ws = [w[strided(y), :] for y in range(CY)]
     fwd, bwd, link = pivots(ws)
     for y in range(CY):
@@ -641,11 +644,11 @@
     hbm = [pltpu.with_memory_space_constraint(a, pltpu.HBM) for a in (
         e, h, mat, permittivity, conductivity, electrode_cells.reshape(row),
         electrode_dest.reshape(row), target_cells.reshape(row), electrode_gain.reshape(row))]
-    msg1, w, v, fx, bx = call(
-        k1, [(C_ALL, NZ), FIELD, FIELD, LINE, LINE],
+    msg1, w, v, fx, bx, e, h = call(
+        k1, [(C_ALL, NZ), FIELD, FIELD, LINE, LINE, (3,) + FIELD, (3,) + FIELD],
         hbm,
         scratch=[FIELD, FACE, FACE, pltpu.VMEM(FIELD, jnp.int32), pltpu.SMEM((8,), F32), pltpu.SMEM((8,), F32),
-                 pltpu.VMEM(row, jnp.int32), pltpu.VMEM(row, jnp.int32), pltpu.VMEM(row, jnp.int32), row, dma((10,))],
+                 pltpu.VMEM(row, jnp.int32), pltpu.VMEM(row, jnp.int32), pltpu.VMEM(row, jnp.int32), row, dma((12,))],
         hbm_in=range(9))
     chain2 = [(2,) + FACE, (2,) + FACE, (3,) + FACE, (3,) + FACE]
     chain = [(4,) + FACE, (4,) + FACE, (5,) + FACE, (5,) + FACE]
@@ -654,7 +657,7 @@
     msgz, ownz, blkx, pstat = out[:3], out[3], out[4], out[5:]
     msgz, w1 = lax.optimization_barrier((msgz, w))
     rz = [ring_z(m, d) for d, m in enumerate(msgz, 1)]
-    fy, by, g = call(k1b, [LINE, LINE, (3,) + FACE], (e, h, w1))
+    fy, by, g = call(k1b, [LINE, LINE, (3,) + FACE], (w1,))
     out = call(
         k2, [(X_HALO + HALO[d], NZ) for d in (1, 2, 3)] + [
             (X_HALO, NZ), FIELD, FIELD, FACE] + chain + chain2,

time: 56.8 us -> 56.7 us (level)
  waiting for transfers between devices: 16 us -> 18 us
  local copies, waits for them, and re-layouts: 1.99 us -> 0 us
    ppermute x6, waiting for transfers between devices: 4.52 us -> 6.51 us  [ring_z(): return lax.ppermute(message, 'gx', pairs)]
    unnamed x4 -> x0, local copies, waits for them, and re-layouts: 1.99 us -> none
where the time goes in v5:
time: 56.7 us; the launch traced here: 56.5 us
  starting transfers between devices  25.7 us (45%)
  waiting for transfers between devices  18 us (32%)
  Pallas kernels  12.1 us (21%)
  between operations  0.74 us (1%)
    pallas_call x12, Pallas kernels, call(): pl.pallas_call(kernel, out_shape=[jax.ShapeDtypeStruct(s, F32) for s in s...  12.1 us
    ppermute x6, starting transfers between devices, ring_z(): return lax.ppermute(message, 'gx', pairs)  10.5 us
    ppermute x6, waiting for transfers between devices, ring_z(): return lax.ppermute(message, 'gx', pairs)  6.51 us
    ppermute x3, starting transfers between devices, ring_y(): return lax.ppermute(message, 'gy', pairs)  5.29 us
    ppermute x3, starting transfers between devices, ring_x(): return lax.ppermute(message, 'gy', pairs)  5.12 us
    all_to_all x1, starting transfers between devices, exchange(): lax.all_to_all(message, axis, split_axis=0, concat_axis=0, tiled=True)  4.61 us
    all_to_all x1, waiting for transfers between devices, exchange(): lax.all_to_all(message, axis, split_axis=0, concat_axis=0, tiled=True)  4.43 us
    ppermute x3, waiting for transfers between devices, ring_y(): return lax.ppermute(message, 'gy', pairs)  3.1 us
  transfers between devices with their start and end apart: 15, of which 8 were waited for; matrix products, arithmetic and copies ran while one was open for 0% of the time, Pallas kernels for 13%

profile of v5, /device:TPU:0, one launch (start us, length us, event | category | flops | bytes accessed | tf_op | source)
XLA Modules:
  0.0 56.5 jit_solution(10214191849074559708)
XLA Ops:
  0.6 1.7 %k1.1 = (f32[344,128]{1,0:T(8,128)S(1)}, f32[256,128]{1,0:T(8,128)S(1)}, f32[256,128]{1,0:T(8,128)S(1)}, f32[16,16,128]{2,1,0:T(8,128)S(1)}, f32[16,16,128]{2,1,...) custom-call(f32[3,256,128]{2,1,0:T(8,128)} %bitcast.9, f32[3,256,128]{2,1,0:T(8,128)} %bitcast.10, ...), custom_call_target="tpu_custom_call" | custom-call | tf_op jit(solution)/shard_map/k1/pallas_call | solution.py:597
  2.3 0.1 collective-permute-start
  2.4 1.4 %collective-permute-done.rc = f32[344,128]{1,0:T(8,128)S(1)} collective-permute-done((f32[344,128]{1,0:T(8,128)S(1)}, f32[344,128]{1,0:T(8,128)S(1)}, u32[]{:S(2)}, u32[]{:S(2)}) %collective-permute-start) | collective-permute-done | bytes 176160 | tf_op jit(solution)/shard_map/ppermute | solution.py:610
  3.9 2.1 %collective-permute-start.1 = (f32[136,128]{1,0:T(8,128)S(1)}, f32[136,128]{1,0:T(8,128)S(1)}, u32[]{:S(2)}, u32[]{:S(2)}) collective-permute-start(f32[136,128]{1,0:T(8,128)S(1)} %get-tuple-element.99), channel_id=1, source_target_pairs={{0,32},{16,48},{32,64},{48,80},{64,96},{80,112},{96,0},{112,16},{1... | collective-permute-start | bytes 208904 | tf_op jit(solution)/shard_map/ppermute | solution.py:615
  5.9 2.2 %collective-permute-start.3 = (f32[136,128]{1,0:T(8,128)S(1)}, f32[136,128]{1,0:T(8,128)S(1)}, u32[]{:S(2)}, u32[]{:S(2)}) collective-permute-start(f32[136,128]{1,0:T(8,128)S(1)} %get-tuple-element.101), channel_id=1, source_target_pairs={{0,96},{16,112},{32,0},{48,16},{64,32},{80,48},{96,64},{112,80},{1... | collective-permute-start | bytes 208904 | tf_op jit(solution)/shard_map/ppermute | solution.py:615
  8.1 1.8 %collective-permute-start.2 = (f32[120,128]{1,0:T(8,128)S(1)}, f32[120,128]{1,0:T(8,128)S(1)}, u32[]{:S(2)}, u32[]{:S(2)}) collective-permute-start(f32[120,128]{1,0:T(8,128)S(1)} %get-tuple-element.100), channel_id=1, source_target_pairs={{0,64},{16,80},{32,96},{48,112},{64,0},{80,16},{96,32},{112,48},{1... | collective-permute-start | bytes 184328 | tf_op jit(solution)/shard_map/ppermute | solution.py:615
  9.9 0.2 k1b.1
  10.1 3.8 %collective-permute-done.2.z2 = f32[120,128]{1,0:T(8,128)S(1)} collective-permute-done((f32[120,128]{1,0:T(8,128)S(1)}, f32[120,128]{1,0:T(8,128)S(1)}, u32[]{:S(2)}, u32[]{:S(2)}) %collective-permute-start.2) | collective-permute-done | bytes 61472 | tf_op jit(solution)/shard_map/ppermute | solution.py:615
  13.9 0.3 k2.1
  14.2 1.6 %collective-permute-start.4 = (f32[184,128]{1,0:T(8,128)S(1)}, f32[184,128]{1,0:T(8,128)S(1)}, u32[]{:S(2)}, u32[]{:S(2)}) collective-permute-start(f32[184,128]{1,0:T(8,128)S(1)} %get-tuple-element.114), channel_id=1, source_target_pairs={{0,1},{1,2},{2,3},{3,0},{4,5},{5,6},{6,7},{7,4},{8,9},{9,10},{10,1... | collective-permute-start | bytes 282632 | tf_op jit(solution)/shard_map/ppermute | solution.py:620
  15.7 1.7 %collective-permute-start.6 = (f32[168,128]{1,0:T(8,128)S(1)}, f32[168,128]{1,0:T(8,128)S(1)}, u32[]{:S(2)}, u32[]{:S(2)}) collective-permute-start(f32[168,128]{1,0:T(8,128)S(1)} %get-tuple-element.116), channel_id=1, source_target_pairs={{0,3},{1,0},{2,1},{3,2},{4,7},{5,4},{6,5},{7,6},{8,11},{9,8},{10,9... | collective-permute-start | bytes 258056 | tf_op jit(solution)/shard_map/ppermute | solution.py:620
  17.5 1.8 %collective-permute-start.5 = (f32[152,128]{1,0:T(8,128)S(1)}, f32[152,128]{1,0:T(8,128)S(1)}, u32[]{:S(2)}, u32[]{:S(2)}) collective-permute-start(f32[152,128]{1,0:T(8,128)S(1)} %get-tuple-element.115), channel_id=1, source_target_pairs={{0,2},{1,3},{2,0},{3,1},{4,6},{5,7},{6,4},{7,5},{8,10},{9,11},{10,... | collective-permute-start | bytes 233480 | tf_op jit(solution)/shard_map/ppermute | solution.py:620
  19.3 2.7 %k2a.1 = (f32[256,128]{1,0:T(8,128)S(1)}, f32[256,128]{1,0:T(8,128)S(1)}, f32[256,128]{1,0:T(8,128)S(1)}, f32[256,128]{1,0:T(8,128)S(1)}, f32[15,256,128]{2,1,0:T(8,128)S(1)}) custom-call(f32[3,256,128]{2,1,0:T(8,128)S(1)} %get-tuple-element.103.e, f32[3,256,128]{2,1,0:T(8,128)S(1)} %get-tuple-element.104.h, f32[256,128]{1,0:T(8,128)S(1)} %get-tuple-element.121.w, ...), custom_call_target="tpu_custom_call" | custom-call | tf_op jit(solution)/shard_map/k2a/pallas_call | solution.py:597
  22.0 1.4 %collective-permute-done.5.r2 = f32[152,128]{1,0:T(8,128)S(1)} collective-permute-done((f32[152,128]{1,0:T(8,128)S(1)}, f32[152,128]{1,0:T(8,128)S(1)}, u32[]{:S(2)}, u32[]{:S(2)}) %collective-permute-start.5) | collective-permute-done | bytes 77856 | tf_op jit(solution)/shard_map/ppermute | solution.py:620
  23.5 1.6 %collective-permute-start.7 = (f32[208,128]{1,0:T(8,128)S(1)}, f32[208,128]{1,0:T(8,128)S(1)}, u32[]{:S(2)}, u32[]{:S(2)}) collective-permute-start(f32[208,128]{1,0:T(8,128)S(1)} %get-tuple-element.123), channel_id=1, source_target_pairs={{0,4},{1,5},{2,6},{3,7},{4,8},{5,9},{6,10},{7,11},{8,12},{9,13},{1... | collective-permute-start | bytes 319496 | tf_op jit(solution)/shard_map/ppermute | solution.py:625
  25.1 1.7 %collective-permute-start.9 = (f32[192,128]{1,0:T(8,128)S(1)}, f32[192,128]{1,0:T(8,128)S(1)}, u32[]{:S(2)}, u32[]{:S(2)}) collective-permute-start(f32[192,128]{1,0:T(8,128)S(1)} %get-tuple-element.125), channel_id=1, source_target_pairs={{0,12},{1,13},{2,14},{3,15},{4,0},{5,1},{6,2},{7,3},{8,4},{9,5},{1... | collective-permute-start | bytes 294920 | tf_op jit(solution)/shard_map/ppermute | solution.py:625
  26.8 2.0 %collective-permute-start.8 = (f32[176,128]{1,0:T(8,128)S(1)}, f32[176,128]{1,0:T(8,128)S(1)}, u32[]{:S(2)}, u32[]{:S(2)}) collective-permute-start(f32[176,128]{1,0:T(8,128)S(1)} %get-tuple-element.124), channel_id=1, source_target_pairs={{0,8},{1,9},{2,10},{3,11},{4,12},{5,13},{6,14},{7,15},{8,0},{9,1},... | collective-permute-start | bytes 270344 | tf_op jit(solution)/shard_map/ppermute | solution.py:625
  28.8 0.9 %k2b.1 = (f32[256,128]{1,0:T(8,128)S(1)}, f32[256,128]{1,0:T(8,128)S(1)}) custom-call(f32[256,128]{1,0:T(8,128)S(1)} %get-tuple-element.105.v, f32[256,128]{1,0:T(8,128)S(1)} %get-tuple-element.136.hxp, f32[256,128]{1,0:T(8,128)S(1)} %get-tuple-element.137.dy1, f32[15,256,128]{2,1,0:T(8,128)S(1)} %get-tuple-element.138.zf), custom_call_target="tpu_custom_call" | custom-call | tf_op jit(solution)/shard_map/k2b/pallas_call | solution.py:597
  29.7 3.1 %collective-permute-done.8.s2 = f32[176,128]{1,0:T(8,128)S(1)} collective-permute-done((f32[176,128]{1,0:T(8,128)S(1)}, f32[176,128]{1,0:T(8,128)S(1)}, u32[]{:S(2)}, u32[]{:S(2)}) %collective-permute-start.8) | collective-permute-done | bytes 90144 | tf_op jit(solution)/shard_map/ppermute | solution.py:625
  32.8 0.9 %k3.1 = (f32[80,128]{1,0:T(8,128)S(1)}, f32[4,16,128]{2,1,0:T(8,128)S(1)}, f32[4,16,128]{2,1,0:T(8,128)S(1)}, f32[5,16,128]{2,1,0:T(8,128)S(1)}, f32[5,16,128]{2...) custom-call(f32[176,128]{1,0:T(8,128)S(1)} %get-tuple-element.117.ow, ...), custom_call_target="tpu_custom_call" | custom-call | tf_op jit(solution)/shard_map/k3/pallas_call | solution.py:597
  33.7 0.1 collective-permute-start.10
  33.8 1.2 %collective-permute-done.10.rc = f32[80,128]{1,0:T(8,128)S(1)} collective-permute-done((f32[80,128]{1,0:T(8,128)S(1)}, f32[80,128]{1,0:T(8,128)S(1)}, u32[]{:S(2)}, u32[]{:S(2)}) %collective-permute-start.10) | collective-permute-done | bytes 40992 | tf_op jit(solution)/shard_map/ppermute | solution.py:610
  35.0 0.4 collective-permute-start.11
  35.4 3.1 %collective-permute-start.12 = (f32[32,128]{1,0:T(8,128)S(1)}, f32[32,128]{1,0:T(8,128)S(1)}, u32[]{:S(2)}, u32[]{:S(2)}) collective-permute-start(f32[32,128]{1,0:T(8,128)S(1)} %get-tuple-element.151), channel_id=1, source_target_pairs={{0,64},{16,80},{32,96},{48,112},{64,0},{80,16},{96,32},{112,48},{1... | collective-permute-start | bytes 49160 | tf_op jit(solution)/shard_map/ppermute | solution.py:615
  38.5 1.0 %collective-permute-start.13 = (f32[32,128]{1,0:T(8,128)S(1)}, f32[32,128]{1,0:T(8,128)S(1)}, u32[]{:S(2)}, u32[]{:S(2)}) collective-permute-start(f32[32,128]{1,0:T(8,128)S(1)} %get-tuple-element.152), channel_id=1, source_target_pairs={{0,96},{16,112},{32,0},{48,16},{64,32},{80,48},{96,64},{112,80},{1... | collective-permute-start | bytes 49160 | tf_op jit(solution)/shard_map/ppermute | solution.py:615
  39.5 1.1 %collective-permute-done.12.z2 = f32[32,128]{1,0:T(8,128)S(1)} collective-permute-done((f32[32,128]{1,0:T(8,128)S(1)}, f32[32,128]{1,0:T(8,128)S(1)}, u32[]{:S(2)}, u32[]{:S(2)}) %collective-permute-start.12) | collective-permute-done | bytes 16416 | tf_op jit(solution)/shard_map/ppermute | solution.py:615
  40.6 1.6 %collective-permute-done.13.z3 = f32[32,128]{1,0:T(8,128)S(1)} collective-permute-done((f32[32,128]{1,0:T(8,128)S(1)}, f32[32,128]{1,0:T(8,128)S(1)}, u32[]{:S(2)}, u32[]{:S(2)}) %collective-permute-start.13) | collective-permute-done | bytes 16416 | tf_op jit(solution)/shard_map/ppermute | solution.py:615
  42.2 0.9 %k4.1 = (f32[16,16,128]{2,1,0:T(8,128)}, f32[256,128]{1,0:T(8,128)S(1)}, f32[256,128]{1,0:T(8,128)S(1)}, f32[2,16,128]{2,1,0:T(8,128)S(1)}) custom-call(f32[80,128]{1,0:T(8,128)S(1)} %get-tuple-element.141.own, f32[80,128]{1,0:T(8,128)S(1)} %collective-permute-done.10.rc, f32[48,128]{1,0:T(8,128)S(1)} %collective-permute-done.11.z1, ...), custom_call_target="tpu_custom_call" | custom-call | tf_op jit(solution)/shard_map/k4/pallas_call | solution.py:597
  43.1 4.6 %all-to-all-start = ((f32[16,16,128]{2,1,0:T(8,128)}), f32[16,16,128]{2,1,0:T(8,128)S(1)}, u32[]{:S(2)}, u32[]{:S(2)}) async-start(f32[16,16,128]{2,1,0:T(8,128)} %get-tuple-element.171), calls=%async_computation | async-start | bytes 262144 | tf_op jit(solution)/shard_map/all_to_all | solution.py:629
  47.7 3.6 %k4b.1 = (f32[3,256,128]{2,1,0:T(8,128)}, f32[3,256,128]{2,1,0:T(8,128)}) custom-call(f32[80,128]{1,0:T(8,128)S(1)} %get-tuple-element.141.own, f32[80,128]{1,0:T(8,128)S(1)} %collective-permute-done.10.rc, f32[48,128]{1,0:T(8,128)S(1)} %collective-permute-done.11.z1, f32[32,128]{1,0:T(8,128)S(1)} %collective-permute-done.12.z2, ...), custom_call_target="tpu_custom_call" | custom-call | tf_op jit(solution)/shard_map/k4b/pallas_call | solution.py:597
  51.3 4.4 %all-to-all-done.m4 = f32[16,16,128]{2,1,0:T(8,128)S(1)} async-done(((f32[16,16,128]{2,1,0:T(8,128)}), f32[16,16,128]{2,1,0:T(8,128)S(1)}, u32[]{:S(2)}, u32[]{:S(2)}) %all-to-all-start) | async-done | bytes 131104 | tf_op jit(solution)/shard_map/all_to_all | solution.py:629
  55.7 0.8 %k5.1 = (f32[3,256,128]{2,1,0:T(8,128)}, f32[3,256,128]{2,1,0:T(8,128)}) custom-call(f32[16,16,128]{2,1,0:T(8,128)S(1)} %all-to-all-done.m4, f32[2,16,128]{2,1,0:T(8,128)S(1)} %get-tuple-element.172.own, f32[256,128]{1,0:T(8,128)S(1)} %get-tuple-element.173.dz2, ...), custom_call_target="tpu_custom_call", output_to_operand_aliasing={{0}: (11, {}), {1}: (12, {})} | custom-call | tf_op jit(solution)/shard_map/k5/pallas_call | solution.py:597
  (10 shorter events, 0.2 us)
Async XLA Ops:
  2.3 1.5 %collective-permute-start = (f32[344,128]{1,0:T(8,128)S(1)}, f32[344,128]{1,0:T(8,128)S(1)}, u32[]{:S(2)}, u32[]{:S(2)}) collective-permute-start(f32[344,128]{1,0:T(8,128)S(1)} %get-tuple-element.93.own), channel_id=1, source_target_pairs={{0,16},{16,0},{32,48},{48,32},{64,80},{80,64},{96,112},{112,96},{1... | collective-permute-start | bytes 528392 | tf_op jit(solution)/shard_map/ppermute | solution.py:610
  3.9 10.0 %collective-permute-start.1 = (f32[136,128]{1,0:T(8,128)S(1)}, f32[136,128]{1,0:T(8,128)S(1)}, u32[]{:S(2)}, u32[]{:S(2)}) collective-permute-start(f32[136,128]{1,0:T(8,128)S(1)} %get-tuple-element.99), channel_id=1, source_target_pairs={{0,32},{16,48},{32,64},{48,80},{64,96},{80,112},{96,0},{112,16},{1... | collective-permute-start | bytes 208904 | tf_op jit(solution)/shard_map/ppermute | solution.py:615
  5.9 7.9 %collective-permute-start.3 = (f32[136,128]{1,0:T(8,128)S(1)}, f32[136,128]{1,0:T(8,128)S(1)}, u32[]{:S(2)}, u32[]{:S(2)}) collective-permute-start(f32[136,128]{1,0:T(8,128)S(1)} %get-tuple-element.101), channel_id=1, source_target_pairs={{0,96},{16,112},{32,0},{48,16},{64,32},{80,48},{96,64},{112,80},{1... | collective-permute-start | bytes 208904 | tf_op jit(solution)/shard_map/ppermute | solution.py:615
  8.1 5.7 %collective-permute-start.2 = (f32[120,128]{1,0:T(8,128)S(1)}, f32[120,128]{1,0:T(8,128)S(1)}, u32[]{:S(2)}, u32[]{:S(2)}) collective-permute-start(f32[120,128]{1,0:T(8,128)S(1)} %get-tuple-element.100), channel_id=1, source_target_pairs={{0,64},{16,80},{32,96},{48,112},{64,0},{80,16},{96,32},{112,48},{1... | collective-permute-start | bytes 184328 | tf_op jit(solution)/shard_map/ppermute | solution.py:615
  14.2 9.2 %collective-permute-start.4 = (f32[184,128]{1,0:T(8,128)S(1)}, f32[184,128]{1,0:T(8,128)S(1)}, u32[]{:S(2)}, u32[]{:S(2)}) collective-permute-start(f32[184,128]{1,0:T(8,128)S(1)} %get-tuple-element.114), channel_id=1, source_target_pairs={{0,1},{1,2},{2,3},{3,0},{4,5},{5,6},{6,7},{7,4},{8,9},{9,10},{10,1... | collective-permute-start | bytes 282632 | tf_op jit(solution)/shard_map/ppermute | solution.py:620
  15.7 7.7 %collective-permute-start.6 = (f32[168,128]{1,0:T(8,128)S(1)}, f32[168,128]{1,0:T(8,128)S(1)}, u32[]{:S(2)}, u32[]{:S(2)}) collective-permute-start(f32[168,128]{1,0:T(8,128)S(1)} %get-tuple-element.116), channel_id=1, source_target_pairs={{0,3},{1,0},{2,1},{3,2},{4,7},{5,4},{6,5},{7,6},{8,11},{9,8},{10,9... | collective-permute-start | bytes 258056 | tf_op jit(solution)/shard_map/ppermute | solution.py:620
  17.5 5.9 %collective-permute-start.5 = (f32[152,128]{1,0:T(8,128)S(1)}, f32[152,128]{1,0:T(8,128)S(1)}, u32[]{:S(2)}, u32[]{:S(2)}) collective-permute-start(f32[152,128]{1,0:T(8,128)S(1)} %get-tuple-element.115), channel_id=1, source_target_pairs={{0,2},{1,3},{2,0},{3,1},{4,6},{5,7},{6,4},{7,5},{8,10},{9,11},{10,... | collective-permute-start | bytes 233480 | tf_op jit(solution)/shard_map/ppermute | solution.py:620
  23.5 9.3 %collective-permute-start.7 = (f32[208,128]{1,0:T(8,128)S(1)}, f32[208,128]{1,0:T(8,128)S(1)}, u32[]{:S(2)}, u32[]{:S(2)}) collective-permute-start(f32[208,128]{1,0:T(8,128)S(1)} %get-tuple-element.123), channel_id=1, source_target_pairs={{0,4},{1,5},{2,6},{3,7},{4,8},{5,9},{6,10},{7,11},{8,12},{9,13},{1... | collective-permute-start | bytes 319496 | tf_op jit(solution)/shard_map/ppermute | solution.py:625
  25.1 7.7 %collective-permute-start.9 = (f32[192,128]{1,0:T(8,128)S(1)}, f32[192,128]{1,0:T(8,128)S(1)}, u32[]{:S(2)}, u32[]{:S(2)}) collective-permute-start(f32[192,128]{1,0:T(8,128)S(1)} %get-tuple-element.125), channel_id=1, source_target_pairs={{0,12},{1,13},{2,14},{3,15},{4,0},{5,1},{6,2},{7,3},{8,4},{9,5},{1... | collective-permute-start | bytes 294920 | tf_op jit(solution)/shard_map/ppermute | solution.py:625
  26.8 6.0 %collective-permute-start.8 = (f32[176,128]{1,0:T(8,128)S(1)}, f32[176,128]{1,0:T(8,128)S(1)}, u32[]{:S(2)}, u32[]{:S(2)}) collective-permute-start(f32[176,128]{1,0:T(8,128)S(1)} %get-tuple-element.124), channel_id=1, source_target_pairs={{0,8},{1,9},{2,10},{3,11},{4,12},{5,13},{6,14},{7,15},{8,0},{9,1},... | collective-permute-start | bytes 270344 | tf_op jit(solution)/shard_map/ppermute | solution.py:625
  33.7 1.3 %collective-permute-start.10 = (f32[80,128]{1,0:T(8,128)S(1)}, f32[80,128]{1,0:T(8,128)S(1)}, u32[]{:S(2)}, u32[]{:S(2)}) collective-permute-start(f32[80,128]{1,0:T(8,128)S(1)} %get-tuple-element.141.own), channel_id=1, source_target_pairs={{0,16},{16,0},{32,48},{48,32},{64,80},{80,64},{96,112},{112,96},{1... | collective-permute-start | bytes 122888 | tf_op jit(solution)/shard_map/ppermute | solution.py:610
  35.0 7.2 %collective-permute-start.11 = (f32[48,128]{1,0:T(8,128)S(1)}, f32[48,128]{1,0:T(8,128)S(1)}, u32[]{:S(2)}, u32[]{:S(2)}) collective-permute-start(f32[48,128]{1,0:T(8,128)S(1)} %get-tuple-element.150), channel_id=1, source_target_pairs={{0,32},{16,48},{32,64},{48,80},{64,96},{80,112},{96,0},{112,16},{1... | collective-permute-start | bytes 73736 | tf_op jit(solution)/shard_map/ppermute | solution.py:615
  35.4 5.2 %collective-permute-start.12 = (f32[32,128]{1,0:T(8,128)S(1)}, f32[32,128]{1,0:T(8,128)S(1)}, u32[]{:S(2)}, u32[]{:S(2)}) collective-permute-start(f32[32,128]{1,0:T(8,128)S(1)} %get-tuple-element.151), channel_id=1, source_target_pairs={{0,64},{16,80},{32,96},{48,112},{64,0},{80,16},{96,32},{112,48},{1... | collective-permute-start | bytes 49160 | tf_op jit(solution)/shard_map/ppermute | solution.py:615
  38.5 3.7 %collective-permute-start.13 = (f32[32,128]{1,0:T(8,128)S(1)}, f32[32,128]{1,0:T(8,128)S(1)}, u32[]{:S(2)}, u32[]{:S(2)}) collective-permute-start(f32[32,128]{1,0:T(8,128)S(1)} %get-tuple-element.152), channel_id=1, source_target_pairs={{0,96},{16,112},{32,0},{48,16},{64,32},{80,48},{96,64},{112,80},{1... | collective-permute-start | bytes 49160 | tf_op jit(solution)/shard_map/ppermute | solution.py:615
  43.1 12.6 %all-to-all-start = ((f32[16,16,128]{2,1,0:T(8,128)}), f32[16,16,128]{2,1,0:T(8,128)S(1)}, u32[]{:S(2)}, u32[]{:S(2)}) async-start(f32[16,16,128]{2,1,0:T(8,128)} %get-tuple-element.171), calls=%async_computation | async-start | bytes 262144 | tf_op jit(solution)/shard_map/all_to_all | solution.py:629

commit v6 on v4

--- a/solution.py
+++ b/solution.py
@@ -19,7 +19,7 @@
 C_CODE, C_HALO, C_COEF, C_ALL = 256, 264, 296, 344
 Z_CODE, Z_COEF, Z_HALO = 64, 72, 120
 X_CODE, X_BLOCK, X_HALO = 64, 72, 152
-Y_CODE, Y_BLOCK, Y_HALO = 64, 96, 176
+Y_CODE, Y_BLOCK, Y_HALO = 64, 72, 152
 HALO = (0, 32, 0, 16)
 Z_ROWS = (0, 16, 0, 16)
 R4 = 16
@@ -384,13 +384,16 @@
         al = terms[k][0] + h_o[k] * al
         ga = terms[3 - k][1] + hr_o[3 - k] * ga
         link = link * h_o[k]
+    code = own[X_CODE:X_CODE + 8, :]
+    for k in range(1, 4):
+        code = code + pltpu.roll(srcs[k][X_CODE:X_CODE + 8, :], 32 * k, 1)
     for d, ref in enumerate((own_o, my1, my2, my3)):
+        ref[Y_CODE:Y_CODE + 8, :] = code
         y = (to + d) & 3
         for k, src in enumerate(srcs):
             for r in range(2):
                 row = pl.multiple_of((r * 4 + y) * 8, 8)
                 ref[(k * 2 + r) * 8:(k * 2 + r) * 8 + 8, :] = src[pl.ds(row, 8), :]
-            ref[Y_CODE + k * 8:Y_CODE + k * 8 + 8, :] = src[X_CODE:X_CODE + 8, :]
         for f, face in enumerate((ga, al, de_o[0], link, be_o[4])):
             ref[Y_BLOCK + 16 * f:Y_BLOCK + 16 * f + 16, :] = face
     my1[Y_HALO:Y_HALO + 32, :] = r1[X_HALO:X_HALO + 32, :]
@@ -437,14 +440,16 @@
     hx_low = jnp.where(gy > 0, low[0:16], 0.0)
     ez_high = jnp.where(gy < GY - 1, high, 0.0)
     srcs = (own, s1, s2, s3)
-    codes = jnp.concatenate([r[Y_CODE:Y_CODE + 32, :] for r in srcs], axis=0).astype(BF16)
+    tile = iota((8, NZ), 1) >> 5
+    codes = jnp.concatenate(
+        [jnp.where(tile == k, ref[Y_CODE:Y_CODE + 8, :], 0.0) for k in range(4) for ref in srcs], axis=0).astype(BF16)
     inj = None
     for r in range(2):
-        lane = (iota((8, 128), 1) == r * GY + gy).astype(BF16)
+        lane = ((iota((8, 128), 1) & 31) == r * GY + gy).astype(BF16)
         code_row = lax.dot_general(lane, codes, (((1,), (1,)), ((), ())), preferred_element_type=F32)[0:1]
         land = ((iota((CELLS, 128), 0) + 1).astype(F32) == code_row).astype(BF16)
         vals = jnp.concatenate(
-            [ref[(k * 2 + r) * 8:(k * 2 + r) * 8 + 8, :] for ref in srcs for k in range(4)], axis=0)
+            [ref[(k * 2 + r) * 8:(k * 2 + r) * 8 + 8, :] for k in range(4) for ref in srcs], axis=0)
         part = split_dot(land, vals)
         inj = part if inj is None else inj + part
     inj_o[...] = inj

time: 56.8 us -> 56.7 us (level)
  no operation moved by 1% of the time
where the time goes in v6:
time: 56.7 us; the launch traced here: 56.4 us
  starting transfers between devices  25.7 us (45%)
  waiting for transfers between devices  15.9 us (28%)
  Pallas kernels  12 us (21%)
  local copies, waits for them, and re-layouts  1.99 us (4%)
  between operations  0.74 us (1%)
    pallas_call x12, Pallas kernels, call(): pl.pallas_call(kernel, out_shape=[jax.ShapeDtypeStruct(s, F32) for s in s...  12 us
    ppermute x6, starting transfers between devices, ring_z(): return lax.ppermute(message, 'gx', pairs)  10.5 us
    ppermute x3, starting transfers between devices, ring_y(): return lax.ppermute(message, 'gy', pairs)  5.29 us
    ppermute x3, starting transfers between devices, ring_x(): return lax.ppermute(message, 'gy', pairs)  5.12 us
    all_to_all x1, starting transfers between devices, exchange(): lax.all_to_all(message, axis, split_axis=0, concat_axis=0, tiled=True)  4.61 us
    ppermute x6, waiting for transfers between devices, ring_z(): return lax.ppermute(message, 'gx', pairs)  4.52 us
    all_to_all x1, waiting for transfers between devices, exchange(): lax.all_to_all(message, axis, split_axis=0, concat_axis=0, tiled=True)  4.43 us
    ppermute x3, waiting for transfers between devices, ring_y(): return lax.ppermute(message, 'gy', pairs)  2.97 us
  transfers between devices with their start and end apart: 15, of which 8 were waited for; matrix products, arithmetic and copies ran while one was open for 0% of the time, Pallas kernels for 13%

profile of v6, /device:TPU:0, one launch (start us, length us, event | category | flops | bytes accessed | tf_op | source)
XLA Modules:
  0.0 56.4 jit_solution(9864157716677727120)
XLA Ops:
  0.6 1.7 %k1.1 = (f32[344,128]{1,0:T(8,128)S(1)}, f32[256,128]{1,0:T(8,128)S(1)}, f32[256,128]{1,0:T(8,128)S(1)}, f32[16,16,128]{2,1,0:T(8,128)S(1)}, f32[16,16,128]{2,1,0:T(8,128)S(1)}) custom-call(f32[3,256,128]{2,1,0:T(8,128)} %bitcast.9, f32[3,256,128]{2,1,0:T(8,128)} %bitcast.13, s32[256,128]{1,0:T(8,128)} %bitcast.19, f32[8]{0:T(128)} %perm_h.1, f32[8]{0:T(128)} %cond_h.1, ...), custom_call_target="tpu_custom_call" | custom-call | tf_op jit(solution)/shard_map/k1/pallas_call | solution.py:599
  2.4 1.4 %collective-permute-done.rc = f32[344,128]{1,0:T(8,128)S(1)} collective-permute-done((f32[344,128]{1,0:T(8,128)S(1)}, f32[344,128]{1,0:T(8,128)S(1)}, u32[]{:S(2)}, u32[]{:S(2)}) %collective-permute-start) | collective-permute-done | bytes 176160 | tf_op jit(solution)/shard_map/ppermute | solution.py:612
  3.8 2.1 %collective-permute-start.1 = (f32[136,128]{1,0:T(8,128)S(1)}, f32[136,128]{1,0:T(8,128)S(1)}, u32[]{:S(2)}, u32[]{:S(2)}) collective-permute-start(f32[136,128]{1,0:T(8,128)S(1)} %get-tuple-element.97), channel_id=1, source_target_pairs={{0,32},{16,48},{32,64},{48,80},{64,96},{80,112},{96,0},{112,16},{1... | collective-permute-start | bytes 208904 | tf_op jit(solution)/shard_map/ppermute | solution.py:617
  5.9 2.2 %collective-permute-start.3 = (f32[136,128]{1,0:T(8,128)S(1)}, f32[136,128]{1,0:T(8,128)S(1)}, u32[]{:S(2)}, u32[]{:S(2)}) collective-permute-start(f32[136,128]{1,0:T(8,128)S(1)} %get-tuple-element.99), channel_id=1, source_target_pairs={{0,96},{16,112},{32,0},{48,16},{64,32},{80,48},{96,64},{112,80},{1... | collective-permute-start | bytes 208904 | tf_op jit(solution)/shard_map/ppermute | solution.py:617
  8.1 1.8 %collective-permute-start.2 = (f32[120,128]{1,0:T(8,128)S(1)}, f32[120,128]{1,0:T(8,128)S(1)}, u32[]{:S(2)}, u32[]{:S(2)}) collective-permute-start(f32[120,128]{1,0:T(8,128)S(1)} %get-tuple-element.98), channel_id=1, source_target_pairs={{0,64},{16,80},{32,96},{48,112},{64,0},{80,16},{96,32},{112,48},{1... | collective-permute-start | bytes 184328 | tf_op jit(solution)/shard_map/ppermute | solution.py:617
  9.9 1.0 %copy-done = f32[3,16,16,128]{3,2,1,0:T(8,128)S(1)} copy-done((f32[3,16,16,128]{3,2,1,0:T(8,128)S(1)}, f32[3,16,16,128]{3,2,1,0:T(8,128)}, u32[]{:S(2)}) %copy-start) | copy-done | bytes 393240
  10.9 1.0 %copy-done.1 = f32[3,16,16,128]{3,2,1,0:T(8,128)S(1)} copy-done((f32[3,16,16,128]{3,2,1,0:T(8,128)S(1)}, f32[3,16,16,128]{3,2,1,0:T(8,128)}, u32[]{:S(2)}) %copy-start.1) | copy-done | bytes 393240
  11.9 0.2 k1b.1
  12.0 1.8 %collective-permute-done.2.z2 = f32[120,128]{1,0:T(8,128)S(1)} collective-permute-done((f32[120,128]{1,0:T(8,128)S(1)}, f32[120,128]{1,0:T(8,128)S(1)}, u32[]{:S(2)}, u32[]{:S(2)}) %collective-permute-start.2) | collective-permute-done | bytes 61472 | tf_op jit(solution)/shard_map/ppermute | solution.py:617
  13.8 0.3 k2.1
  14.1 1.6 %collective-permute-start.4 = (f32[184,128]{1,0:T(8,128)S(1)}, f32[184,128]{1,0:T(8,128)S(1)}, u32[]{:S(2)}, u32[]{:S(2)}) collective-permute-start(f32[184,128]{1,0:T(8,128)S(1)} %get-tuple-element.110), channel_id=1, source_target_pairs={{0,1},{1,2},{2,3},{3,0},{4,5},{5,6},{6,7},{7,4},{8,9},{9,10},{10,1... | collective-permute-start | bytes 282632 | tf_op jit(solution)/shard_map/ppermute | solution.py:622
  15.7 1.7 %collective-permute-start.6 = (f32[168,128]{1,0:T(8,128)S(1)}, f32[168,128]{1,0:T(8,128)S(1)}, u32[]{:S(2)}, u32[]{:S(2)}) collective-permute-start(f32[168,128]{1,0:T(8,128)S(1)} %get-tuple-element.112), channel_id=1, source_target_pairs={{0,3},{1,0},{2,1},{3,2},{4,7},{5,4},{6,5},{7,6},{8,11},{9,8},{10,9... | collective-permute-start | bytes 258056 | tf_op jit(solution)/shard_map/ppermute | solution.py:622
  17.4 1.8 %collective-permute-start.5 = (f32[152,128]{1,0:T(8,128)S(1)}, f32[152,128]{1,0:T(8,128)S(1)}, u32[]{:S(2)}, u32[]{:S(2)}) collective-permute-start(f32[152,128]{1,0:T(8,128)S(1)} %get-tuple-element.111), channel_id=1, source_target_pairs={{0,2},{1,3},{2,0},{3,1},{4,6},{5,7},{6,4},{7,5},{8,10},{9,11},{10,... | collective-permute-start | bytes 233480 | tf_op jit(solution)/shard_map/ppermute | solution.py:622
  19.2 2.7 %k2a.1 = (f32[256,128]{1,0:T(8,128)S(1)}, f32[256,128]{1,0:T(8,128)S(1)}, f32[256,128]{1,0:T(8,128)S(1)}, f32[256,128]{1,0:T(8,128)S(1)}, f32[15,256,128]{2,1,0:T(8,128)S(1)}) custom-call(f32[3,256,128]{2,1,0:T(8,128)S(1)} %bitcast.12, f32[3,256,128]{2,1,0:T(8,128)S(1)} %bitcast.16, f32[256,128]{1,0:T(8,128)S(1)} %get-tuple-element.117.w, ...), custom_call_target="tpu_custom_call" | custom-call | tf_op jit(solution)/shard_map/k2a/pallas_call | solution.py:599
  22.0 1.4 %collective-permute-done.5.r2 = f32[152,128]{1,0:T(8,128)S(1)} collective-permute-done((f32[152,128]{1,0:T(8,128)S(1)}, f32[152,128]{1,0:T(8,128)S(1)}, u32[]{:S(2)}, u32[]{:S(2)}) %collective-permute-start.5) | collective-permute-done | bytes 77856 | tf_op jit(solution)/shard_map/ppermute | solution.py:622
  23.4 1.6 %collective-permute-start.7 = (f32[184,128]{1,0:T(8,128)S(1)}, f32[184,128]{1,0:T(8,128)S(1)}, u32[]{:S(2)}, u32[]{:S(2)}) collective-permute-start(f32[184,128]{1,0:T(8,128)S(1)} %get-tuple-element.119), channel_id=1, source_target_pairs={{0,4},{1,5},{2,6},{3,7},{4,8},{5,9},{6,10},{7,11},{8,12},{9,13},{1... | collective-permute-start | bytes 282632 | tf_op jit(solution)/shard_map/ppermute | solution.py:627
  25.1 1.7 %collective-permute-start.9 = (f32[168,128]{1,0:T(8,128)S(1)}, f32[168,128]{1,0:T(8,128)S(1)}, u32[]{:S(2)}, u32[]{:S(2)}) collective-permute-start(f32[168,128]{1,0:T(8,128)S(1)} %get-tuple-element.121), channel_id=1, source_target_pairs={{0,12},{1,13},{2,14},{3,15},{4,0},{5,1},{6,2},{7,3},{8,4},{9,5},{1... | collective-permute-start | bytes 258056 | tf_op jit(solution)/shard_map/ppermute | solution.py:627
  26.7 2.0 %collective-permute-start.8 = (f32[152,128]{1,0:T(8,128)S(1)}, f32[152,128]{1,0:T(8,128)S(1)}, u32[]{:S(2)}, u32[]{:S(2)}) collective-permute-start(f32[152,128]{1,0:T(8,128)S(1)} %get-tuple-element.120), channel_id=1, source_target_pairs={{0,8},{1,9},{2,10},{3,11},{4,12},{5,13},{6,14},{7,15},{8,0},{9,1},... | collective-permute-start | bytes 233480 | tf_op jit(solution)/shard_map/ppermute | solution.py:627
  28.7 0.9 %k2b.1 = (f32[256,128]{1,0:T(8,128)S(1)}, f32[256,128]{1,0:T(8,128)S(1)}) custom-call(f32[256,128]{1,0:T(8,128)S(1)} %get-tuple-element.101.v, f32[256,128]{1,0:T(8,128)S(1)} %get-tuple-element.132.hxp, f32[256,128]{1,0:T(8,128)S(1)} %get-tuple-element.133.dy1, f32[15,256,128]{2,1,0:T(8,128)S(1)} %get-tuple-element.134.zf), custom_call_target="tpu_custom_call" | custom-call | tf_op jit(solution)/shard_map/k2b/pallas_call | solution.py:599
  29.7 3.0 %collective-permute-done.8.s2 = f32[152,128]{1,0:T(8,128)S(1)} collective-permute-done((f32[152,128]{1,0:T(8,128)S(1)}, f32[152,128]{1,0:T(8,128)S(1)}, u32[]{:S(2)}, u32[]{:S(2)}) %collective-permute-start.8) | collective-permute-done | bytes 77856 | tf_op jit(solution)/shard_map/ppermute | solution.py:627
  32.6 0.9 %k3.1 = (f32[80,128]{1,0:T(8,128)S(1)}, f32[4,16,128]{2,1,0:T(8,128)S(1)}, f32[4,16,128]{2,1,0:T(8,128)S(1)}, f32[5,16,128]{2,1,0:T(8,128)S(1)}, f32[5,16,128]{2...) custom-call(f32[152,128]{1,0:T(8,128)S(1)} %get-tuple-element.113.ow, ...), custom_call_target="tpu_custom_call" | custom-call | tf_op jit(solution)/shard_map/k3/pallas_call | solution.py:599
  33.6 1.2 %collective-permute-done.10.rc = f32[80,128]{1,0:T(8,128)S(1)} collective-permute-done((f32[80,128]{1,0:T(8,128)S(1)}, f32[80,128]{1,0:T(8,128)S(1)}, u32[]{:S(2)}, u32[]{:S(2)}) %collective-permute-start.10) | collective-permute-done | bytes 40992 | tf_op jit(solution)/shard_map/ppermute | solution.py:612
  34.8 0.4 collective-permute-start.11
  35.2 3.1 %collective-permute-start.12 = (f32[32,128]{1,0:T(8,128)S(1)}, f32[32,128]{1,0:T(8,128)S(1)}, u32[]{:S(2)}, u32[]{:S(2)}) collective-permute-start(f32[32,128]{1,0:T(8,128)S(1)} %get-tuple-element.147), channel_id=1, source_target_pairs={{0,64},{16,80},{32,96},{48,112},{64,0},{80,16},{96,32},{112,48},{1... | collective-permute-start | bytes 49160 | tf_op jit(solution)/shard_map/ppermute | solution.py:617
  38.3 1.0 %collective-permute-start.13 = (f32[32,128]{1,0:T(8,128)S(1)}, f32[32,128]{1,0:T(8,128)S(1)}, u32[]{:S(2)}, u32[]{:S(2)}) collective-permute-start(f32[32,128]{1,0:T(8,128)S(1)} %get-tuple-element.148), channel_id=1, source_target_pairs={{0,96},{16,112},{32,0},{48,16},{64,32},{80,48},{96,64},{112,80},{1... | collective-permute-start | bytes 49160 | tf_op jit(solution)/shard_map/ppermute | solution.py:617
  39.3 1.1 %collective-permute-done.12.z2 = f32[32,128]{1,0:T(8,128)S(1)} collective-permute-done((f32[32,128]{1,0:T(8,128)S(1)}, f32[32,128]{1,0:T(8,128)S(1)}, u32[]{:S(2)}, u32[]{:S(2)}) %collective-permute-start.12) | collective-permute-done | bytes 16416 | tf_op jit(solution)/shard_map/ppermute | solution.py:617
  40.5 1.6 %collective-permute-done.13.z3 = f32[32,128]{1,0:T(8,128)S(1)} collective-permute-done((f32[32,128]{1,0:T(8,128)S(1)}, f32[32,128]{1,0:T(8,128)S(1)}, u32[]{:S(2)}, u32[]{:S(2)}) %collective-permute-start.13) | collective-permute-done | bytes 16416 | tf_op jit(solution)/shard_map/ppermute | solution.py:617
  42.1 0.9 %k4.1 = (f32[16,16,128]{2,1,0:T(8,128)}, f32[256,128]{1,0:T(8,128)S(1)}, f32[256,128]{1,0:T(8,128)S(1)}, f32[2,16,128]{2,1,0:T(8,128)S(1)}) custom-call(f32[80,128]{1,0:T(8,128)S(1)} %get-tuple-element.137.own, f32[80,128]{1,0:T(8,128)S(1)} %collective-permute-done.10.rc, f32[48,128]{1,0:T(8,128)S(1)} %collective-permute-done.11.z1, ...), custom_call_target="tpu_custom_call" | custom-call | tf_op jit(solution)/shard_map/k4/pallas_call | solution.py:599
  42.9 4.6 %all-to-all-start = ((f32[16,16,128]{2,1,0:T(8,128)}), f32[16,16,128]{2,1,0:T(8,128)S(1)}, u32[]{:S(2)}, u32[]{:S(2)}) async-start(f32[16,16,128]{2,1,0:T(8,128)} %get-tuple-element.167), calls=%async_computation | async-start | bytes 262144 | tf_op jit(solution)/shard_map/all_to_all | solution.py:631
  47.5 3.6 %k4b.1 = (f32[3,256,128]{2,1,0:T(8,128)}, f32[3,256,128]{2,1,0:T(8,128)}) custom-call(f32[80,128]{1,0:T(8,128)S(1)} %get-tuple-element.137.own, f32[80,128]{1,0:T(8,128)S(1)} %collective-permute-done.10.rc, f32[48,128]{1,0:T(8,128)S(1)} %collective-permute-done.11.z1, f32[32,128]{1,0:T(8,128)S(1)} %collective-permute-done.12.z2, ...), custom_call_target="tpu_custom_call" | custom-call | tf_op jit(solution)/shard_map/k4b/pallas_call | solution.py:599
  51.1 4.4 %all-to-all-done.m4 = f32[16,16,128]{2,1,0:T(8,128)S(1)} async-done(((f32[16,16,128]{2,1,0:T(8,128)}), f32[16,16,128]{2,1,0:T(8,128)S(1)}, u32[]{:S(2)}, u32[]{:S(2)}) %all-to-all-start) | async-done | bytes 131104 | tf_op jit(solution)/shard_map/all_to_all | solution.py:631
  55.5 0.8 %k5.1 = (f32[3,256,128]{2,1,0:T(8,128)}, f32[3,256,128]{2,1,0:T(8,128)}) custom-call(f32[16,16,128]{2,1,0:T(8,128)S(1)} %all-to-all-done.m4, f32[2,16,128]{2,1,0:T(8,128)S(1)} %get-tuple-element.168.own, f32[256,128]{1,0:T(8,128)S(1)} %get-tuple-element.169.dz2, ...), custom_call_target="tpu_custom_call", output_to_operand_aliasing={{0}: (11, {}), {1}: (12, {})} | custom-call | tf_op jit(solution)/shard_map/k5/pallas_call | solution.py:599
  (14 shorter events, 0.3 us)
Async XLA Ops:
  2.3 1.5 %collective-permute-start = (f32[344,128]{1,0:T(8,128)S(1)}, f32[344,128]{1,0:T(8,128)S(1)}, u32[]{:S(2)}, u32[]{:S(2)}) collective-permute-start(f32[344,128]{1,0:T(8,128)S(1)} %get-tuple-element.91.own), channel_id=1, source_target_pairs={{0,16},{16,0},{32,48},{48,32},{64,80},{80,64},{96,112},{112,96},{1... | collective-permute-start | bytes 528392 | tf_op jit(solution)/shard_map/ppermute | solution.py:612
  3.8 10.0 %collective-permute-start.1 = (f32[136,128]{1,0:T(8,128)S(1)}, f32[136,128]{1,0:T(8,128)S(1)}, u32[]{:S(2)}, u32[]{:S(2)}) collective-permute-start(f32[136,128]{1,0:T(8,128)S(1)} %get-tuple-element.97), channel_id=1, source_target_pairs={{0,32},{16,48},{32,64},{48,80},{64,96},{80,112},{96,0},{112,16},{1... | collective-permute-start | bytes 208904 | tf_op jit(solution)/shard_map/ppermute | solution.py:617
  5.9 7.9 %collective-permute-start.3 = (f32[136,128]{1,0:T(8,128)S(1)}, f32[136,128]{1,0:T(8,128)S(1)}, u32[]{:S(2)}, u32[]{:S(2)}) collective-permute-start(f32[136,128]{1,0:T(8,128)S(1)} %get-tuple-element.99), channel_id=1, source_target_pairs={{0,96},{16,112},{32,0},{48,16},{64,32},{80,48},{96,64},{112,80},{1... | collective-permute-start | bytes 208904 | tf_op jit(solution)/shard_map/ppermute | solution.py:617
  8.1 5.7 %collective-permute-start.2 = (f32[120,128]{1,0:T(8,128)S(1)}, f32[120,128]{1,0:T(8,128)S(1)}, u32[]{:S(2)}, u32[]{:S(2)}) collective-permute-start(f32[120,128]{1,0:T(8,128)S(1)} %get-tuple-element.98), channel_id=1, source_target_pairs={{0,64},{16,80},{32,96},{48,112},{64,0},{80,16},{96,32},{112,48},{1... | collective-permute-start | bytes 184328 | tf_op jit(solution)/shard_map/ppermute | solution.py:617
  9.9 1.0 %copy-start = (f32[3,16,16,128]{3,2,1,0:T(8,128)S(1)}, f32[3,16,16,128]{3,2,1,0:T(8,128)}, u32[]{:S(2)}) copy-start(f32[3,16,16,128]{3,2,1,0:T(8,128)} %param.9) | copy-start | bytes 1179652
  10.9 1.0 %copy-start.1 = (f32[3,16,16,128]{3,2,1,0:T(8,128)S(1)}, f32[3,16,16,128]{3,2,1,0:T(8,128)}, u32[]{:S(2)}) copy-start(f32[3,16,16,128]{3,2,1,0:T(8,128)} %param.10) | copy-start | bytes 1179652
  14.1 9.2 %collective-permute-start.4 = (f32[184,128]{1,0:T(8,128)S(1)}, f32[184,128]{1,0:T(8,128)S(1)}, u32[]{:S(2)}, u32[]{:S(2)}) collective-permute-start(f32[184,128]{1,0:T(8,128)S(1)} %get-tuple-element.110), channel_id=1, source_target_pairs={{0,1},{1,2},{2,3},{3,0},{4,5},{5,6},{6,7},{7,4},{8,9},{9,10},{10,1... | collective-permute-start | bytes 282632 | tf_op jit(solution)/shard_map/ppermute | solution.py:622
  15.7 7.7 %collective-permute-start.6 = (f32[168,128]{1,0:T(8,128)S(1)}, f32[168,128]{1,0:T(8,128)S(1)}, u32[]{:S(2)}, u32[]{:S(2)}) collective-permute-start(f32[168,128]{1,0:T(8,128)S(1)} %get-tuple-element.112), channel_id=1, source_target_pairs={{0,3},{1,0},{2,1},{3,2},{4,7},{5,4},{6,5},{7,6},{8,11},{9,8},{10,9... | collective-permute-start | bytes 258056 | tf_op jit(solution)/shard_map/ppermute | solution.py:622
  17.4 5.9 %collective-permute-start.5 = (f32[152,128]{1,0:T(8,128)S(1)}, f32[152,128]{1,0:T(8,128)S(1)}, u32[]{:S(2)}, u32[]{:S(2)}) collective-permute-start(f32[152,128]{1,0:T(8,128)S(1)} %get-tuple-element.111), channel_id=1, source_target_pairs={{0,2},{1,3},{2,0},{3,1},{4,6},{5,7},{6,4},{7,5},{8,10},{9,11},{10,... | collective-permute-start | bytes 233480 | tf_op jit(solution)/shard_map/ppermute | solution.py:622
  23.4 9.2 %collective-permute-start.7 = (f32[184,128]{1,0:T(8,128)S(1)}, f32[184,128]{1,0:T(8,128)S(1)}, u32[]{:S(2)}, u32[]{:S(2)}) collective-permute-start(f32[184,128]{1,0:T(8,128)S(1)} %get-tuple-element.119), channel_id=1, source_target_pairs={{0,4},{1,5},{2,6},{3,7},{4,8},{5,9},{6,10},{7,11},{8,12},{9,13},{1... | collective-permute-start | bytes 282632 | tf_op jit(solution)/shard_map/ppermute | solution.py:627
  25.1 7.6 %collective-permute-start.9 = (f32[168,128]{1,0:T(8,128)S(1)}, f32[168,128]{1,0:T(8,128)S(1)}, u32[]{:S(2)}, u32[]{:S(2)}) collective-permute-start(f32[168,128]{1,0:T(8,128)S(1)} %get-tuple-element.121), channel_id=1, source_target_pairs={{0,12},{1,13},{2,14},{3,15},{4,0},{5,1},{6,2},{7,3},{8,4},{9,5},{1... | collective-permute-start | bytes 258056 | tf_op jit(solution)/shard_map/ppermute | solution.py:627
  26.7 5.9 %collective-permute-start.8 = (f32[152,128]{1,0:T(8,128)S(1)}, f32[152,128]{1,0:T(8,128)S(1)}, u32[]{:S(2)}, u32[]{:S(2)}) collective-permute-start(f32[152,128]{1,0:T(8,128)S(1)} %get-tuple-element.120), channel_id=1, source_target_pairs={{0,8},{1,9},{2,10},{3,11},{4,12},{5,13},{6,14},{7,15},{8,0},{9,1},... | collective-permute-start | bytes 233480 | tf_op jit(solution)/shard_map/ppermute | solution.py:627
  33.5 1.3 %collective-permute-start.10 = (f32[80,128]{1,0:T(8,128)S(1)}, f32[80,128]{1,0:T(8,128)S(1)}, u32[]{:S(2)}, u32[]{:S(2)}) collective-permute-start(f32[80,128]{1,0:T(8,128)S(1)} %get-tuple-element.137.own), channel_id=1, source_target_pairs={{0,16},{16,0},{32,48},{48,32},{64,80},{80,64},{96,112},{112,96},{1... | collective-permute-start | bytes 122888 | tf_op jit(solution)/shard_map/ppermute | solution.py:612
  34.8 7.2 %collective-permute-start.11 = (f32[48,128]{1,0:T(8,128)S(1)}, f32[48,128]{1,0:T(8,128)S(1)}, u32[]{:S(2)}, u32[]{:S(2)}) collective-permute-start(f32[48,128]{1,0:T(8,128)S(1)} %get-tuple-element.146), channel_id=1, source_target_pairs={{0,32},{16,48},{32,64},{48,80},{64,96},{80,112},{96,0},{112,16},{1... | collective-permute-start | bytes 73736 | tf_op jit(solution)/shard_map/ppermute | solution.py:617
  35.2 5.2 %collective-permute-start.12 = (f32[32,128]{1,0:T(8,128)S(1)}, f32[32,128]{1,0:T(8,128)S(1)}, u32[]{:S(2)}, u32[]{:S(2)}) collective-permute-start(f32[32,128]{1,0:T(8,128)S(1)} %get-tuple-element.147), channel_id=1, source_target_pairs={{0,64},{16,80},{32,96},{48,112},{64,0},{80,16},{96,32},{112,48},{1... | collective-permute-start | bytes 49160 | tf_op jit(solution)/shard_map/ppermute | solution.py:617
  38.3 3.7 %collective-permute-start.13 = (f32[32,128]{1,0:T(8,128)S(1)}, f32[32,128]{1,0:T(8,128)S(1)}, u32[]{:S(2)}, u32[]{:S(2)}) collective-permute-start(f32[32,128]{1,0:T(8,128)S(1)} %get-tuple-element.148), channel_id=1, source_target_pairs={{0,96},{16,112},{32,0},{48,16},{64,32},{80,48},{96,64},{112,80},{1... | collective-permute-start | bytes 49160 | tf_op jit(solution)/shard_map/ppermute | solution.py:617
  42.9 12.6 %all-to-all-start = ((f32[16,16,128]{2,1,0:T(8,128)}), f32[16,16,128]{2,1,0:T(8,128)S(1)}, u32[]{:S(2)}, u32[]{:S(2)}) async-start(f32[16,16,128]{2,1,0:T(8,128)} %get-tuple-element.167), calls=%async_computation | async-start | bytes 262144 | tf_op jit(solution)/shard_map/all_to_all | solution.py:631

commit v7 on v5

--- a/solution.py
+++ b/solution.py
@@ -19,7 +19,7 @@
 C_CODE, C_HALO, C_COEF, C_ALL = 256, 264, 296, 344
 Z_CODE, Z_COEF, Z_HALO = 64, 72, 120
 X_CODE, X_BLOCK, X_HALO = 64, 72, 152
-Y_CODE, Y_BLOCK, Y_HALO = 64, 96, 176
+Y_CODE, Y_BLOCK, Y_HALO = 64, 72, 152
 HALO = (0, 32, 0, 16)
 Z_ROWS = (0, 16, 0, 16)
 R4 = 16
@@ -387,13 +387,16 @@
         al = terms[k][0] + h_o[k] * al
         ga = terms[3 - k][1] + hr_o[3 - k] * ga
         link = link * h_o[k]
+    code = own[X_CODE:X_CODE + 8, :]
+    for k in range(1, 4):
+        code = code + pltpu.roll(srcs[k][X_CODE:X_CODE + 8, :], 32 * k, 1)
     for d, ref in enumerate((own_o, my1, my2, my3)):
+        ref[Y_CODE:Y_CODE + 8, :] = code
         y = (to + d) & 3
         for k, src in enumerate(srcs):
             for r in range(2):
                 row = pl.multiple_of((r * 4 + y) * 8, 8)
                 ref[(k * 2 + r) * 8:(k * 2 + r) * 8 + 8, :] = src[pl.ds(row, 8), :]
-            ref[Y_CODE + k * 8:Y_CODE + k * 8 + 8, :] = src[X_CODE:X_CODE + 8, :]
         for f, face in enumerate((ga, al, de_o[0], link, be_o[4])):
             ref[Y_BLOCK + 16 * f:Y_BLOCK + 16 * f + 16, :] = face
     my1[Y_HALO:Y_HALO + 32, :] = r1[X_HALO:X_HALO + 32, :]
@@ -440,14 +443,16 @@
     hx_low = jnp.where(gy > 0, low[0:16], 0.0)
     ez_high = jnp.where(gy < GY - 1, high, 0.0)
     srcs = (own, s1, s2, s3)
-    codes = jnp.concatenate([r[Y_CODE:Y_CODE + 32, :] for r in srcs], axis=0).astype(BF16)
+    tile = iota((8, NZ), 1) >> 5
+    codes = jnp.concatenate(
+        [jnp.where(tile == k, ref[Y_CODE:Y_CODE + 8, :], 0.0) for k in range(4) for ref in srcs], axis=0).astype(BF16)
     inj = None
     for r in range(2):
-        lane = (iota((8, 128), 1) == r * GY + gy).astype(BF16)
+        lane = ((iota((8, 128), 1) & 31) == r * GY + gy).astype(BF16)
         code_row = lax.dot_general(lane, codes, (((1,), (1,)), ((), ())), preferred_element_type=F32)[0:1]
         land = ((iota((CELLS, 128), 0) + 1).astype(F32) == code_row).astype(BF16)
         vals = jnp.concatenate(
-            [ref[(k * 2 + r) * 8:(k * 2 + r) * 8 + 8, :] for ref in srcs for k in range(4)], axis=0)
+            [ref[(k * 2 + r) * 8:(k * 2 + r) * 8 + 8, :] for k in range(4) for ref in srcs], axis=0)
         part = split_dot(land, vals)
         inj = part if inj is None else inj + part
     inj_o[...] = inj

time: 56.7 us -> 56.6 us (level)
  no operation moved by 1% of the time
where the time goes in v7:
time: 56.6 us; the launch traced here: 56.4 us
  starting transfers between devices  25.7 us (45%)
  waiting for transfers between devices  17.9 us (32%)
  Pallas kernels  12.1 us (21%)
  between operations  0.74 us (1%)
    pallas_call x12, Pallas kernels, call(): pl.pallas_call(kernel, out_shape=[jax.ShapeDtypeStruct(s, F32) for s in s...  12.1 us
    ppermute x6, starting transfers between devices, ring_z(): return lax.ppermute(message, 'gx', pairs)  10.5 us
    ppermute x6, waiting for transfers between devices, ring_z(): return lax.ppermute(message, 'gx', pairs)  6.51 us
    ppermute x3, starting transfers between devices, ring_y(): return lax.ppermute(message, 'gy', pairs)  5.29 us
    ppermute x3, starting transfers between devices, ring_x(): return lax.ppermute(message, 'gy', pairs)  5.12 us
    all_to_all x1, starting transfers between devices, exchange(): lax.all_to_all(message, axis, split_axis=0, concat_axis=0, tiled=True)  4.61 us
    all_to_all x1, waiting for transfers between devices, exchange(): lax.all_to_all(message, axis, split_axis=0, concat_axis=0, tiled=True)  4.43 us
    ppermute x3, waiting for transfers between devices, ring_y(): return lax.ppermute(message, 'gy', pairs)  2.97 us
  transfers between devices with their start and end apart: 15, of which 8 were waited for; matrix products, arithmetic and copies ran while one was open for 0% of the time, Pallas kernels for 13%

profile of v7, /device:TPU:0, one launch (start us, length us, event | category | flops | bytes accessed | tf_op | source)
XLA Modules:
  0.0 56.4 jit_solution(7168891477535087878)
XLA Ops:
  0.6 1.7 %k1.1 = (f32[344,128]{1,0:T(8,128)S(1)}, f32[256,128]{1,0:T(8,128)S(1)}, f32[256,128]{1,0:T(8,128)S(1)}, f32[16,16,128]{2,1,0:T(8,128)S(1)}, f32[16,16,128]{2,1,...) custom-call(f32[3,256,128]{2,1,0:T(8,128)} %bitcast.9, f32[3,256,128]{2,1,0:T(8,128)} %bitcast.10, ...), custom_call_target="tpu_custom_call" | custom-call | tf_op jit(solution)/shard_map/k1/pallas_call | solution.py:602
  2.3 0.1 collective-permute-start
  2.4 1.4 %collective-permute-done.rc = f32[344,128]{1,0:T(8,128)S(1)} collective-permute-done((f32[344,128]{1,0:T(8,128)S(1)}, f32[344,128]{1,0:T(8,128)S(1)}, u32[]{:S(2)}, u32[]{:S(2)}) %collective-permute-start) | collective-permute-done | bytes 176160 | tf_op jit(solution)/shard_map/ppermute | solution.py:615
  3.9 2.1 %collective-permute-start.1 = (f32[136,128]{1,0:T(8,128)S(1)}, f32[136,128]{1,0:T(8,128)S(1)}, u32[]{:S(2)}, u32[]{:S(2)}) collective-permute-start(f32[136,128]{1,0:T(8,128)S(1)} %get-tuple-element.99), channel_id=1, source_target_pairs={{0,32},{16,48},{32,64},{48,80},{64,96},{80,112},{96,0},{112,16},{1... | collective-permute-start | bytes 208904 | tf_op jit(solution)/shard_map/ppermute | solution.py:620
  5.9 2.2 %collective-permute-start.3 = (f32[136,128]{1,0:T(8,128)S(1)}, f32[136,128]{1,0:T(8,128)S(1)}, u32[]{:S(2)}, u32[]{:S(2)}) collective-permute-start(f32[136,128]{1,0:T(8,128)S(1)} %get-tuple-element.101), channel_id=1, source_target_pairs={{0,96},{16,112},{32,0},{48,16},{64,32},{80,48},{96,64},{112,80},{1... | collective-permute-start | bytes 208904 | tf_op jit(solution)/shard_map/ppermute | solution.py:620
  8.1 1.8 %collective-permute-start.2 = (f32[120,128]{1,0:T(8,128)S(1)}, f32[120,128]{1,0:T(8,128)S(1)}, u32[]{:S(2)}, u32[]{:S(2)}) collective-permute-start(f32[120,128]{1,0:T(8,128)S(1)} %get-tuple-element.100), channel_id=1, source_target_pairs={{0,64},{16,80},{32,96},{48,112},{64,0},{80,16},{96,32},{112,48},{1... | collective-permute-start | bytes 184328 | tf_op jit(solution)/shard_map/ppermute | solution.py:620
  9.9 0.2 k1b.1
  10.1 3.8 %collective-permute-done.2.z2 = f32[120,128]{1,0:T(8,128)S(1)} collective-permute-done((f32[120,128]{1,0:T(8,128)S(1)}, f32[120,128]{1,0:T(8,128)S(1)}, u32[]{:S(2)}, u32[]{:S(2)}) %collective-permute-start.2) | collective-permute-done | bytes 61472 | tf_op jit(solution)/shard_map/ppermute | solution.py:620
  13.9 0.3 k2.1
  14.2 1.6 %collective-permute-start.4 = (f32[184,128]{1,0:T(8,128)S(1)}, f32[184,128]{1,0:T(8,128)S(1)}, u32[]{:S(2)}, u32[]{:S(2)}) collective-permute-start(f32[184,128]{1,0:T(8,128)S(1)} %get-tuple-element.114), channel_id=1, source_target_pairs={{0,1},{1,2},{2,3},{3,0},{4,5},{5,6},{6,7},{7,4},{8,9},{9,10},{10,1... | collective-permute-start | bytes 282632 | tf_op jit(solution)/shard_map/ppermute | solution.py:625
  15.7 1.7 %collective-permute-start.6 = (f32[168,128]{1,0:T(8,128)S(1)}, f32[168,128]{1,0:T(8,128)S(1)}, u32[]{:S(2)}, u32[]{:S(2)}) collective-permute-start(f32[168,128]{1,0:T(8,128)S(1)} %get-tuple-element.116), channel_id=1, source_target_pairs={{0,3},{1,0},{2,1},{3,2},{4,7},{5,4},{6,5},{7,6},{8,11},{9,8},{10,9... | collective-permute-start | bytes 258056 | tf_op jit(solution)/shard_map/ppermute | solution.py:625
  17.5 1.8 %collective-permute-start.5 = (f32[152,128]{1,0:T(8,128)S(1)}, f32[152,128]{1,0:T(8,128)S(1)}, u32[]{:S(2)}, u32[]{:S(2)}) collective-permute-start(f32[152,128]{1,0:T(8,128)S(1)} %get-tuple-element.115), channel_id=1, source_target_pairs={{0,2},{1,3},{2,0},{3,1},{4,6},{5,7},{6,4},{7,5},{8,10},{9,11},{10,... | collective-permute-start | bytes 233480 | tf_op jit(solution)/shard_map/ppermute | solution.py:625
  19.3 2.7 %k2a.1 = (f32[256,128]{1,0:T(8,128)S(1)}, f32[256,128]{1,0:T(8,128)S(1)}, f32[256,128]{1,0:T(8,128)S(1)}, f32[256,128]{1,0:T(8,128)S(1)}, f32[15,256,128]{2,1,0:T(8,128)S(1)}) custom-call(f32[3,256,128]{2,1,0:T(8,128)S(1)} %get-tuple-element.103.e, f32[3,256,128]{2,1,0:T(8,128)S(1)} %get-tuple-element.104.h, f32[256,128]{1,0:T(8,128)S(1)} %get-tuple-element.121.w, ...), custom_call_target="tpu_custom_call" | custom-call | tf_op jit(solution)/shard_map/k2a/pallas_call | solution.py:602
  22.0 1.4 %collective-permute-done.5.r2 = f32[152,128]{1,0:T(8,128)S(1)} collective-permute-done((f32[152,128]{1,0:T(8,128)S(1)}, f32[152,128]{1,0:T(8,128)S(1)}, u32[]{:S(2)}, u32[]{:S(2)}) %collective-permute-start.5) | collective-permute-done | bytes 77856 | tf_op jit(solution)/shard_map/ppermute | solution.py:625
  23.4 0.1 k2c.1
  23.5 1.6 %collective-permute-start.7 = (f32[184,128]{1,0:T(8,128)S(1)}, f32[184,128]{1,0:T(8,128)S(1)}, u32[]{:S(2)}, u32[]{:S(2)}) collective-permute-start(f32[184,128]{1,0:T(8,128)S(1)} %get-tuple-element.123), channel_id=1, source_target_pairs={{0,4},{1,5},{2,6},{3,7},{4,8},{5,9},{6,10},{7,11},{8,12},{9,13},{1... | collective-permute-start | bytes 282632 | tf_op jit(solution)/shard_map/ppermute | solution.py:630
  25.1 1.7 %collective-permute-start.9 = (f32[168,128]{1,0:T(8,128)S(1)}, f32[168,128]{1,0:T(8,128)S(1)}, u32[]{:S(2)}, u32[]{:S(2)}) collective-permute-start(f32[168,128]{1,0:T(8,128)S(1)} %get-tuple-element.125), channel_id=1, source_target_pairs={{0,12},{1,13},{2,14},{3,15},{4,0},{5,1},{6,2},{7,3},{8,4},{9,5},{1... | collective-permute-start | bytes 258056 | tf_op jit(solution)/shard_map/ppermute | solution.py:630
  26.8 2.0 %collective-permute-start.8 = (f32[152,128]{1,0:T(8,128)S(1)}, f32[152,128]{1,0:T(8,128)S(1)}, u32[]{:S(2)}, u32[]{:S(2)}) collective-permute-start(f32[152,128]{1,0:T(8,128)S(1)} %get-tuple-element.124), channel_id=1, source_target_pairs={{0,8},{1,9},{2,10},{3,11},{4,12},{5,13},{6,14},{7,15},{8,0},{9,1},... | collective-permute-start | bytes 233480 | tf_op jit(solution)/shard_map/ppermute | solution.py:630
  28.8 0.9 %k2b.1 = (f32[256,128]{1,0:T(8,128)S(1)}, f32[256,128]{1,0:T(8,128)S(1)}) custom-call(f32[256,128]{1,0:T(8,128)S(1)} %get-tuple-element.105.v, f32[256,128]{1,0:T(8,128)S(1)} %get-tuple-element.136.hxp, f32[256,128]{1,0:T(8,128)S(1)} %get-tuple-element.137.dy1, f32[15,256,128]{2,1,0:T(8,128)S(1)} %get-tuple-element.138.zf), custom_call_target="tpu_custom_call" | custom-call | tf_op jit(solution)/shard_map/k2b/pallas_call | solution.py:602
  29.7 3.0 %collective-permute-done.8.s2 = f32[152,128]{1,0:T(8,128)S(1)} collective-permute-done((f32[152,128]{1,0:T(8,128)S(1)}, f32[152,128]{1,0:T(8,128)S(1)}, u32[]{:S(2)}, u32[]{:S(2)}) %collective-permute-start.8) | collective-permute-done | bytes 77856 | tf_op jit(solution)/shard_map/ppermute | solution.py:630
  32.7 0.9 %k3.1 = (f32[80,128]{1,0:T(8,128)S(1)}, f32[4,16,128]{2,1,0:T(8,128)S(1)}, f32[4,16,128]{2,1,0:T(8,128)S(1)}, f32[5,16,128]{2,1,0:T(8,128)S(1)}, f32[5,16,128]{2...) custom-call(f32[152,128]{1,0:T(8,128)S(1)} %get-tuple-element.117.ow, ...), custom_call_target="tpu_custom_call" | custom-call | tf_op jit(solution)/shard_map/k3/pallas_call | solution.py:602
  33.6 1.2 %collective-permute-done.10.rc = f32[80,128]{1,0:T(8,128)S(1)} collective-permute-done((f32[80,128]{1,0:T(8,128)S(1)}, f32[80,128]{1,0:T(8,128)S(1)}, u32[]{:S(2)}, u32[]{:S(2)}) %collective-permute-start.10) | collective-permute-done | bytes 40992 | tf_op jit(solution)/shard_map/ppermute | solution.py:615
  34.9 0.4 collective-permute-start.11
  35.3 3.1 %collective-permute-start.12 = (f32[32,128]{1,0:T(8,128)S(1)}, f32[32,128]{1,0:T(8,128)S(1)}, u32[]{:S(2)}, u32[]{:S(2)}) collective-permute-start(f32[32,128]{1,0:T(8,128)S(1)} %get-tuple-element.151), channel_id=1, source_target_pairs={{0,64},{16,80},{32,96},{48,112},{64,0},{80,16},{96,32},{112,48},{1... | collective-permute-start | bytes 49160 | tf_op jit(solution)/shard_map/ppermute | solution.py:620
  38.4 1.0 %collective-permute-start.13 = (f32[32,128]{1,0:T(8,128)S(1)}, f32[32,128]{1,0:T(8,128)S(1)}, u32[]{:S(2)}, u32[]{:S(2)}) collective-permute-start(f32[32,128]{1,0:T(8,128)S(1)} %get-tuple-element.152), channel_id=1, source_target_pairs={{0,96},{16,112},{32,0},{48,16},{64,32},{80,48},{96,64},{112,80},{1... | collective-permute-start | bytes 49160 | tf_op jit(solution)/shard_map/ppermute | solution.py:620
  39.4 1.1 %collective-permute-done.12.z2 = f32[32,128]{1,0:T(8,128)S(1)} collective-permute-done((f32[32,128]{1,0:T(8,128)S(1)}, f32[32,128]{1,0:T(8,128)S(1)}, u32[]{:S(2)}, u32[]{:S(2)}) %collective-permute-start.12) | collective-permute-done | bytes 16416 | tf_op jit(solution)/shard_map/ppermute | solution.py:620
  40.5 1.6 %collective-permute-done.13.z3 = f32[32,128]{1,0:T(8,128)S(1)} collective-permute-done((f32[32,128]{1,0:T(8,128)S(1)}, f32[32,128]{1,0:T(8,128)S(1)}, u32[]{:S(2)}, u32[]{:S(2)}) %collective-permute-start.13) | collective-permute-done | bytes 16416 | tf_op jit(solution)/shard_map/ppermute | solution.py:620
  42.1 0.9 %k4.1 = (f32[16,16,128]{2,1,0:T(8,128)}, f32[256,128]{1,0:T(8,128)S(1)}, f32[256,128]{1,0:T(8,128)S(1)}, f32[2,16,128]{2,1,0:T(8,128)S(1)}) custom-call(f32[80,128]{1,0:T(8,128)S(1)} %get-tuple-element.141.own, f32[80,128]{1,0:T(8,128)S(1)} %collective-permute-done.10.rc, f32[48,128]{1,0:T(8,128)S(1)} %collective-permute-done.11.z1, ...), custom_call_target="tpu_custom_call" | custom-call | tf_op jit(solution)/shard_map/k4/pallas_call | solution.py:602
  43.0 4.6 %all-to-all-start = ((f32[16,16,128]{2,1,0:T(8,128)}), f32[16,16,128]{2,1,0:T(8,128)S(1)}, u32[]{:S(2)}, u32[]{:S(2)}) async-start(f32[16,16,128]{2,1,0:T(8,128)} %get-tuple-element.171), calls=%async_computation | async-start | bytes 262144 | tf_op jit(solution)/shard_map/all_to_all | solution.py:634
  47.6 3.6 %k4b.1 = (f32[3,256,128]{2,1,0:T(8,128)}, f32[3,256,128]{2,1,0:T(8,128)}) custom-call(f32[80,128]{1,0:T(8,128)S(1)} %get-tuple-element.141.own, f32[80,128]{1,0:T(8,128)S(1)} %collective-permute-done.10.rc, f32[48,128]{1,0:T(8,128)S(1)} %collective-permute-done.11.z1, f32[32,128]{1,0:T(8,128)S(1)} %collective-permute-done.12.z2, ...), custom_call_target="tpu_custom_call" | custom-call | tf_op jit(solution)/shard_map/k4b/pallas_call | solution.py:602
  51.1 4.4 %all-to-all-done.m4 = f32[16,16,128]{2,1,0:T(8,128)S(1)} async-done(((f32[16,16,128]{2,1,0:T(8,128)}), f32[16,16,128]{2,1,0:T(8,128)S(1)}, u32[]{:S(2)}, u32[]{:S(2)}) %all-to-all-start) | async-done | bytes 131104 | tf_op jit(solution)/shard_map/all_to_all | solution.py:634
  55.6 0.8 %k5.1 = (f32[3,256,128]{2,1,0:T(8,128)}, f32[3,256,128]{2,1,0:T(8,128)}) custom-call(f32[16,16,128]{2,1,0:T(8,128)S(1)} %all-to-all-done.m4, f32[2,16,128]{2,1,0:T(8,128)S(1)} %get-tuple-element.172.own, f32[256,128]{1,0:T(8,128)S(1)} %get-tuple-element.173.dz2, ...), custom_call_target="tpu_custom_call", output_to_operand_aliasing={{0}: (11, {}), {1}: (12, {})} | custom-call | tf_op jit(solution)/shard_map/k5/pallas_call | solution.py:602
  (10 shorter events, 0.2 us)
Async XLA Ops:
  2.3 1.5 %collective-permute-start = (f32[344,128]{1,0:T(8,128)S(1)}, f32[344,128]{1,0:T(8,128)S(1)}, u32[]{:S(2)}, u32[]{:S(2)}) collective-permute-start(f32[344,128]{1,0:T(8,128)S(1)} %get-tuple-element.93.own), channel_id=1, source_target_pairs={{0,16},{16,0},{32,48},{48,32},{64,80},{80,64},{96,112},{112,96},{1... | collective-permute-start | bytes 528392 | tf_op jit(solution)/shard_map/ppermute | solution.py:615
  3.9 10.0 %collective-permute-start.1 = (f32[136,128]{1,0:T(8,128)S(1)}, f32[136,128]{1,0:T(8,128)S(1)}, u32[]{:S(2)}, u32[]{:S(2)}) collective-permute-start(f32[136,128]{1,0:T(8,128)S(1)} %get-tuple-element.99), channel_id=1, source_target_pairs={{0,32},{16,48},{32,64},{48,80},{64,96},{80,112},{96,0},{112,16},{1... | collective-permute-start | bytes 208904 | tf_op jit(solution)/shard_map/ppermute | solution.py:620
  5.9 7.9 %collective-permute-start.3 = (f32[136,128]{1,0:T(8,128)S(1)}, f32[136,128]{1,0:T(8,128)S(1)}, u32[]{:S(2)}, u32[]{:S(2)}) collective-permute-start(f32[136,128]{1,0:T(8,128)S(1)} %get-tuple-element.101), channel_id=1, source_target_pairs={{0,96},{16,112},{32,0},{48,16},{64,32},{80,48},{96,64},{112,80},{1... | collective-permute-start | bytes 208904 | tf_op jit(solution)/shard_map/ppermute | solution.py:620
  8.1 5.7 %collective-permute-start.2 = (f32[120,128]{1,0:T(8,128)S(1)}, f32[120,128]{1,0:T(8,128)S(1)}, u32[]{:S(2)}, u32[]{:S(2)}) collective-permute-start(f32[120,128]{1,0:T(8,128)S(1)} %get-tuple-element.100), channel_id=1, source_target_pairs={{0,64},{16,80},{32,96},{48,112},{64,0},{80,16},{96,32},{112,48},{1... | collective-permute-start | bytes 184328 | tf_op jit(solution)/shard_map/ppermute | solution.py:620
  14.2 9.2 %collective-permute-start.4 = (f32[184,128]{1,0:T(8,128)S(1)}, f32[184,128]{1,0:T(8,128)S(1)}, u32[]{:S(2)}, u32[]{:S(2)}) collective-permute-start(f32[184,128]{1,0:T(8,128)S(1)} %get-tuple-element.114), channel_id=1, source_target_pairs={{0,1},{1,2},{2,3},{3,0},{4,5},{5,6},{6,7},{7,4},{8,9},{9,10},{10,1... | collective-permute-start | bytes 282632 | tf_op jit(solution)/shard_map/ppermute | solution.py:625
  15.7 7.7 %collective-permute-start.6 = (f32[168,128]{1,0:T(8,128)S(1)}, f32[168,128]{1,0:T(8,128)S(1)}, u32[]{:S(2)}, u32[]{:S(2)}) collective-permute-start(f32[168,128]{1,0:T(8,128)S(1)} %get-tuple-element.116), channel_id=1, source_target_pairs={{0,3},{1,0},{2,1},{3,2},{4,7},{5,4},{6,5},{7,6},{8,11},{9,8},{10,9... | collective-permute-start | bytes 258056 | tf_op jit(solution)/shard_map/ppermute | solution.py:625
  17.5 5.9 %collective-permute-start.5 = (f32[152,128]{1,0:T(8,128)S(1)}, f32[152,128]{1,0:T(8,128)S(1)}, u32[]{:S(2)}, u32[]{:S(2)}) collective-permute-start(f32[152,128]{1,0:T(8,128)S(1)} %get-tuple-element.115), channel_id=1, source_target_pairs={{0,2},{1,3},{2,0},{3,1},{4,6},{5,7},{6,4},{7,5},{8,10},{9,11},{10,... | collective-permute-start | bytes 233480 | tf_op jit(solution)/shard_map/ppermute | solution.py:625
  23.5 9.2 %collective-permute-start.7 = (f32[184,128]{1,0:T(8,128)S(1)}, f32[184,128]{1,0:T(8,128)S(1)}, u32[]{:S(2)}, u32[]{:S(2)}) collective-permute-start(f32[184,128]{1,0:T(8,128)S(1)} %get-tuple-element.123), channel_id=1, source_target_pairs={{0,4},{1,5},{2,6},{3,7},{4,8},{5,9},{6,10},{7,11},{8,12},{9,13},{1... | collective-permute-start | bytes 282632 | tf_op jit(solution)/shard_map/ppermute | solution.py:630
  25.1 7.6 %collective-permute-start.9 = (f32[168,128]{1,0:T(8,128)S(1)}, f32[168,128]{1,0:T(8,128)S(1)}, u32[]{:S(2)}, u32[]{:S(2)}) collective-permute-start(f32[168,128]{1,0:T(8,128)S(1)} %get-tuple-element.125), channel_id=1, source_target_pairs={{0,12},{1,13},{2,14},{3,15},{4,0},{5,1},{6,2},{7,3},{8,4},{9,5},{1... | collective-permute-start | bytes 258056 | tf_op jit(solution)/shard_map/ppermute | solution.py:630
  26.8 5.9 %collective-permute-start.8 = (f32[152,128]{1,0:T(8,128)S(1)}, f32[152,128]{1,0:T(8,128)S(1)}, u32[]{:S(2)}, u32[]{:S(2)}) collective-permute-start(f32[152,128]{1,0:T(8,128)S(1)} %get-tuple-element.124), channel_id=1, source_target_pairs={{0,8},{1,9},{2,10},{3,11},{4,12},{5,13},{6,14},{7,15},{8,0},{9,1},... | collective-permute-start | bytes 233480 | tf_op jit(solution)/shard_map/ppermute | solution.py:630
  33.5 1.3 %collective-permute-start.10 = (f32[80,128]{1,0:T(8,128)S(1)}, f32[80,128]{1,0:T(8,128)S(1)}, u32[]{:S(2)}, u32[]{:S(2)}) collective-permute-start(f32[80,128]{1,0:T(8,128)S(1)} %get-tuple-element.141.own), channel_id=1, source_target_pairs={{0,16},{16,0},{32,48},{48,32},{64,80},{80,64},{96,112},{112,96},{1... | collective-permute-start | bytes 122888 | tf_op jit(solution)/shard_map/ppermute | solution.py:615
  34.9 7.2 %collective-permute-start.11 = (f32[48,128]{1,0:T(8,128)S(1)}, f32[48,128]{1,0:T(8,128)S(1)}, u32[]{:S(2)}, u32[]{:S(2)}) collective-permute-start(f32[48,128]{1,0:T(8,128)S(1)} %get-tuple-element.150), channel_id=1, source_target_pairs={{0,32},{16,48},{32,64},{48,80},{64,96},{80,112},{96,0},{112,16},{1... | collective-permute-start | bytes 73736 | tf_op jit(solution)/shard_map/ppermute | solution.py:620
  35.3 5.2 %collective-permute-start.12 = (f32[32,128]{1,0:T(8,128)S(1)}, f32[32,128]{1,0:T(8,128)S(1)}, u32[]{:S(2)}, u32[]{:S(2)}) collective-permute-start(f32[32,128]{1,0:T(8,128)S(1)} %get-tuple-element.151), channel_id=1, source_target_pairs={{0,64},{16,80},{32,96},{48,112},{64,0},{80,16},{96,32},{112,48},{1... | collective-permute-start | bytes 49160 | tf_op jit(solution)/shard_map/ppermute | solution.py:620
  38.4 3.7 %collective-permute-start.13 = (f32[32,128]{1,0:T(8,128)S(1)}, f32[32,128]{1,0:T(8,128)S(1)}, u32[]{:S(2)}, u32[]{:S(2)}) collective-permute-start(f32[32,128]{1,0:T(8,128)S(1)} %get-tuple-element.152), channel_id=1, source_target_pairs={{0,96},{16,112},{32,0},{48,16},{64,32},{80,48},{96,64},{112,80},{1... | collective-permute-start | bytes 49160 | tf_op jit(solution)/shard_map/ppermute | solution.py:620
  43.0 12.6 %all-to-all-start = ((f32[16,16,128]{2,1,0:T(8,128)}), f32[16,16,128]{2,1,0:T(8,128)S(1)}, u32[]{:S(2)}, u32[]{:S(2)}) async-start(f32[16,16,128]{2,1,0:T(8,128)} %get-tuple-element.171), calls=%async_computation | async-start | bytes 262144 | tf_op jit(solution)/shard_map/all_to_all | solution.py:634
